TPU v7x, 768 devices: a whole 4x8x12 slice. The times are simulated.
768 devices in a mesh: frame: 96 (over x, z, core), head: 8 (over y).
Axes of the slice: x: 4, y: 8, z: 12, core: 2. Of those that a mesh axis runs over, the one named last changes fastest.
Arguments:
- queries: bfloat16 [49152, 3072], P('frame', 'head'), may hold values from -128 to 128
- keys: bfloat16 [49152, 3072], P('frame', 'head'), may hold values from -8 to 8
- values: bfloat16 [49152, 3072], P('frame', 'head'), may hold values from -6 to 6
- out_weight: bfloat16 [3072, 3072], P('head'), may hold values from -0.109375 to 0.109375
- span: int32 [96], replicated, may hold values from 1 to 8, as said below
- counts: int32 [96], replicated, may hold values from 128 to 512, as said below
Outputs:
- projected: bfloat16 [49152, 3072], P('frame', 'head')
Inputs may be any that keep to these rules, and one draw needn't show every extreme that they name: `span`: every frame attends at least to itself; some frames reach the full window of 8 frames. `counts`: some frame is full and some frame holds exactly 128 live tokens.
All inputs are finite; a program needn't handle non-finite values.
Results may differ from a plain program's by a relative error of at most 0.02.
Values may be sent and summed in bfloat16 or wider, within the bound.
No kernel may reach another device: no remote copies, remote signals or barrier semaphores. Data moves between devices by JAX's collectives and lax.ppermute only.
A program may use at most 128 MiB of HBM per device.

v0:
```python
import jax
import jax.numpy as jnp
from jax import lax
from jax.sharding import PartitionSpec as P

HD = 128
WIN = 8


def from_behind(block, axis, distance):
    devices = range(lax.axis_size(axis))
    route = [(i - distance, i) for i in devices if i - distance in devices]
    return lax.ppermute(block, axis, route)


def pick_entry(table, position):
    return jnp.sum(jnp.where(jnp.arange(table.shape[0], dtype=jnp.int32) == position, table, 0))


def allowed(first_frame, frames_in, per_frame, own_frame, own_span, counts):
    sources = first_frame + jnp.arange(frames_in, dtype=jnp.int32)
    table_index = jnp.arange(counts.shape[0], dtype=jnp.int32)
    frame_counts = jnp.sum(
        jnp.where(table_index[None, :] == sources[:, None], counts[None, :], 0), axis=1
    )
    slot_index = jnp.arange(per_frame, dtype=jnp.int32)
    visible = (
        (sources[:, None] >= 0)
        & (own_frame - sources[:, None] < own_span)
        & (slot_index[None, :] < frame_counts[:, None])
    )
    return visible.reshape(frames_in * per_frame)


def on_device(queries, keys, values, out_weight, span, counts):
    per_frame = queries.shape[0]
    head_width = queries.shape[1]
    local_heads = head_width // HD
    scaling = HD ** (-0.5)
    own_frame = lax.axis_index("frame")
    own_span = pick_entry(span, own_frame)
    query_rows = queries.reshape(per_frame, local_heads, HD)

    def block_scores(key_block, visible):
        scores = (
            jnp.einsum(
                "thd,khd->htk",
                query_rows,
                key_block.reshape(-1, local_heads, HD),
                preferred_element_type=jnp.float32,
            )
            * scaling
        )
        return jnp.where(visible[None, None, :], scores, -1e30)

    def block_values(weights, value_block):
        return jnp.einsum(
            "htk,khd->htd",
            weights.astype(jnp.bfloat16),
            value_block.reshape(-1, local_heads, HD),
            preferred_element_type=jnp.float32,
        )

    scores = block_scores(keys, allowed(own_frame, 1, per_frame, own_frame, own_span, counts))
    row_top = jnp.max(scores, axis=-1, keepdims=True)
    weights = jnp.exp(scores - row_top)
    row_total = jnp.sum(weights, axis=-1, keepdims=True)
    carried = block_values(weights, values)

    def advance(offset, carried_state):
        key_block, value_block, row_top, row_total, carried = carried_state
        key_block, value_block = from_behind((key_block, value_block), "frame", 1)
        visible = allowed(own_frame - offset, 1, per_frame, own_frame, own_span, counts)
        scores = block_scores(key_block, visible)
        new_top = jnp.maximum(row_top, jnp.max(scores, axis=-1, keepdims=True))
        rescale = jnp.exp(row_top - new_top)
        weights = jnp.exp(scores - new_top)
        row_total = row_total * rescale + jnp.sum(weights, axis=-1, keepdims=True)
        carried = carried * rescale + block_values(weights, value_block)
        return (key_block, value_block, new_top, row_total, carried)

    final_state = lax.fori_loop(1, WIN, advance, (keys, values, row_top, row_total, carried))
    row_total = final_state[3]
    carried = final_state[4]
    attention = (
        (carried / row_total).transpose(1, 0, 2).reshape(per_frame, head_width).astype(jnp.bfloat16)
    )
    partial_value = jnp.dot(attention, out_weight, preferred_element_type=jnp.float32)
    return lax.psum_scatter(
        partial_value.astype(jnp.bfloat16), "head", scatter_dimension=1, tiled=True
    )


def solution(mesh):
    return jax.shard_map(
        on_device,
        mesh=mesh,
        in_specs=(
            P("frame", "head"),
            P("frame", "head"),
            P("frame", "head"),
            P("head", None),
            P(),
            P(),
        ),
        out_specs=P("frame", "head"),
        check_vma=False,
    )
```

profile of v0, /device:TPU:2, one launch (start us, length us, event | category | flops | bytes accessed | tf_op | source)
XLA Modules:
  0.0 222.7 jit_solution(17379380424937279754)
XLA Ops:
  9.9 1.9 copy.35
  11.8 1.9 copy.36
  17.2 3.0 %fusion.20 = f32[3,512,128]{2,1,0:T(8,128)} fusion(bf16[512,3,128]{0,2,1:T(8,128)(2,1)} %bitcast.10, f32[3,512,512]{1,2,0:T(8,128)S(1)} %get-tuple-element.222, f32[3,512]{1,0:T(4,128)S(1)} %get-tuple-element.221, pred[512]{0:T(512)(128)(4,1)S(1)} %fusion.26), kind=kOutput, calls=%fused_computation.27 | convolution fusion | flops 204472320 | bytes 4332032 | tf_op jit(solution)/shard_map/htk,khd->htd/dot_general | solution.py:57
  20.2 138.6 %while.21 = (s32[]{:T(128)}, bf16[512,384]{0,1:T(8,128)(2,1)}, bf16[512,384]{0,1:T(8,128)(2,1)}, f32[3,512,1]{1,0,2:T(4,128)S(1)}, f32[3,512,1]{1,0,2:T(4,128)S(...) while((s32[]{:T(128)}, bf16[512,384]{0,1:T(8,128)(2,1)}, ...), condition=%wide.region_8.9_spmd, body=%wide.region_4.8_spmd.sunk | while | flops 411703072 | bytes 23300780 | solution.py:82
  22.1 4.4 %collective-permute-start.1 = (bf16[512,384]{0,1:T(8,128)(2,1)}, bf16[512,384]{0,1:T(8,128)(2,1)S(1)}, u32[]{:S(2)}, u32[]{:S(2)}) collective-permute-start(bf16[512,384]{0,1:T(8,128)(2,1)} %get-tuple-element.308), channel_id=1, source_target_pairs={{0,8},{8,16},{16,24},{24,32},{32,40},{40,48},{48,56},{56,64},{64,7... | collective-permute-start | bytes 1179656 | tf_op jit(solution)/shard_map/while/body/eval_jaxpr/ppermute | solution.py:13
  29.1 10.8 %collective-permute-done = bf16[512,384]{0,1:T(8,128)(2,1)S(1)} collective-permute-done((bf16[512,384]{0,1:T(8,128)(2,1)}, bf16[512,384]{0,1:T(8,128)(2,1)S(1)}, u32[]{:S(2)}, u32[]{:S(2)}) %collective-permute-start) | collective-permute-done | bytes 393248 | tf_op jit(solution)/shard_map/while/body/eval_jaxpr/ppermute | solution.py:13
  41.4 2.6 %collective-permute-done.1 = bf16[512,384]{0,1:T(8,128)(2,1)S(1)} collective-permute-done((bf16[512,384]{0,1:T(8,128)(2,1)}, bf16[512,384]{0,1:T(8,128)(2,1)S(1)}, u32[]{:S(2)}, u32[]{:S(2)}) %collective-permute-start.1) | collective-permute-done | bytes 393248 | tf_op jit(solution)/shard_map/while/body/eval_jaxpr/ppermute | solution.py:13
  47.0 1.9 collective-permute-start
  48.9 1.9 collective-permute-start.1
  53.5 5.0 %collective-permute-done = bf16[512,384]{0,1:T(8,128)(2,1)S(1)} collective-permute-done((bf16[512,384]{0,1:T(8,128)(2,1)}, bf16[512,384]{0,1:T(8,128)(2,1)S(1)}, u32[]{:S(2)}, u32[]{:S(2)}) %collective-permute-start) | collective-permute-done | bytes 393248 | tf_op jit(solution)/shard_map/while/body/eval_jaxpr/ppermute | solution.py:13
  60.0 2.6 %collective-permute-done.1 = bf16[512,384]{0,1:T(8,128)(2,1)S(1)} collective-permute-done((bf16[512,384]{0,1:T(8,128)(2,1)}, bf16[512,384]{0,1:T(8,128)(2,1)S(1)}, u32[]{:S(2)}, u32[]{:S(2)}) %collective-permute-start.1) | collective-permute-done | bytes 393248 | tf_op jit(solution)/shard_map/while/body/eval_jaxpr/ppermute | solution.py:13
  65.6 1.9 collective-permute-start
  67.6 1.9 collective-permute-start.1
  72.1 5.0 %collective-permute-done = bf16[512,384]{0,1:T(8,128)(2,1)S(1)} collective-permute-done((bf16[512,384]{0,1:T(8,128)(2,1)}, bf16[512,384]{0,1:T(8,128)(2,1)S(1)}, u32[]{:S(2)}, u32[]{:S(2)}) %collective-permute-start) | collective-permute-done | bytes 393248 | tf_op jit(solution)/shard_map/while/body/eval_jaxpr/ppermute | solution.py:13
  78.6 2.6 %collective-permute-done.1 = bf16[512,384]{0,1:T(8,128)(2,1)S(1)} collective-permute-done((bf16[512,384]{0,1:T(8,128)(2,1)}, bf16[512,384]{0,1:T(8,128)(2,1)S(1)}, u32[]{:S(2)}, u32[]{:S(2)}) %collective-permute-start.1) | collective-permute-done | bytes 393248 | tf_op jit(solution)/shard_map/while/body/eval_jaxpr/ppermute | solution.py:13
  84.3 1.9 collective-permute-start
  86.2 1.9 collective-permute-start.1
  90.7 5.0 %collective-permute-done = bf16[512,384]{0,1:T(8,128)(2,1)S(1)} collective-permute-done((bf16[512,384]{0,1:T(8,128)(2,1)}, bf16[512,384]{0,1:T(8,128)(2,1)S(1)}, u32[]{:S(2)}, u32[]{:S(2)}) %collective-permute-start) | collective-permute-done | bytes 393248 | tf_op jit(solution)/shard_map/while/body/eval_jaxpr/ppermute | solution.py:13
  97.3 2.6 %collective-permute-done.1 = bf16[512,384]{0,1:T(8,128)(2,1)S(1)} collective-permute-done((bf16[512,384]{0,1:T(8,128)(2,1)}, bf16[512,384]{0,1:T(8,128)(2,1)S(1)}, u32[]{:S(2)}, u32[]{:S(2)}) %collective-permute-start.1) | collective-permute-done | bytes 393248 | tf_op jit(solution)/shard_map/while/body/eval_jaxpr/ppermute | solution.py:13
  104.8 1.9 collective-permute-start.1
  109.3 5.0 %collective-permute-done = bf16[512,384]{0,1:T(8,128)(2,1)S(1)} collective-permute-done((bf16[512,384]{0,1:T(8,128)(2,1)}, bf16[512,384]{0,1:T(8,128)(2,1)S(1)}, u32[]{:S(2)}, u32[]{:S(2)}) %collective-permute-start) | collective-permute-done | bytes 393248 | tf_op jit(solution)/shard_map/while/body/eval_jaxpr/ppermute | solution.py:13
  115.9 2.6 %collective-permute-done.1 = bf16[512,384]{0,1:T(8,128)(2,1)S(1)} collective-permute-done((bf16[512,384]{0,1:T(8,128)(2,1)}, bf16[512,384]{0,1:T(8,128)(2,1)S(1)}, u32[]{:S(2)}, u32[]{:S(2)}) %collective-permute-start.1) | collective-permute-done | bytes 393248 | tf_op jit(solution)/shard_map/while/body/eval_jaxpr/ppermute | solution.py:13
  123.4 1.9 collective-permute-start.1
  127.9 5.0 %collective-permute-done = bf16[512,384]{0,1:T(8,128)(2,1)S(1)} collective-permute-done((bf16[512,384]{0,1:T(8,128)(2,1)}, bf16[512,384]{0,1:T(8,128)(2,1)S(1)}, u32[]{:S(2)}, u32[]{:S(2)}) %collective-permute-start) | collective-permute-done | bytes 393248 | tf_op jit(solution)/shard_map/while/body/eval_jaxpr/ppermute | solution.py:13
  134.5 2.6 %collective-permute-done.1 = bf16[512,384]{0,1:T(8,128)(2,1)S(1)} collective-permute-done((bf16[512,384]{0,1:T(8,128)(2,1)}, bf16[512,384]{0,1:T(8,128)(2,1)S(1)}, u32[]{:S(2)}, u32[]{:S(2)}) %collective-permute-start.1) | collective-permute-done | bytes 393248 | tf_op jit(solution)/shard_map/while/body/eval_jaxpr/ppermute | solution.py:13
  142.0 1.9 collective-permute-start.1
  146.5 5.0 %collective-permute-done = bf16[512,384]{0,1:T(8,128)(2,1)S(1)} collective-permute-done((bf16[512,384]{0,1:T(8,128)(2,1)}, bf16[512,384]{0,1:T(8,128)(2,1)S(1)}, u32[]{:S(2)}, u32[]{:S(2)}) %collective-permute-start) | collective-permute-done | bytes 393248 | tf_op jit(solution)/shard_map/while/body/eval_jaxpr/ppermute | solution.py:13
  153.1 2.6 %collective-permute-done.1 = bf16[512,384]{0,1:T(8,128)(2,1)S(1)} collective-permute-done((bf16[512,384]{0,1:T(8,128)(2,1)}, bf16[512,384]{0,1:T(8,128)(2,1)S(1)}, u32[]{:S(2)}, u32[]{:S(2)}) %collective-permute-start.1) | collective-permute-done | bytes 393248 | tf_op jit(solution)/shard_map/while/body/eval_jaxpr/ppermute | solution.py:13
  160.2 3.5 %convolution_convert_fusion = bf16[512,3072]{1,0:T(8,128)(2,1)} fusion(bf16[512,384]{0,1:T(8,128)(2,1)S(1)} %bitcast.56, bf16[384,3072]{1,0:T(8,128)(2,1)S(1)} %copy-done), kind=kOutput, calls=%fused_computation.21 | convolution fusion | flops 1209532416 | bytes 5898240 | tf_op jit(solution)/shard_map/dot_general | solution.py:88
  163.8 4.7 %copy.46 = bf16[512,3072]{0,1:T(8,128)(2,1)} copy(bf16[512,3072]{1,0:T(8,128)(2,1)} %convolution_convert_fusion) | data formatting | bytes 6291456
  168.4 45.5 %reduce-scatter.4.cloned.1.call-done = bf16[384,512]{1,0:T(8,128)(2,1)} async-done(((bf16[3072,512]{1,0:T(8,128)(2,1)}), bf16[384,512]{1,0:T(8,128)(2,1)}) %reduce-scatter.4.cloned.1.call-update) | async-done | bytes 393232
  214.0 1.9 copy.47
  (114 shorter events, 60.9 us)
Async XLA Ops:
  6.5 153.7 %copy-start = (bf16[384,3072]{1,0:T(8,128)(2,1)S(1)}, bf16[384,3072]{1,0:T(8,128)(2,1)}, u32[]{:S(2)}) copy-start(bf16[384,3072]{1,0:T(8,128)(2,1)} %param.11) | copy-start | bytes 7077892
  6.5 207.4 %reduce-scatter.4.cloned.1.call-start = ((), (), s32[]{:S(2)}) async-start(), calls=%async_computation.1 | async-start | bytes 3538944
  20.2 19.6 %collective-permute-start = (bf16[512,384]{0,1:T(8,128)(2,1)}, bf16[512,384]{0,1:T(8,128)(2,1)S(1)}, u32[]{:S(2)}, u32[]{:S(2)}) collective-permute-start(bf16[512,384]{0,1:T(8,128)(2,1)} %get-tuple-element.307), channel_id=1, source_target_pairs={{0,8},{8,16},{16,24},{24,32},{32,40},{40,48},{48,56},{56,64},{64,7... | collective-permute-start | bytes 1179656 | tf_op jit(solution)/shard_map/while/body/eval_jaxpr/ppermute | solution.py:13
  22.1 21.9 %collective-permute-start.1 = (bf16[512,384]{0,1:T(8,128)(2,1)}, bf16[512,384]{0,1:T(8,128)(2,1)S(1)}, u32[]{:S(2)}, u32[]{:S(2)}) collective-permute-start(bf16[512,384]{0,1:T(8,128)(2,1)} %get-tuple-element.308), channel_id=1, source_target_pairs={{0,8},{8,16},{16,24},{24,32},{32,40},{40,48},{48,56},{56,64},{64,7... | collective-permute-start | bytes 1179656 | tf_op jit(solution)/shard_map/while/body/eval_jaxpr/ppermute | solution.py:13
  39.8 4.2 %copy-start.1 = (f32[3,512,128]{2,1,0:T(8,128)S(1)}, f32[3,512,128]{2,1,0:T(8,128)}, u32[]{:S(2)}) copy-start(f32[3,512,128]{2,1,0:T(8,128)} %get-tuple-element.311) | copy-start | bytes 2359300 | tf_op jit(solution)/shard_map/while
  45.5 1.5 copy-start.2
  47.0 11.4 %collective-permute-start = (bf16[512,384]{0,1:T(8,128)(2,1)}, bf16[512,384]{0,1:T(8,128)(2,1)S(1)}, u32[]{:S(2)}, u32[]{:S(2)}) collective-permute-start(bf16[512,384]{0,1:T(8,128)(2,1)} %get-tuple-element.307), channel_id=1, source_target_pairs={{0,8},{8,16},{16,24},{24,32},{32,40},{40,48},{48,56},{56,64},{64,7... | collective-permute-start | bytes 1179656 | tf_op jit(solution)/shard_map/while/body/eval_jaxpr/ppermute | solution.py:13
  48.9 13.7 %collective-permute-start.1 = (bf16[512,384]{0,1:T(8,128)(2,1)}, bf16[512,384]{0,1:T(8,128)(2,1)S(1)}, u32[]{:S(2)}, u32[]{:S(2)}) collective-permute-start(bf16[512,384]{0,1:T(8,128)(2,1)} %get-tuple-element.308), channel_id=1, source_target_pairs={{0,8},{8,16},{16,24},{24,32},{32,40},{40,48},{48,56},{56,64},{64,7... | collective-permute-start | bytes 1179656 | tf_op jit(solution)/shard_map/while/body/eval_jaxpr/ppermute | solution.py:13
  58.4 4.2 %copy-start.1 = (f32[3,512,128]{2,1,0:T(8,128)S(1)}, f32[3,512,128]{2,1,0:T(8,128)}, u32[]{:S(2)}) copy-start(f32[3,512,128]{2,1,0:T(8,128)} %get-tuple-element.311) | copy-start | bytes 2359300 | tf_op jit(solution)/shard_map/while
  64.1 1.5 copy-start.2
  65.6 11.4 %collective-permute-start = (bf16[512,384]{0,1:T(8,128)(2,1)}, bf16[512,384]{0,1:T(8,128)(2,1)S(1)}, u32[]{:S(2)}, u32[]{:S(2)}) collective-permute-start(bf16[512,384]{0,1:T(8,128)(2,1)} %get-tuple-element.307), channel_id=1, source_target_pairs={{0,8},{8,16},{16,24},{24,32},{32,40},{40,48},{48,56},{56,64},{64,7... | collective-permute-start | bytes 1179656 | tf_op jit(solution)/shard_map/while/body/eval_jaxpr/ppermute | solution.py:13
  67.6 13.7 %collective-permute-start.1 = (bf16[512,384]{0,1:T(8,128)(2,1)}, bf16[512,384]{0,1:T(8,128)(2,1)S(1)}, u32[]{:S(2)}, u32[]{:S(2)}) collective-permute-start(bf16[512,384]{0,1:T(8,128)(2,1)} %get-tuple-element.308), channel_id=1, source_target_pairs={{0,8},{8,16},{16,24},{24,32},{32,40},{40,48},{48,56},{56,64},{64,7... | collective-permute-start | bytes 1179656 | tf_op jit(solution)/shard_map/while/body/eval_jaxpr/ppermute | solution.py:13
  77.0 4.2 %copy-start.1 = (f32[3,512,128]{2,1,0:T(8,128)S(1)}, f32[3,512,128]{2,1,0:T(8,128)}, u32[]{:S(2)}) copy-start(f32[3,512,128]{2,1,0:T(8,128)} %get-tuple-element.311) | copy-start | bytes 2359300 | tf_op jit(solution)/shard_map/while
  82.7 1.5 copy-start.2
  84.3 11.4 %collective-permute-start = (bf16[512,384]{0,1:T(8,128)(2,1)}, bf16[512,384]{0,1:T(8,128)(2,1)S(1)}, u32[]{:S(2)}, u32[]{:S(2)}) collective-permute-start(bf16[512,384]{0,1:T(8,128)(2,1)} %get-tuple-element.307), channel_id=1, source_target_pairs={{0,8},{8,16},{16,24},{24,32},{32,40},{40,48},{48,56},{56,64},{64,7... | collective-permute-start | bytes 1179656 | tf_op jit(solution)/shard_map/while/body/eval_jaxpr/ppermute | solution.py:13
  86.2 13.7 %collective-permute-start.1 = (bf16[512,384]{0,1:T(8,128)(2,1)}, bf16[512,384]{0,1:T(8,128)(2,1)S(1)}, u32[]{:S(2)}, u32[]{:S(2)}) collective-permute-start(bf16[512,384]{0,1:T(8,128)(2,1)} %get-tuple-element.308), channel_id=1, source_target_pairs={{0,8},{8,16},{16,24},{24,32},{32,40},{40,48},{48,56},{56,64},{64,7... | collective-permute-start | bytes 1179656 | tf_op jit(solution)/shard_map/while/body/eval_jaxpr/ppermute | solution.py:13
  95.7 4.2 %copy-start.1 = (f32[3,512,128]{2,1,0:T(8,128)S(1)}, f32[3,512,128]{2,1,0:T(8,128)}, u32[]{:S(2)}) copy-start(f32[3,512,128]{2,1,0:T(8,128)} %get-tuple-element.311) | copy-start | bytes 2359300 | tf_op jit(solution)/shard_map/while
  101.3 1.5 copy-start.2
  102.9 11.4 %collective-permute-start = (bf16[512,384]{0,1:T(8,128)(2,1)}, bf16[512,384]{0,1:T(8,128)(2,1)S(1)}, u32[]{:S(2)}, u32[]{:S(2)}) collective-permute-start(bf16[512,384]{0,1:T(8,128)(2,1)} %get-tuple-element.307), channel_id=1, source_target_pairs={{0,8},{8,16},{16,24},{24,32},{32,40},{40,48},{48,56},{56,64},{64,7... | collective-permute-start | bytes 1179656 | tf_op jit(solution)/shard_map/while/body/eval_jaxpr/ppermute | solution.py:13
  104.8 13.7 %collective-permute-start.1 = (bf16[512,384]{0,1:T(8,128)(2,1)}, bf16[512,384]{0,1:T(8,128)(2,1)S(1)}, u32[]{:S(2)}, u32[]{:S(2)}) collective-permute-start(bf16[512,384]{0,1:T(8,128)(2,1)} %get-tuple-element.308), channel_id=1, source_target_pairs={{0,8},{8,16},{16,24},{24,32},{32,40},{40,48},{48,56},{56,64},{64,7... | collective-permute-start | bytes 1179656 | tf_op jit(solution)/shard_map/while/body/eval_jaxpr/ppermute | solution.py:13
  114.3 4.2 %copy-start.1 = (f32[3,512,128]{2,1,0:T(8,128)S(1)}, f32[3,512,128]{2,1,0:T(8,128)}, u32[]{:S(2)}) copy-start(f32[3,512,128]{2,1,0:T(8,128)} %get-tuple-element.311) | copy-start | bytes 2359300 | tf_op jit(solution)/shard_map/while
  120.0 1.5 copy-start.2
  121.5 11.4 %collective-permute-start = (bf16[512,384]{0,1:T(8,128)(2,1)}, bf16[512,384]{0,1:T(8,128)(2,1)S(1)}, u32[]{:S(2)}, u32[]{:S(2)}) collective-permute-start(bf16[512,384]{0,1:T(8,128)(2,1)} %get-tuple-element.307), channel_id=1, source_target_pairs={{0,8},{8,16},{16,24},{24,32},{32,40},{40,48},{48,56},{56,64},{64,7... | collective-permute-start | bytes 1179656 | tf_op jit(solution)/shard_map/while/body/eval_jaxpr/ppermute | solution.py:13
  123.4 13.7 %collective-permute-start.1 = (bf16[512,384]{0,1:T(8,128)(2,1)}, bf16[512,384]{0,1:T(8,128)(2,1)S(1)}, u32[]{:S(2)}, u32[]{:S(2)}) collective-permute-start(bf16[512,384]{0,1:T(8,128)(2,1)} %get-tuple-element.308), channel_id=1, source_target_pairs={{0,8},{8,16},{16,24},{24,32},{32,40},{40,48},{48,56},{56,64},{64,7... | collective-permute-start | bytes 1179656 | tf_op jit(solution)/shard_map/while/body/eval_jaxpr/ppermute | solution.py:13
  132.9 4.2 %copy-start.1 = (f32[3,512,128]{2,1,0:T(8,128)S(1)}, f32[3,512,128]{2,1,0:T(8,128)}, u32[]{:S(2)}) copy-start(f32[3,512,128]{2,1,0:T(8,128)} %get-tuple-element.311) | copy-start | bytes 2359300 | tf_op jit(solution)/shard_map/while
  138.6 1.5 copy-start.2
  140.1 11.4 %collective-permute-start = (bf16[512,384]{0,1:T(8,128)(2,1)}, bf16[512,384]{0,1:T(8,128)(2,1)S(1)}, u32[]{:S(2)}, u32[]{:S(2)}) collective-permute-start(bf16[512,384]{0,1:T(8,128)(2,1)} %get-tuple-element.307), channel_id=1, source_target_pairs={{0,8},{8,16},{16,24},{24,32},{32,40},{40,48},{48,56},{56,64},{64,7... | collective-permute-start | bytes 1179656 | tf_op jit(solution)/shard_map/while/body/eval_jaxpr/ppermute | solution.py:13
  142.0 13.7 %collective-permute-start.1 = (bf16[512,384]{0,1:T(8,128)(2,1)}, bf16[512,384]{0,1:T(8,128)(2,1)S(1)}, u32[]{:S(2)}, u32[]{:S(2)}) collective-permute-start(bf16[512,384]{0,1:T(8,128)(2,1)} %get-tuple-element.308), channel_id=1, source_target_pairs={{0,8},{8,16},{16,24},{24,32},{32,40},{40,48},{48,56},{56,64},{64,7... | collective-permute-start | bytes 1179656 | tf_op jit(solution)/shard_map/while/body/eval_jaxpr/ppermute | solution.py:13
  151.5 4.2 %copy-start.1 = (f32[3,512,128]{2,1,0:T(8,128)S(1)}, f32[3,512,128]{2,1,0:T(8,128)}, u32[]{:S(2)}) copy-start(f32[3,512,128]{2,1,0:T(8,128)} %get-tuple-element.311) | copy-start | bytes 2359300 | tf_op jit(solution)/shard_map/while
  157.2 1.5 copy-start.2
Sparse Core Ops, SparseCore 0:
  168.6 45.3 reduce-scatter.3
where the time goes:
time: 224 us; the launch traced here: 223 us
  waiting for transfers between devices  104 us (46%)
  starting transfers between devices  29.3 us (13%)
  matrix products  24.3 us (11%)
  local copies, waits for them, and re-layouts  23.9 us (11%)
  other arithmetic  21.9 us (10%)
  between operations  14.1 us (6%)
  loops' own time  4.86 us (2%)
    ppermute x14, waiting for transfers between devices, from_behind(): return lax.ppermute(block, axis, route)  58.9 us
    unnamed x2, waiting for transfers between devices  45.5 us
    ppermute x14, starting transfers between devices, from_behind(): return lax.ppermute(block, axis, route)  29.3 us
    dot_general x8, matrix products, block_values(): jnp.einsum('htk,khd->htd', weights.astype(jnp.bfloat16), value_block.resh...  13.1 us
    while x49, local copies, waits for them, and re-layouts  10.8 us
    reduce_sum x7, other arithmetic, allowed(): jnp.sum(jnp.where(table_index[None, :] == sources[:, None], counts[None,...  9.23 us
    unnamed x5, local copies, waits for them, and re-layouts  7.74 us
    dot_general x8, matrix products, block_scores(): jnp.einsum('thd,khd->htk', query_rows, key_block.reshape(-1, local_heads,...  7.62 us
  transfers between devices with their start and end apart: 15, of which 15 were waited for; matrix products, arithmetic and copies ran while one was open for 11% of the time, Pallas kernels for 0%

commit v1 on v0

v1 whole, which is shorter than its diff:
```python
import jax
import jax.numpy as jnp
from jax import lax
from jax.experimental import pallas as pl
from jax.experimental.pallas import tpu as pltpu
from jax.sharding import PartitionSpec as P

HD = 128
WIN = 8
NEG = -1e30
EXP2_SCALE = HD ** (-0.5) * 1.4426950408889634
ROW_BLOCK = 256


def _attend(limit, q_ref, k_ref, v_ref, acc_ref, top_ref):
    slots = k_ref.shape[0]

    @pl.when(limit > 0)
    def _():
        keys = k_ref[...]
        values = jnp.concatenate([v_ref[...], jnp.ones((slots, HD), jnp.bfloat16)], axis=1)
        slot = lax.broadcasted_iota(jnp.int32, (1, slots), 1)
        hidden = jnp.where(slot < limit, 0.0, NEG)
        for start in range(0, q_ref.shape[0], ROW_BLOCK):
            rows = pl.ds(start, ROW_BLOCK)
            scores = lax.dot_general(
                q_ref[rows, :], keys, (((1,), (1,)), ((), ())), preferred_element_type=jnp.float32
            )
            scores = scores + hidden
            old_top = top_ref[0, rows, :]
            new_top = jnp.maximum(old_top, jnp.max(scores, axis=1, keepdims=True))
            wide_top = jnp.tile(new_top, (1, slots // HD))
            weights = jnp.exp2((scores - wide_top) * EXP2_SCALE).astype(jnp.bfloat16)
            rescale = jnp.exp2((old_top - new_top) * EXP2_SCALE)
            acc_ref[0, rows, :] = acc_ref[0, rows, :] * jnp.tile(rescale, (1, 2)) + jnp.dot(
                weights, values, preferred_element_type=jnp.float32
            )
            top_ref[0, rows, :] = new_top


def _visible(frame, side, behind, span_ref, counts_ref):
    query = frame if side == 0 else frame + 1 - 2 * (frame % 2)
    source = frame - behind
    back = query - source
    seen = (source >= 0) & (back >= 0) & (back < span_ref[query])
    return jnp.where(seen, counts_ref[jnp.maximum(source, 0)], 0)


def _start(acc, top):
    acc[...] = jnp.zeros_like(acc)
    top[...] = jnp.full_like(top, NEG)


def _attention_body(hops, first, hand_over):
    def body(frame_ref, span_ref, counts_ref, *refs):
        refs = list(refs)
        q_refs = [refs.pop(0), refs.pop(0)]
        kv_refs = [(refs.pop(0), refs.pop(0)) for _ in hops]
        if first:
            state_in = None
        else:
            state_in = [refs.pop(0) for _ in range(4)]
        if hand_over:
            own_acc, own_top, packed, other_acc, other_top = refs
        else:
            own_acc, own_top, other_acc, other_top = refs
        state = (own_acc, own_top, other_acc, other_top)
        if first:
            _start(own_acc, own_top)
            _start(other_acc, other_top)
        else:
            for ref, ref_in in zip(state, state_in):
                ref[...] = ref_in[...]
        frame = frame_ref[0]
        for hop, (k_ref, v_ref) in zip(hops, kv_refs):
            for side in (0, 1):
                limit = _visible(frame, side, 2 * hop, span_ref, counts_ref)
                _attend(limit, q_refs[side], k_ref, v_ref, state[2 * side], state[2 * side + 1])
        if hand_over:
            lane = lax.broadcasted_iota(jnp.int32, (1, HD), 1)
            packed[0, :, :HD] = other_acc[0, :, :HD]
            packed[0, :, HD:] = jnp.where(lane < HD // 2, other_top[0], other_acc[0, :, HD:])

    return body


def attention_call(scalars, q_own, q_other, sources, hops, state, head0, heads, hand_over, name):
    per_frame = q_own.shape[0]
    first = state is None
    q_spec = pl.BlockSpec((per_frame, HD), lambda h, *_: (0, head0 + h))
    k_spec = pl.BlockSpec((per_frame, HD), lambda h, *_: (0, h))
    v_spec = pl.BlockSpec((per_frame, HD), lambda h, *_: (0, heads + h))
    acc_spec = pl.BlockSpec((1, per_frame, 2 * HD), lambda h, *_: (h, 0, 0))
    top_spec = pl.BlockSpec((1, per_frame, HD), lambda h, *_: (h, 0, 0))
    in_specs = [q_spec, q_spec]
    operands = [q_own, q_other]
    for source in sources:
        in_specs += [k_spec, v_spec]
        operands += [source, source]
    if not first:
        in_specs += [acc_spec, top_spec] * 2
        operands += list(state)
    acc_shape = jax.ShapeDtypeStruct((heads, per_frame, 2 * HD), jnp.float32)
    top_shape = jax.ShapeDtypeStruct((heads, per_frame, HD), jnp.float32)
    scratch = []
    if hand_over:
        out_specs = [acc_spec, top_spec, acc_spec]
        out_shape = [acc_shape, top_shape, acc_shape]
        scratch = [
            pltpu.VMEM((1, per_frame, 2 * HD), jnp.float32),
            pltpu.VMEM((1, per_frame, HD), jnp.float32),
        ]
    else:
        out_specs = [acc_spec, top_spec] * 2
        out_shape = [acc_shape, top_shape] * 2
    pairs = 2 * len(hops) * heads * per_frame * per_frame
    return pl.pallas_call(
        _attention_body(hops, first, hand_over),
        out_shape=out_shape,
        grid_spec=pltpu.PrefetchScalarGridSpec(
            num_scalar_prefetch=3,
            grid=(heads,),
            in_specs=in_specs,
            out_specs=out_specs,
            scratch_shapes=scratch,
        ),
        cost_estimate=pl.CostEstimate(
            flops=pairs * HD * 8, transcendentals=pairs, bytes_accessed=per_frame * HD * 16 * heads
        ),
        compiler_params=pltpu.CompilerParams(vmem_limit_bytes=40 << 20),
        name=name,
    )(*scalars, *operands)


def _finish_body(frame_ref, span_ref, counts_ref, q_ref, k_ref, v_ref, acc_in, top_in, packed, out_ref, acc, top):
    acc[...] = acc_in[...]
    top[...] = top_in[...]
    limit = _visible(frame_ref[0], 0, WIN - 1, span_ref, counts_ref)
    limit = jnp.where(frame_ref[0] % 2 == 0, limit, 0)
    _attend(limit, q_ref, k_ref, v_ref, acc, top)
    own_top, other_top = top[0], packed[0, :, HD : HD + 1]
    own_total, other_total = acc[0, :, HD:], packed[0, :, 2 * HD - 1 :]
    both_top = jnp.maximum(own_top, other_top)
    own_part = jnp.exp2((own_top - both_top) * EXP2_SCALE)
    other_part = jnp.exp2((other_top - both_top) * EXP2_SCALE)
    total = own_total * own_part + other_total * other_part
    mixed = acc[0, :, :HD] * own_part + packed[0, :, :HD] * other_part
    out_ref[...] = (mixed / total).astype(jnp.bfloat16)


def finish_call(scalars, q_own, source, state, packed, head0, heads, name):
    per_frame = q_own.shape[0]
    acc_spec = pl.BlockSpec((1, per_frame, 2 * HD), lambda h, *_: (h, 0, 0))
    top_spec = pl.BlockSpec((1, per_frame, HD), lambda h, *_: (h, 0, 0))
    pairs = heads * per_frame * per_frame
    return pl.pallas_call(
        _finish_body,
        out_shape=jax.ShapeDtypeStruct((per_frame, heads * HD), jnp.bfloat16),
        grid_spec=pltpu.PrefetchScalarGridSpec(
            num_scalar_prefetch=3,
            grid=(heads,),
            in_specs=[
                pl.BlockSpec((per_frame, HD), lambda h, *_: (0, head0 + h)),
                pl.BlockSpec((per_frame, HD), lambda h, *_: (0, h)),
                pl.BlockSpec((per_frame, HD), lambda h, *_: (0, heads + h)),
                acc_spec,
                top_spec,
                acc_spec,
            ],
            out_specs=pl.BlockSpec((per_frame, HD), lambda h, *_: (0, h)),
            scratch_shapes=[
                pltpu.VMEM((1, per_frame, 2 * HD), jnp.float32),
                pltpu.VMEM((1, per_frame, HD), jnp.float32),
            ],
        ),
        cost_estimate=pl.CostEstimate(
            flops=pairs * HD * 8, transcendentals=pairs, bytes_accessed=per_frame * HD * 16 * heads
        ),
        compiler_params=pltpu.CompilerParams(vmem_limit_bytes=40 << 20),
        name=name,
    )(*scalars, q_own, source, source, *state, packed)


def _copy_body(in_ref, out_ref):
    out_ref[0] = in_ref[...]


def column_blocks(weight, groups):
    rows, width = weight.shape
    columns = width // groups
    return pl.pallas_call(
        _copy_body,
        out_shape=jax.ShapeDtypeStruct((groups, rows, columns), weight.dtype),
        grid=(groups,),
        in_specs=[pl.BlockSpec((rows, columns), lambda g: (0, g))],
        out_specs=pl.BlockSpec((1, rows, columns), lambda g: (g, 0, 0)),
        name="column_blocks",
    )(weight)


def _project_body(groups, row0, width, has_base):
    def body(*refs):
        if has_base:
            base_ref, a_ref, w_ref, out_ref = refs
            total = base_ref[...]
        else:
            a_ref, w_ref, out_ref = refs
            total = None
        for group in range(groups):
            part = jnp.dot(
                a_ref[group], w_ref[group, row0 : row0 + width, :], preferred_element_type=jnp.float32
            )
            total = part if total is None else total + part
        out_ref[...] = total.astype(out_ref.dtype)

    return body


def project_call(base, gathered, weight, row0, dtype, name, block=128):
    groups, per_frame, width = gathered.shape
    columns = weight.shape[2]
    rows = pl.BlockSpec((block, columns), lambda r: (r, 0))
    in_specs = [
        pl.BlockSpec((groups, block, width), lambda r: (0, r, 0)),
        pl.BlockSpec(weight.shape, lambda r: (0, 0, 0)),
    ]
    operands = [gathered, weight]
    if base is not None:
        in_specs.insert(0, rows)
        operands.insert(0, base)
    flops = 2 * groups * per_frame * width * columns
    return pl.pallas_call(
        _project_body(groups, row0, width, base is not None),
        out_shape=jax.ShapeDtypeStruct((per_frame, columns), dtype),
        grid=(per_frame // block,),
        in_specs=in_specs,
        out_specs=rows,
        cost_estimate=pl.CostEstimate(flops=flops, transcendentals=0, bytes_accessed=4 << 20),
        compiler_params=pltpu.CompilerParams(vmem_limit_bytes=40 << 20),
        name=name,
    )(*operands)


def on_device(queries, keys, values, out_weight, span, counts):
    per_frame, head_width = queries.shape
    frames = lax.axis_size("frame")
    groups = lax.axis_size("head")
    frame = lax.axis_index("frame").astype(jnp.int32).reshape(1)
    scalars = (frame, span, counts)
    swap = [(i, i ^ 1) for i in range(frames)]
    by_chip = [(i, i + 2) for i in range(frames - 2)]
    to_even = [(i, i + 1) for i in range(1, frames - 1, 2)]
    after = lax.optimization_barrier

    def send(block, route):
        return lax.ppermute(block, "frame", route)

    def pack(lo, hi):
        return jnp.concatenate([keys[:, lo:hi], values[:, lo:hi]], axis=1)

    def attend_a(sources, hops, state, hand_over, name):
        return attention_call(scalars, queries, q_other, sources, hops, state, 0, 2, hand_over, name)

    def attend_b(sources, hops, state, hand_over, name):
        return attention_call(scalars, queries, q_other, sources, hops, state, 2, 1, hand_over, name)

    a0 = pack(0, 2 * HD)
    a1 = send(a0, by_chip)
    q_other = send(queries, swap)
    blocks = column_blocks(out_weight, groups)
    weight = lax.all_to_all(blocks, "head", split_axis=0, concat_axis=0, tiled=True)
    b0 = pack(2 * HD, 3 * HD)

    a1, q_other, b0, blocks = after((a1, q_other, b0, blocks))
    a2 = send(a1, by_chip)
    b1 = send(b0, by_chip)
    state_a = attend_a([a0, a1], (0, 1), None, False, "attend_a01")

    a2, b1, state_a = after((a2, b1, state_a))
    a3 = send(a2, by_chip)
    b2 = send(b1, by_chip)
    state_a = attend_a([a2], (2,), state_a, False, "attend_a2")
    state_b = attend_b([b0, b1], (0, 1), None, False, "attend_b01")

    a3, b2, state_a, state_b = after((a3, b2, state_a, state_b))
    a4 = send(a3, to_even)
    *own_a, packed_a = attend_a([a3], (3,), state_a, True, "attend_a3")
    from_other_a = send(packed_a, swap)
    b2, packed_a = after((b2, packed_a))
    b3 = send(b2, by_chip)
    state_b = attend_b([b2], (2,), state_b, False, "attend_b2")
    attended_a = finish_call(scalars, queries, a4, own_a, from_other_a, 0, 2, "finish_a")
    gathered_a = lax.all_gather(attended_a, "head", axis=0, tiled=False)

    b4 = send(b3, to_even)
    *own_b, packed_b = attend_b([b3], (3,), state_b, True, "attend_b3")
    from_other_b = send(packed_b, swap)
    attended_b = finish_call(scalars, queries, b4, own_b, from_other_b, 2, 1, "finish_b")
    gathered_b = lax.all_to_all(
        jnp.broadcast_to(attended_b[None], (groups, per_frame, HD)),
        "head", split_axis=0, concat_axis=0, tiled=True,
    )
    base = project_call(None, gathered_b, weight, 2 * HD, jnp.float32, "project_b")
    return project_call(base, gathered_a, weight, 0, jnp.bfloat16, "project_a")


def solution(mesh):
    return jax.shard_map(
        on_device,
        mesh=mesh,
        in_specs=(
            P("frame", "head"),
            P("frame", "head"),
            P("frame", "head"),
            P("head", None),
            P(),
            P(),
        ),
        out_specs=P("frame", "head"),
        check_vma=False,
    )
```

time: 224 us -> 180 us (0.80)
  the two profiles are of different devices: /device:TPU:2 before, /device:TPU:10 now
where the time goes in v1:
time: 180 us; the launch traced here: 179 us
  waiting for transfers between devices  52.5 us (29%)
  blocking collectives  38.9 us (22%)
  Pallas kernels  31.4 us (17%)
  starting transfers between devices  29.9 us (17%)
  between operations  13.7 us (8%)
  local copies, waits for them, and re-layouts  11.6 us (6%)
    ppermute x11, waiting for transfers between devices, send(): return lax.ppermute(block, 'frame', route)  52.5 us
    all_to_all x1, blocking collectives, on_device(): lax.all_to_all(jnp.broadcast_to(attended_b[None], (groups, per_frame, HD)...  38.9 us
    ppermute x11, starting transfers between devices, send(): return lax.ppermute(block, 'frame', route)  22.2 us
    pallas_call x6, Pallas kernels, attention_call(): pl.pallas_call(_attention_body(hops, first, hand_over), out_shape=out_sha...  19.1 us
    unnamed x30, local copies, waits for them, and re-layouts  8.6 us
    all_to_all x1, starting transfers between devices, on_device(): lax.all_to_all(blocks, 'head', split_axis=0, concat_axis=0, tiled=True)  7.69 us
    pallas_call x1, Pallas kernels, column_blocks(): pl.pallas_call(_copy_body, out_shape=jax.ShapeDtypeStruct((groups, rows,...  5.81 us
    pallas_call x2, Pallas kernels, project_call(): pl.pallas_call(_project_body(groups, row0, width, base is not None), out_...  4.28 us
  transfers between devices with their start and end apart: 13, of which 6 were waited for; matrix products, arithmetic and copies ran while one was open for 1% of the time, Pallas kernels for 16%

profile of v1, /device:TPU:10, one launch (start us, length us, event | category | flops | bytes accessed | tf_op | source)
XLA Modules:
  0.0 178.9 jit_solution(2018223845434537899)
XLA Ops:
  9.3 4.3 %collective-permute-start = (bf16[512,512]{1,0:T(8,128)(2,1)}, bf16[512,512]{1,0:T(8,128)(2,1)}, u32[]{:S(2)}, u32[]{:S(2)}) collective-permute-start(bf16[512,512]{1,0:T(8,128)(2,1)} %pad_maximum_fusion.refs_2_.refs_3_), channel_id=1, source_target_pairs={{0,16},{8,24},{16,32},{24,40},{32,48},{40,56},{48,64},{56,72},{64,... | collective-permute-start | bytes 1572872 | tf_op jit(solution)/shard_map/ppermute | solution.py:256
  13.6 1.9 %collective-permute-start.1 = (bf16[512,384]{1,0:T(8,128)(2,1)}, bf16[512,384]{1,0:T(8,128)(2,1)S(1)}, u32[]{:S(2)}, u32[]{:S(2)}) collective-permute-start(bf16[512,384]{1,0:T(8,128)(2,1)} %q_ref.3), channel_id=1, source_target_pairs={{0,8},{8,0},{16,24},{24,16},{32,40},{40,32},{48,56},{56,48},{64,72... | collective-permute-start | bytes 1179656 | tf_op jit(solution)/shard_map/ppermute | solution.py:256
  15.5 5.8 %column_blocks.1 = bf16[8,384,384]{2,1,0:T(8,128)(2,1)} custom-call(bf16[384,3072]{1,0:T(8,128)(2,1)} %in_ref.1), custom_call_target="tpu_custom_call" | custom-call | tf_op jit(solution)/shard_map/column_blocks/pallas_call | solution.py:191
  21.3 7.7 %all-to-all-start.1 = ((bf16[8,384,384]{2,1,0:T(8,128)(2,1)}), bf16[8,384,384]{2,1,0:T(8,128)(2,1)S(1)}, u32[]{:S(2)}, u32[]{:S(2)}) async-start(bf16[8,384,384]{2,1,0:T(8,128)(2,1)} %column_blocks.1), calls=%async_computation.1 | async-start | bytes 4718592 | tf_op jit(solution)/shard_map/all_to_all | solution.py:271
  30.0 6.1 %collective-permute-done.refs_4_.refs_5_ = bf16[512,512]{1,0:T(8,128)(2,1)} collective-permute-done((bf16[512,512]{1,0:T(8,128)(2,1)}, bf16[512,512]{1,0:T(8,128)(2,1)}, u32[]{:S(2)}, u32[]{:S(2)}) %collective-permute-start) | collective-permute-done | bytes 524320 | tf_op jit(solution)/shard_map/ppermute | solution.py:256
  36.1 1.9 %collective-permute-start.2 = (bf16[512,512]{1,0:T(8,128)(2,1)}, bf16[512,512]{1,0:T(8,128)(2,1)}, u32[]{:S(2)}, u32[]{:S(2)}) collective-permute-start(bf16[512,512]{1,0:T(8,128)(2,1)} %collective-permute-done.refs_4_.refs_5_), channel_id=1, source_target_pairs={{0,16},{8,24},{16,32},{24,40},{32,48},{40,56},{48,64},{56,72},{64,... | collective-permute-start | bytes 1572872 | tf_op jit(solution)/shard_map/ppermute | solution.py:256
  38.0 1.9 %collective-permute-start.3 = (bf16[512,256]{1,0:T(8,128)(2,1)S(1)}, bf16[512,256]{1,0:T(8,128)(2,1)}, u32[]{:S(2)}, u32[]{:S(2)}) collective-permute-start(bf16[512,256]{1,0:T(8,128)(2,1)S(1)} %pad_maximum_fusion.1.refs_2_.refs_3_), channel_id=1, source_target_pairs={{0,16},{8,24},{16,32},{24,40},{32,48},{40,56},{48,64},{56,72},{64,... | collective-permute-start | bytes 786440 | tf_op jit(solution)/shard_map/ppermute | solution.py:256
  40.0 6.3 %attend_a01.1 = (f32[2,512,256]{2,1,0:T(8,128)S(1)}, f32[2,512,128]{2,1,0:T(8,128)S(1)}, f32[2,512,256]{2,1,0:T(8,128)S(1)}, f32[2,512,128]{2,1,0:T(8,128)S(1)}) custom-call(s32[1]{0:T(128)} %bitcast.frame_ref, s32[96]{0:T(128)S(1)} %copy-done.13, s32[96]{0:T(128)S(1)} %copy-done.14, bf16[512,384]{1,0:T(8,128)(2,1)S(1)} %copy-done, ...), custom_call_target="tpu_custom_call" | custom-call | flops 2147483648 | bytes 2097152 | tf_op jit(solution)/shard_map/attend_a01/pallas_call | solution.py:117
  46.3 13.9 %collective-permute-done.3.refs_4_.refs_5_ = bf16[512,256]{1,0:T(8,128)(2,1)} collective-permute-done((bf16[512,256]{1,0:T(8,128)(2,1)S(1)}, bf16[512,256]{1,0:T(8,128)(2,1)}, u32[]{:S(2)}, u32[]{:S(2)}) %collective-permute-start.3) | collective-permute-done | bytes 262176 | tf_op jit(solution)/shard_map/ppermute | solution.py:256
  60.2 1.9 %collective-permute-start.4 = (bf16[512,512]{1,0:T(8,128)(2,1)}, bf16[512,512]{1,0:T(8,128)(2,1)S(1)}, u32[]{:S(2)}, u32[]{:S(2)}) collective-permute-start(bf16[512,512]{1,0:T(8,128)(2,1)} %collective-permute-done.2.refs_2_.refs_3_), channel_id=1, source_target_pairs={{0,16},{8,24},{16,32},{24,40},{32,48},{40,56},{48,64},{56,72},{64,... | collective-permute-start | bytes 1572872 | tf_op jit(solution)/shard_map/ppermute | solution.py:256
  62.1 1.9 %collective-permute-start.5 = (bf16[512,256]{1,0:T(8,128)(2,1)}, bf16[512,256]{1,0:T(8,128)(2,1)S(1)}, u32[]{:S(2)}, u32[]{:S(2)}) collective-permute-start(bf16[512,256]{1,0:T(8,128)(2,1)} %collective-permute-done.3.refs_4_.refs_5_), channel_id=1, source_target_pairs={{0,16},{8,24},{16,32},{24,40},{32,48},{40,56},{48,64},{56,72},{64,... | collective-permute-start | bytes 786440 | tf_op jit(solution)/shard_map/ppermute | solution.py:256
  65.0 3.9 %attend_b01.1 = (f32[1,512,256]{2,1,0:T(8,128)S(1)}, f32[1,512,128]{2,1,0:T(8,128)S(1)}, f32[1,512,256]{2,1,0:T(8,128)S(1)}, f32[1,512,128]{2,1,0:T(8,128)S(1)}) custom-call(s32[1]{0:T(128)} %bitcast.frame_ref, s32[96]{0:T(128)S(1)} %copy-done.13, s32[96]{0:T(128)S(1)} %copy-done.14, bf16[512,384]{1,0:T(8,128)(2,1)S(1)} %copy-done, ...), custom_call_target="tpu_custom_call" | custom-call | flops 1073741824 | bytes 1048576 | tf_op jit(solution)/shard_map/attend_b01/pallas_call | solution.py:117
  70.3 3.3 %attend_a2.1 = (f32[2,512,256]{2,1,0:T(8,128)S(1)}, f32[2,512,128]{2,1,0:T(8,128)S(1)}, f32[2,512,256]{2,1,0:T(8,128)S(1)}, f32[2,512,128]{2,1,0:T(8,128)S(1)}) custom-call(s32[1]{0:T(128)} %bitcast.frame_ref, s32[96]{0:T(128)S(1)} %copy-done.13, s32[96]{0:T(128)S(1)} %copy-done.14, bf16[512,384]{1,0:T(8,128)(2,1)S(1)} %copy-done, ...), custom_call_target="tpu_custom_call" | custom-call | flops 1073741824 | bytes 2097152 | tf_op jit(solution)/shard_map/attend_a2/pallas_call | solution.py:117
  73.6 9.7 %collective-permute-done.5.refs_2_.refs_3_ = bf16[512,256]{1,0:T(8,128)(2,1)S(1)} collective-permute-done((bf16[512,256]{1,0:T(8,128)(2,1)}, bf16[512,256]{1,0:T(8,128)(2,1)S(1)}, u32[]{:S(2)}, u32[]{:S(2)}) %collective-permute-start.5) | collective-permute-done | bytes 262176 | tf_op jit(solution)/shard_map/ppermute | solution.py:256
  83.2 2.5 %attend_a3.1 = (f32[2,512,256]{2,1,0:T(8,128)S(1)}, f32[2,512,128]{2,1,0:T(8,128)S(1)}, f32[2,512,256]{2,1,0:T(8,128)S(1)}) custom-call(s32[1]{0:T(128)} %bitcast.frame_ref, s32[96]{0:T(128)S(1)} %copy-done.13, s32[96]{0:T(128)S(1)} %copy-done.14, bf16[512,384]{1,0:T(8,128)(2,1)S(1)} %copy-done, bf16[512,384]{1,0:T(8,128)(2,1)S(1)} %collective-permute-done.1.refs_1_, ...), custom_call_target="tpu_custom_call" | custom-call | flops 1073741824 | bytes 2097152 | tf_op jit(solution)/shard_map/attend_a3/pallas_call | solution.py:117
  85.8 1.9 %collective-permute-start.10 = (f32[2,512,256]{2,1,0:T(8,128)S(1)}, f32[2,512,256]{2,1,0:T(8,128)S(1)}, u32[]{:S(2)}, u32[]{:S(2)}) collective-permute-start(f32[2,512,256]{2,1,0:T(8,128)S(1)} %get-tuple-element.74), channel_id=1, source_target_pairs={{0,8},{8,0},{16,24},{24,16},{32,40},{40,32},{48,56},{56,48},{64,72... | collective-permute-start | bytes 3145736 | tf_op jit(solution)/shard_map/ppermute | solution.py:256
  87.7 1.3 collective-permute-start.9
  89.0 11.3 %collective-permute-done.9.k_ref.v_ref = bf16[512,512]{1,0:T(8,128)(2,1)S(1)} collective-permute-done((bf16[512,512]{1,0:T(8,128)(2,1)S(1)}, bf16[512,512]{1,0:T(8,128)(2,1)S(1)}, u32[]{:S(2)}, u32[]{:S(2)}) %collective-permute-start.9) | collective-permute-done | bytes 524320 | tf_op jit(solution)/shard_map/ppermute | solution.py:256
  100.3 1.3 finish_a.1
  102.4 1.9 %collective-permute-start.6 = (bf16[512,256]{1,0:T(8,128)(2,1)S(1)}, bf16[512,256]{1,0:T(8,128)(2,1)S(1)}, u32[]{:S(2)}, u32[]{:S(2)}) collective-permute-start(bf16[512,256]{1,0:T(8,128)(2,1)S(1)} %collective-permute-done.5.refs_2_.refs_3_), channel_id=1, source_target_pairs={{0,16},{8,24},{16,32},{24,40},{32,48},{40,56},{48,64},{56,72},{64,... | collective-permute-start | bytes 786440 | tf_op jit(solution)/shard_map/ppermute | solution.py:256
  104.3 1.0 copy-done.4
  105.4 1.0 copy-done.6
  108.3 1.5 attend_b2.1
  109.8 3.0 %collective-permute-done.6.refs_2_.refs_3_ = bf16[512,256]{1,0:T(8,128)(2,1)S(1)} collective-permute-done((bf16[512,256]{1,0:T(8,128)(2,1)S(1)}, bf16[512,256]{1,0:T(8,128)(2,1)S(1)}, u32[]{:S(2)}, u32[]{:S(2)}) %collective-permute-start.6) | collective-permute-done | bytes 262176 | tf_op jit(solution)/shard_map/ppermute | solution.py:256
  112.8 1.7 attend_b3.1
  114.4 1.9 %collective-permute-start.8 = (f32[1,512,256]{2,1,0:T(8,128)S(1)}, f32[1,512,256]{2,1,0:T(8,128)S(1)}, u32[]{:S(2)}, u32[]{:S(2)}) collective-permute-start(f32[1,512,256]{2,1,0:T(8,128)S(1)} %get-tuple-element.86), channel_id=1, source_target_pairs={{0,8},{8,0},{16,24},{24,16},{32,40},{40,32},{48,56},{56,48},{64,72... | collective-permute-start | bytes 1572872 | tf_op jit(solution)/shard_map/ppermute | solution.py:256
  116.4 1.3 collective-permute-start.7
  117.7 8.5 %collective-permute-done.7.k_ref.v_ref = bf16[512,256]{1,0:T(8,128)(2,1)S(1)} collective-permute-done((bf16[512,256]{1,0:T(8,128)(2,1)S(1)}, bf16[512,256]{1,0:T(8,128)(2,1)S(1)}, u32[]{:S(2)}, u32[]{:S(2)}) %collective-permute-start.7) | collective-permute-done | bytes 262176 | tf_op jit(solution)/shard_map/ppermute | solution.py:256
  127.2 38.9 %all_to_all.10.refs_0_ = bf16[8,512,128]{2,1,0:T(8,128)(2,1)S(1)} all-to-all(bf16[8,512,128]{2,1,0:T(8,128)(2,1)S(1)} %broadcast_in_dim.2), channel_id=1, replica_groups=mesh['frame'=96,'head'=8] {'head'}, dimensions={0} | all-to-all | bytes 2097152 | tf_op jit(solution)/shard_map/all_to_all | solution.py:299
  166.1 1.5 project_b.1.refs_0_
  167.7 1.6 copy-done.1
  169.3 2.7 %project_a.1 = bf16[512,384]{1,0:T(8,128)(2,1)} custom-call(f32[512,384]{1,0:T(8,128)S(1)} %project_b.1.refs_0_, bf16[8,512,256]{2,1,0:T(8,128)(2,1)S(1)} %bitcast.2, bf16[8,384,384]{2,1,0:T(8,128)(2,1)S(1)} %all-to-all-done.1.refs_1_.refs_2_), custom_call_target="tpu_custom_call" | custom-call | flops 805306368 | bytes 4194304 | tf_op jit(solution)/shard_map/project_a/pallas_call | solution.py:232
  (45 shorter events, 9.7 us)
Async XLA Ops:
  9.3 26.8 %collective-permute-start = (bf16[512,512]{1,0:T(8,128)(2,1)}, bf16[512,512]{1,0:T(8,128)(2,1)}, u32[]{:S(2)}, u32[]{:S(2)}) collective-permute-start(bf16[512,512]{1,0:T(8,128)(2,1)} %pad_maximum_fusion.refs_2_.refs_3_), channel_id=1, source_target_pairs={{0,16},{8,24},{16,32},{24,40},{32,48},{40,56},{48,64},{56,72},{64,... | collective-permute-start | bytes 1572872 | tf_op jit(solution)/shard_map/ppermute | solution.py:256
  13.6 16.4 %collective-permute-start.1 = (bf16[512,384]{1,0:T(8,128)(2,1)}, bf16[512,384]{1,0:T(8,128)(2,1)S(1)}, u32[]{:S(2)}, u32[]{:S(2)}) collective-permute-start(bf16[512,384]{1,0:T(8,128)(2,1)} %q_ref.3), channel_id=1, source_target_pairs={{0,8},{8,0},{16,24},{24,16},{32,40},{40,32},{48,56},{56,48},{64,72... | collective-permute-start | bytes 1179656 | tf_op jit(solution)/shard_map/ppermute | solution.py:256
  21.3 8.6 %slice-start = ((bf16[512,384]{1,0:T(8,128)(2,1)}), bf16[512,128]{1,0:T(8,128)(2,1)S(1)}, s32[]{:S(2)}) async-start(bf16[512,384]{1,0:T(8,128)(2,1)} %param.8), calls=%async_computation.3 | async-start | bytes 262144 | tf_op jit(solution)/shard_map/slice | solution.py:259
  21.3 18.6 %copy-start = (bf16[512,384]{1,0:T(8,128)(2,1)S(1)}, bf16[512,384]{1,0:T(8,128)(2,1)}, u32[]{:S(2)}) copy-start(bf16[512,384]{1,0:T(8,128)(2,1)} %q_ref.3) | copy-start | bytes 1179652
  21.3 18.6 %copy-start.13 = (s32[96]{0:T(128)S(1)}, s32[96]{0:T(128)}, u32[]{:S(2)}) copy-start(s32[96]{0:T(128)} %span_ref.15) | copy-start | bytes 1156
  21.3 18.6 %copy-start.14 = (s32[96]{0:T(128)S(1)}, s32[96]{0:T(128)}, u32[]{:S(2)}) copy-start(s32[96]{0:T(128)} %counts_ref.15) | copy-start | bytes 1156
  21.3 105.7 %all-to-all-start.1 = ((bf16[8,384,384]{2,1,0:T(8,128)(2,1)}), bf16[8,384,384]{2,1,0:T(8,128)(2,1)S(1)}, u32[]{:S(2)}, u32[]{:S(2)}) async-start(bf16[8,384,384]{2,1,0:T(8,128)(2,1)} %column_blocks.1), calls=%async_computation.1 | async-start | bytes 4718592 | tf_op jit(solution)/shard_map/all_to_all | solution.py:271
  29.0 138.7 %all-gather.3.cloned.1.call-start = ((), (), s32[]{:S(2)}) async-start(), calls=%async_computation.2 | async-start | bytes 2359296 | tf_op jit(solution)/shard_map/all_gather | solution.py:293
  30.0 16.3 %copy-start.11 = (bf16[512,256]{1,0:T(8,128)(2,1)}, bf16[512,256]{1,0:T(8,128)(2,1)S(1)}, u32[]{:S(2)}) copy-start(bf16[512,256]{1,0:T(8,128)(2,1)S(1)} %pad_maximum_fusion.1.refs_2_.refs_3_) | copy-start | bytes 786436
  36.1 24.1 %collective-permute-start.2 = (bf16[512,512]{1,0:T(8,128)(2,1)}, bf16[512,512]{1,0:T(8,128)(2,1)}, u32[]{:S(2)}, u32[]{:S(2)}) collective-permute-start(bf16[512,512]{1,0:T(8,128)(2,1)} %collective-permute-done.refs_4_.refs_5_), channel_id=1, source_target_pairs={{0,16},{8,24},{16,32},{24,40},{32,48},{40,56},{48,64},{56,72},{64,... | collective-permute-start | bytes 1572872 | tf_op jit(solution)/shard_map/ppermute | solution.py:256
  38.0 22.2 %collective-permute-start.3 = (bf16[512,256]{1,0:T(8,128)(2,1)S(1)}, bf16[512,256]{1,0:T(8,128)(2,1)}, u32[]{:S(2)}, u32[]{:S(2)}) collective-permute-start(bf16[512,256]{1,0:T(8,128)(2,1)S(1)} %pad_maximum_fusion.1.refs_2_.refs_3_), channel_id=1, source_target_pairs={{0,16},{8,24},{16,32},{24,40},{32,48},{40,56},{48,64},{56,72},{64,... | collective-permute-start | bytes 786440 | tf_op jit(solution)/shard_map/ppermute | solution.py:256
  60.2 23.0 %collective-permute-start.4 = (bf16[512,512]{1,0:T(8,128)(2,1)}, bf16[512,512]{1,0:T(8,128)(2,1)S(1)}, u32[]{:S(2)}, u32[]{:S(2)}) collective-permute-start(bf16[512,512]{1,0:T(8,128)(2,1)} %collective-permute-done.2.refs_2_.refs_3_), channel_id=1, source_target_pairs={{0,16},{8,24},{16,32},{24,40},{32,48},{40,56},{48,64},{56,72},{64,... | collective-permute-start | bytes 1572872 | tf_op jit(solution)/shard_map/ppermute | solution.py:256
  62.1 21.1 %collective-permute-start.5 = (bf16[512,256]{1,0:T(8,128)(2,1)}, bf16[512,256]{1,0:T(8,128)(2,1)S(1)}, u32[]{:S(2)}, u32[]{:S(2)}) collective-permute-start(bf16[512,256]{1,0:T(8,128)(2,1)} %collective-permute-done.3.refs_4_.refs_5_), channel_id=1, source_target_pairs={{0,16},{8,24},{16,32},{24,40},{32,48},{40,56},{48,64},{56,72},{64,... | collective-permute-start | bytes 786440 | tf_op jit(solution)/shard_map/ppermute | solution.py:256
  64.0 1.0 copy-start.12
  68.9 0.7 copy-start.7
  69.6 0.7 copy-start.9
  70.3 3.3 %copy-start.3 = (f32[1,512,256]{2,1,0:T(8,128)}, f32[1,512,256]{2,1,0:T(8,128)S(1)}, u32[]{:S(2)}) copy-start(f32[1,512,256]{2,1,0:T(8,128)S(1)} %get-tuple-element.76.refs_4_) | copy-start | bytes 1572868
  70.3 3.3 %copy-start.5 = (f32[1,512,256]{2,1,0:T(8,128)}, f32[1,512,256]{2,1,0:T(8,128)S(1)}, u32[]{:S(2)}) copy-start(f32[1,512,256]{2,1,0:T(8,128)S(1)} %get-tuple-element.78.refs_6_) | copy-start | bytes 1572868
  85.8 14.5 %collective-permute-start.10 = (f32[2,512,256]{2,1,0:T(8,128)S(1)}, f32[2,512,256]{2,1,0:T(8,128)S(1)}, u32[]{:S(2)}, u32[]{:S(2)}) collective-permute-start(f32[2,512,256]{2,1,0:T(8,128)S(1)} %get-tuple-element.74), channel_id=1, source_target_pairs={{0,8},{8,0},{16,24},{24,16},{32,40},{40,32},{48,56},{56,48},{64,72... | collective-permute-start | bytes 3145736 | tf_op jit(solution)/shard_map/ppermute | solution.py:256
  87.7 12.6 %collective-permute-start.9 = (bf16[512,512]{1,0:T(8,128)(2,1)S(1)}, bf16[512,512]{1,0:T(8,128)(2,1)S(1)}, u32[]{:S(2)}, u32[]{:S(2)}) collective-permute-start(bf16[512,512]{1,0:T(8,128)(2,1)S(1)} %collective-permute-done.4.refs_2_.refs_3_), channel_id=1, source_target_pairs={{8,16},{24,32},{40,48},{56,64},{72,80},{88,96},{104,112},{120,128}... | collective-permute-start | bytes 1572872 | tf_op jit(solution)/shard_map/ppermute | solution.py:256
  101.7 0.7 copy-start.2
  102.4 10.4 %collective-permute-start.6 = (bf16[512,256]{1,0:T(8,128)(2,1)S(1)}, bf16[512,256]{1,0:T(8,128)(2,1)S(1)}, u32[]{:S(2)}, u32[]{:S(2)}) collective-permute-start(bf16[512,256]{1,0:T(8,128)(2,1)S(1)} %collective-permute-done.5.refs_2_.refs_3_), channel_id=1, source_target_pairs={{0,16},{8,24},{16,32},{24,40},{32,48},{40,56},{48,64},{56,72},{64,... | collective-permute-start | bytes 786440 | tf_op jit(solution)/shard_map/ppermute | solution.py:256
  104.3 1.0 copy-start.4
  105.4 1.0 copy-start.6
  106.4 0.9 copy-start.8
  107.4 0.9 copy-start.10
  114.4 11.7 %collective-permute-start.8 = (f32[1,512,256]{2,1,0:T(8,128)S(1)}, f32[1,512,256]{2,1,0:T(8,128)S(1)}, u32[]{:S(2)}, u32[]{:S(2)}) collective-permute-start(f32[1,512,256]{2,1,0:T(8,128)S(1)} %get-tuple-element.86), channel_id=1, source_target_pairs={{0,8},{8,0},{16,24},{24,16},{32,40},{40,32},{48,56},{56,48},{64,72... | collective-permute-start | bytes 1572872 | tf_op jit(solution)/shard_map/ppermute | solution.py:256
  116.4 9.8 %collective-permute-start.7 = (bf16[512,256]{1,0:T(8,128)(2,1)S(1)}, bf16[512,256]{1,0:T(8,128)(2,1)S(1)}, u32[]{:S(2)}, u32[]{:S(2)}) collective-permute-start(bf16[512,256]{1,0:T(8,128)(2,1)S(1)} %collective-permute-done.6.refs_2_.refs_3_), channel_id=1, source_target_pairs={{8,16},{24,32},{40,48},{56,64},{72,80},{88,96},{104,112},{120,128}... | collective-permute-start | bytes 786440 | tf_op jit(solution)/shard_map/ppermute | solution.py:256
  167.7 1.6 copy-start.1
Sparse Core Ops, SparseCore 0:
  102.5 59.5 all-gather.2

commit v2 on v1

v2 whole, which is shorter than its diff:
```python
import jax
import jax.numpy as jnp
from jax import lax
from jax.experimental import pallas as pl
from jax.experimental.pallas import tpu as pltpu
from jax.sharding import PartitionSpec as P

HD = 128
WIN = 8
NEG = -1e30
EXP2_SCALE = HD ** (-0.5) * 1.4426950408889634
ROW_BLOCK = 256
SMALL_VMEM = 16 << 20
LARGE_VMEM = 24 << 20
BRIEF = pl.CostEstimate(flops=1, transcendentals=0, bytes_accessed=1)


def _attend(limit, q_ref, k_ref, v_ref, acc_ref, top_ref):
    slots = k_ref.shape[0]

    @pl.when(limit > 0)
    def _():
        keys = k_ref[...]
        values = jnp.concatenate([v_ref[...], jnp.ones((slots, HD), jnp.bfloat16)], axis=1)
        slot = lax.broadcasted_iota(jnp.int32, (1, slots), 1)
        hidden = jnp.where(slot < limit, 0.0, NEG)
        for start in range(0, q_ref.shape[0], ROW_BLOCK):
            rows = pl.ds(start, ROW_BLOCK)
            scores = lax.dot_general(
                q_ref[rows, :], keys, (((1,), (1,)), ((), ())), preferred_element_type=jnp.float32
            )
            scores = scores + hidden
            old_top = top_ref[0, rows, :]
            new_top = jnp.maximum(old_top, jnp.max(scores, axis=1, keepdims=True))
            wide_top = jnp.tile(new_top, (1, slots // HD))
            weights = jnp.exp2((scores - wide_top) * EXP2_SCALE).astype(jnp.bfloat16)
            rescale = jnp.exp2((old_top - new_top) * EXP2_SCALE)
            acc_ref[0, rows, :] = acc_ref[0, rows, :] * jnp.tile(rescale, (1, 2)) + jnp.dot(
                weights, values, preferred_element_type=jnp.float32
            )
            top_ref[0, rows, :] = new_top


def _visible(frame, side, behind, span_ref, counts_ref):
    query = frame if side == 0 else frame + 1 - 2 * (frame % 2)
    source = frame - behind
    back = query - source
    seen = (source >= 0) & (back >= 0) & (back < span_ref[query])
    return jnp.where(seen, counts_ref[jnp.maximum(source, 0)], 0)


def in_hbm(array):
    return pltpu.with_memory_space_constraint(array, pltpu.HBM)


def _start(acc, top):
    acc[...] = jnp.zeros_like(acc)
    top[...] = jnp.full_like(top, NEG)


def _attention_body(hops, first, hand_over):
    def body(frame_ref, span_ref, counts_ref, *refs):
        refs = list(refs)
        q_refs = [refs.pop(0), refs.pop(0)]
        kv_refs = [(refs.pop(0), refs.pop(0)) for _ in hops]
        if first:
            state_in = None
        else:
            state_in = [refs.pop(0) for _ in range(4)]
        if hand_over:
            own_acc, own_top, packed, other_acc, other_top = refs
        else:
            own_acc, own_top, other_acc, other_top = refs
        state = (own_acc, own_top, other_acc, other_top)
        if first:
            _start(own_acc, own_top)
            _start(other_acc, other_top)
        else:
            for ref, ref_in in zip(state, state_in):
                ref[...] = ref_in[...]
        frame = frame_ref[0]
        for hop, (k_ref, v_ref) in zip(hops, kv_refs):
            for side in (0, 1):
                limit = _visible(frame, side, 2 * hop, span_ref, counts_ref)
                _attend(limit, q_refs[side], k_ref, v_ref, state[2 * side], state[2 * side + 1])
        if hand_over:
            lane = lax.broadcasted_iota(jnp.int32, (1, HD), 1)
            packed[0, :, :HD] = other_acc[0, :, :HD]
            packed[0, :, HD:] = jnp.where(lane < HD // 2, other_top[0], other_acc[0, :, HD:])

    return body


def attention_call(scalars, q_own, q_other, sources, hops, state, hand_over, name):
    per_frame, width = q_own.shape
    heads = width // HD
    first = state is None
    column = pl.BlockSpec((per_frame, HD), lambda h, *_: (0, h))
    acc_spec = pl.BlockSpec((1, per_frame, 2 * HD), lambda h, *_: (h, 0, 0))
    top_spec = pl.BlockSpec((1, per_frame, HD), lambda h, *_: (h, 0, 0))
    in_specs = [column, column]
    operands = [q_own, q_other]
    for keys_and_values in sources:
        in_specs += [column, column]
        operands += keys_and_values
    if not first:
        in_specs += [acc_spec, top_spec] * 2
        operands += [in_hbm(x) for x in state]
    acc_shape = jax.ShapeDtypeStruct((heads, per_frame, 2 * HD), jnp.float32)
    top_shape = jax.ShapeDtypeStruct((heads, per_frame, HD), jnp.float32)
    scratch = []
    if hand_over:
        out_specs = [acc_spec, top_spec, acc_spec]
        out_shape = [acc_shape, top_shape, acc_shape]
        scratch = [
            pltpu.VMEM((1, per_frame, 2 * HD), jnp.float32),
            pltpu.VMEM((1, per_frame, HD), jnp.float32),
        ]
    else:
        out_specs = [acc_spec, top_spec] * 2
        out_shape = [pltpu.HBM(s.shape, s.dtype) for s in [acc_shape, top_shape] * 2]
    return pl.pallas_call(
        _attention_body(hops, first, hand_over),
        out_shape=out_shape,
        grid_spec=pltpu.PrefetchScalarGridSpec(
            num_scalar_prefetch=3,
            grid=(heads,),
            in_specs=in_specs,
            out_specs=out_specs,
            scratch_shapes=scratch,
        ),
        cost_estimate=BRIEF,
        compiler_params=pltpu.CompilerParams(vmem_limit_bytes=SMALL_VMEM),
        name=name,
    )(*scalars, *operands)


def _finish_body(frame_ref, span_ref, counts_ref, q_ref, k_ref, v_ref, acc_in, top_in, packed, upper_ref, lower_ref, acc, top):
    acc[...] = acc_in[...]
    top[...] = top_in[...]
    limit = _visible(frame_ref[0], 0, WIN - 1, span_ref, counts_ref)
    limit = jnp.where(frame_ref[0] % 2 == 0, limit, 0)
    _attend(limit, q_ref, k_ref, v_ref, acc, top)
    own_top, other_top = top[0], packed[0, :, HD : HD + 1]
    own_total, other_total = acc[0, :, HD:], packed[0, :, 2 * HD - 1 :]
    both_top = jnp.maximum(own_top, other_top)
    own_part = jnp.exp2((own_top - both_top) * EXP2_SCALE)
    other_part = jnp.exp2((other_top - both_top) * EXP2_SCALE)
    total = own_total * own_part + other_total * other_part
    mixed = acc[0, :, :HD] * own_part + packed[0, :, :HD] * other_part
    mixed = (mixed / total).astype(jnp.bfloat16)
    half = upper_ref.shape[0]
    upper_ref[...] = mixed[:half]
    lower_ref[...] = mixed[half:]


def finish_call(scalars, q_own, keys, values, state, packed, name):
    per_frame, width = q_own.shape
    heads = width // HD
    column = pl.BlockSpec((per_frame, HD), lambda h, *_: (0, h))
    acc_spec = pl.BlockSpec((1, per_frame, 2 * HD), lambda h, *_: (h, 0, 0))
    top_spec = pl.BlockSpec((1, per_frame, HD), lambda h, *_: (h, 0, 0))
    return pl.pallas_call(
        _finish_body,
        out_shape=[jax.ShapeDtypeStruct((per_frame // 2, width), jnp.bfloat16)] * 2,
        grid_spec=pltpu.PrefetchScalarGridSpec(
            num_scalar_prefetch=3,
            grid=(heads,),
            in_specs=[
                column,
                column,
                column,
                acc_spec,
                top_spec,
                acc_spec,
            ],
            out_specs=[pl.BlockSpec((per_frame // 2, HD), lambda h, *_: (0, h))] * 2,
            scratch_shapes=[
                pltpu.VMEM((1, per_frame, 2 * HD), jnp.float32),
                pltpu.VMEM((1, per_frame, HD), jnp.float32),
            ],
        ),
        cost_estimate=BRIEF,
        compiler_params=pltpu.CompilerParams(vmem_limit_bytes=SMALL_VMEM),
        name=name,
    )(*scalars, q_own, keys, values, *state, packed)


def _column_blocks_body(w_ref, out_ref):
    groups, _, columns = out_ref.shape
    for group in range(groups):
        out_ref[group] = w_ref[:, group * columns : (group + 1) * columns]


def column_blocks(weight, groups):
    rows, width = weight.shape
    columns = width // groups
    return pl.pallas_call(
        _column_blocks_body,
        out_shape=pltpu.HBM((groups, rows, columns), weight.dtype),
        grid=(2,),
        in_specs=[pl.BlockSpec((rows // 2, width), lambda r: (r, 0))],
        out_specs=pl.BlockSpec((groups, rows // 2, columns), lambda r: (0, r, 0)),
        cost_estimate=BRIEF,
        compiler_params=pltpu.CompilerParams(vmem_limit_bytes=SMALL_VMEM),
        name="column_blocks",
    )(in_hbm(weight))


def _project_body(places, has_base):
    def body(group_ref, *refs):
        out_ref, w_ref = refs[-1], refs[-2]
        groups, half = w_ref.shape[0], out_ref.shape[0] // 2
        for part in (0, 1):
            rows = pl.ds(part * half, half)
            total = refs[0][rows, :] if has_base else None
            for (place, offset), ref in zip(places, refs[has_base:-2], strict=True):
                if place == part:
                    source = lax.rem(group_ref[0] + offset, groups)
                    product = jnp.dot(ref[...], w_ref[source], preferred_element_type=jnp.float32)
                    total = product if total is None else total + product
            out_ref[rows, :] = total.astype(out_ref.dtype)

    return body


def project_call(group, weight, base, pieces, places, dtype, name):
    groups, height, columns = weight.shape
    half = pieces[0].shape[0]
    operands = ([] if base is None else [base]) + list(pieces) + [weight]
    return pl.pallas_call(
        _project_body(places, base is not None),
        out_shape=jax.ShapeDtypeStruct((2 * half, columns), dtype),
        grid_spec=pltpu.PrefetchScalarGridSpec(
            num_scalar_prefetch=1,
            grid=(1,),
            in_specs=[pl.BlockSpec(x.shape, lambda i, g, n=x.ndim: (0,) * n) for x in operands],
            out_specs=pl.BlockSpec((2 * half, columns), lambda i, g: (0, 0)),
        ),
        cost_estimate=pl.CostEstimate(
            flops=2 * len(pieces) * half * height * columns, transcendentals=0, bytes_accessed=4 << 20
        ),
        compiler_params=pltpu.CompilerParams(vmem_limit_bytes=LARGE_VMEM),
        name=name,
    )(group, *operands)


def on_device(queries, keys, values, out_weight, span, counts):
    per_frame, head_width = queries.shape
    frames = lax.axis_size("frame")
    groups = lax.axis_size("head")
    frame = lax.axis_index("frame").astype(jnp.int32).reshape(1)
    group = lax.axis_index("head").astype(jnp.int32).reshape(1)
    scalars = (frame, span, counts)
    swap = [(i, i ^ 1) for i in range(frames)]
    by_chip = [(i, i + 2) for i in range(frames - 2)]
    to_even = [(i, i + 1) for i in range(1, frames - 1, 2)]
    upward = [(i, (i + 1) % groups) for i in range(groups)]
    downward = [(i, (i - 1) % groups) for i in range(groups)]
    after = lax.optimization_barrier

    def send(block, route, axis="frame"):
        return lax.ppermute(block, axis, route)

    def attend(sources, hops, state, hand_over, name):
        return attention_call(
            scalars, in_hbm(queries), q_other, sources, hops, state, hand_over, name
        )

    k1, v1 = send(keys, by_chip), send(values, by_chip)
    q_other = send(queries, swap)
    blocks, v1 = after((column_blocks(out_weight, groups), v1))
    weight = lax.all_to_all(blocks, "head", split_axis=0, concat_axis=0, tiled=True)
    k2, v2 = send(k1, by_chip), send(v1, by_chip)
    state = attend([(in_hbm(keys), in_hbm(values)), (k1, v1)], (0, 1), None, False, "attend_01")
    k2, v2, state = after((k2, v2, state))
    k3, v3 = send(k2, by_chip), send(v2, by_chip)
    state = attend([(k2, v2)], (2,), state, False, "attend_2")
    k3, v3, state = after((k3, v3, state))
    k4, v4 = send(k3, to_even), send(v3, to_even)
    *own, packed = attend([(k3, v3)], (3,), state, True, "attend_3")
    attended = finish_call(scalars, in_hbm(queries), k4, v4, own, send(packed, swap), "finish")

    def project(base, pieces, places, dtype, name):
        return project_call(group, weight, base, pieces, places, dtype, name)

    up, down = list(attended), list(attended)
    held, places, total = list(attended), ((0, 0), (1, 0)), None
    for step in (1, 2, 3):
        up = [send(block, upward, "head") for block in up]
        down = [send(block, downward, "head") for block in down]
        total = project(total, held, places, jnp.float32, f"project_{step - 1}")
        held = up + down
        places = ((0, groups - step), (1, groups - step), (0, step), (1, step))
        up[1], down[1], total = after((up[1], down[1], total))
    far = [send(up[0], upward, "head"), send(down[1], downward, "head")]
    total = project(total, held, places, jnp.float32, "project_3")
    return project(total, far, ((0, 4), (1, 4)), jnp.bfloat16, "project_4")


def solution(mesh):
    return jax.shard_map(
        on_device,
        mesh=mesh,
        in_specs=(
            P("frame", "head"),
            P("frame", "head"),
            P("frame", "head"),
            P("head", None),
            P(),
            P(),
        ),
        out_specs=P("frame", "head"),
        check_vma=False,
    )
```

time: 180 us -> 171 us (0.950)
  the two profiles are of different devices: /device:TPU:10 before, /device:TPU:26 now
where the time goes in v2:
time: 171 us; the launch traced here: 170 us
  starting transfers between devices  74 us (43%)
  waiting for transfers between devices  62.9 us (37%)
  Pallas kernels  33.1 us (19%)
    ppermute x24, starting transfers between devices, send(): return lax.ppermute(block, axis, route)  66.7 us
    ppermute x24, waiting for transfers between devices, send(): return lax.ppermute(block, axis, route)  62.9 us
    pallas_call x3, Pallas kernels, attention_call(): pl.pallas_call(_attention_body(hops, first, hand_over), out_shape=out_sha...  22.3 us
    all_to_all x1, starting transfers between devices, on_device(): lax.all_to_all(blocks, 'head', split_axis=0, concat_axis=0, tiled=True)  7.32 us
    pallas_call x5, Pallas kernels, project_call(): pl.pallas_call(_project_body(places, base is not None), out_shape=jax.Sha...  4.39 us
    pallas_call x1, Pallas kernels, finish_call(): pl.pallas_call(_finish_body, out_shape=[jax.ShapeDtypeStruct((per_frame /...  3.56 us
  transfers between devices with their start and end apart: 25, of which 9 were waited for; matrix products, arithmetic and copies ran while one was open for 0% of the time, Pallas kernels for 19%

profile of v2, /device:TPU:26, one launch (start us, length us, event | category | flops | bytes accessed | tf_op | source)
XLA Modules:
  0.0 170.3 jit_solution(16958377138585630741)
XLA Ops:
  0.0 4.3 %collective-permute-start.2 = (bf16[512,384]{1,0:T(8,128)(2,1)}, bf16[512,384]{1,0:T(8,128)(2,1)S(1)}, u32[]{:S(2)}, u32[]{:S(2)}) collective-permute-start(bf16[512,384]{1,0:T(8,128)(2,1)} %refs_3_.1), channel_id=1, source_target_pairs={{0,16},{8,24},{16,32},{24,40},{32,48},{40,56},{48,64},{56,72},{64,... | collective-permute-start | bytes 1179656 | tf_op jit(solution)/shard_map/ppermute | solution.py:263
  4.3 2.8 %column_blocks.1 = bf16[8,384,384]{2,1,0:T(8,128)(2,1)} custom-call(bf16[384,3072]{1,0:T(8,128)(2,1)} %w_ref.1), custom_call_target="tpu_custom_call" | custom-call | flops 1 | bytes 1 | tf_op jit(solution)/shard_map/column_blocks/pallas_call | solution.py:198
  7.1 16.8 %collective-permute-done.2.refs_5_ = bf16[512,384]{1,0:T(8,128)(2,1)S(1)} collective-permute-done((bf16[512,384]{1,0:T(8,128)(2,1)}, bf16[512,384]{1,0:T(8,128)(2,1)S(1)}, u32[]{:S(2)}, u32[]{:S(2)}) %collective-permute-start.2) | collective-permute-done | bytes 393248 | tf_op jit(solution)/shard_map/ppermute | solution.py:263
  23.9 7.3 %all-to-all-start = ((bf16[8,384,384]{2,1,0:T(8,128)(2,1)}), bf16[8,384,384]{2,1,0:T(8,128)(2,1)S(1)}, u32[]{:S(2)}, u32[]{:S(2)}) async-start(bf16[8,384,384]{2,1,0:T(8,128)(2,1)} %column_blocks.1), calls=%async_computation | async-start | bytes 4718592 | tf_op jit(solution)/shard_map/all_to_all | solution.py:273
  33.1 1.9 %collective-permute-start.4 = (bf16[512,384]{1,0:T(8,128)(2,1)}, bf16[512,384]{1,0:T(8,128)(2,1)S(1)}, u32[]{:S(2)}, u32[]{:S(2)}) collective-permute-start(bf16[512,384]{1,0:T(8,128)(2,1)} %q_ref.1), channel_id=1, source_target_pairs={{0,8},{8,0},{16,24},{24,16},{32,40},{40,32},{48,56},{56,48},{64,72... | collective-permute-start | bytes 1179656 | tf_op jit(solution)/shard_map/ppermute | solution.py:263
  35.0 10.1 %collective-permute-done.refs_4_ = bf16[512,384]{1,0:T(8,128)(2,1)S(1)} collective-permute-done((bf16[512,384]{1,0:T(8,128)(2,1)}, bf16[512,384]{1,0:T(8,128)(2,1)S(1)}, u32[]{:S(2)}, u32[]{:S(2)}) %collective-permute-start) | collective-permute-done | bytes 393248 | tf_op jit(solution)/shard_map/ppermute | solution.py:263
  47.0 1.9 %collective-permute-start.3 = (bf16[512,384]{1,0:T(8,128)(2,1)S(1)}, bf16[512,384]{1,0:T(8,128)(2,1)}, u32[]{:S(2)}, u32[]{:S(2)}) collective-permute-start(bf16[512,384]{1,0:T(8,128)(2,1)S(1)} %collective-permute-done.2.refs_5_), channel_id=1, source_target_pairs={{0,16},{8,24},{16,32},{24,40},{32,48},{40,56},{48,64},{56,72},{64,... | collective-permute-start | bytes 1179656 | tf_op jit(solution)/shard_map/ppermute | solution.py:263
  49.0 9.6 %attend_01.1 = (f32[3,512,256]{2,1,0:T(8,128)}, f32[3,512,128]{2,1,0:T(8,128)}, f32[3,512,256]{2,1,0:T(8,128)}, f32[3,512,128]{2,1,0:T(8,128)}) custom-call(s32[1]{0:T(128)} %bitcast.1.frame_ref, s32[96]{0:T(128)S(1)} %copy-done, s32[96]{0:T(128)S(1)} %copy-done.1, bf16[512,384]{1,0:T(8,128)(2,1)} %q_ref.1, ...), custom_call_target="tpu_custom_call" | custom-call | flops 1 | bytes 1 | tf_op jit(solution)/shard_map/attend_01/pallas_call | solution.py:122
  58.6 2.7 %collective-permute-done.1.refs_2_ = bf16[512,384]{1,0:T(8,128)(2,1)} collective-permute-done((bf16[512,384]{1,0:T(8,128)(2,1)S(1)}, bf16[512,384]{1,0:T(8,128)(2,1)}, u32[]{:S(2)}, u32[]{:S(2)}) %collective-permute-start.1) | collective-permute-done | bytes 393248 | tf_op jit(solution)/shard_map/ppermute | solution.py:263
  61.3 5.2 %collective-permute-done.3.refs_3_ = bf16[512,384]{1,0:T(8,128)(2,1)} collective-permute-done((bf16[512,384]{1,0:T(8,128)(2,1)S(1)}, bf16[512,384]{1,0:T(8,128)(2,1)}, u32[]{:S(2)}, u32[]{:S(2)}) %collective-permute-start.3) | collective-permute-done | bytes 393248 | tf_op jit(solution)/shard_map/ppermute | solution.py:263
  70.3 7.6 %attend_2.1 = (f32[3,512,256]{2,1,0:T(8,128)}, f32[3,512,128]{2,1,0:T(8,128)}, f32[3,512,256]{2,1,0:T(8,128)}, f32[3,512,128]{2,1,0:T(8,128)}) custom-call(s32[1]{0:T(128)} %bitcast.1.frame_ref, s32[96]{0:T(128)S(1)} %copy-done, s32[96]{0:T(128)S(1)} %copy-done.1, bf16[512,384]{1,0:T(8,128)(2,1)} %q_ref.1, ...), custom_call_target="tpu_custom_call" | custom-call | flops 1 | bytes 1 | tf_op jit(solution)/shard_map/attend_2/pallas_call | solution.py:122
  77.9 4.9 %collective-permute-done.5.refs_2_ = bf16[512,384]{1,0:T(8,128)(2,1)S(1)} collective-permute-done((bf16[512,384]{1,0:T(8,128)(2,1)}, bf16[512,384]{1,0:T(8,128)(2,1)S(1)}, u32[]{:S(2)}, u32[]{:S(2)}) %collective-permute-start.5) | collective-permute-done | bytes 393248 | tf_op jit(solution)/shard_map/ppermute | solution.py:263
  82.7 4.3 %collective-permute-done.6.refs_3_ = bf16[512,384]{1,0:T(8,128)(2,1)S(1)} collective-permute-done((bf16[512,384]{1,0:T(8,128)(2,1)}, bf16[512,384]{1,0:T(8,128)(2,1)S(1)}, u32[]{:S(2)}, u32[]{:S(2)}) %collective-permute-start.6) | collective-permute-done | bytes 393248 | tf_op jit(solution)/shard_map/ppermute | solution.py:263
  87.0 5.2 %attend_3.1 = (f32[3,512,256]{2,1,0:T(8,128)S(1)}, f32[3,512,128]{2,1,0:T(8,128)S(1)}, f32[3,512,256]{2,1,0:T(8,128)S(1)}) custom-call(s32[1]{0:T(128)} %bitcast.1.frame_ref, s32[96]{0:T(128)S(1)} %copy-done, s32[96]{0:T(128)S(1)} %copy-done.1, bf16[512,384]{1,0:T(8,128)(2,1)} %q_ref.1, bf16[512,384]{1,0:T(8,128)(2,1)S(1)} %collective-permute-done.4.refs_1_, ...), custom_call_target="tpu_custom_call" | custom-call | flops 1 | bytes 1 | tf_op jit(solution)/shard_map/attend_3/pallas_call | solution.py:122
  92.2 1.9 %collective-permute-start.9 = (f32[3,512,256]{2,1,0:T(8,128)S(1)}, f32[3,512,256]{2,1,0:T(8,128)S(1)}, u32[]{:S(2)}, u32[]{:S(2)}) collective-permute-start(f32[3,512,256]{2,1,0:T(8,128)S(1)} %get-tuple-element.63), channel_id=1, source_target_pairs={{0,8},{8,0},{16,24},{24,16},{32,40},{40,32},{48,56},{56,48},{64,72... | collective-permute-start | bytes 4718600 | tf_op jit(solution)/shard_map/ppermute | solution.py:263
  96.7 8.6 %collective-permute-done.7.k_ref = bf16[512,384]{1,0:T(8,128)(2,1)S(1)} collective-permute-done((bf16[512,384]{1,0:T(8,128)(2,1)S(1)}, bf16[512,384]{1,0:T(8,128)(2,1)S(1)}, u32[]{:S(2)}, u32[]{:S(2)}) %collective-permute-start.7) | collective-permute-done | bytes 393248 | tf_op jit(solution)/shard_map/ppermute | solution.py:263
  105.3 4.2 %collective-permute-done.8.v_ref = bf16[512,384]{1,0:T(8,128)(2,1)S(1)} collective-permute-done((bf16[512,384]{1,0:T(8,128)(2,1)S(1)}, bf16[512,384]{1,0:T(8,128)(2,1)S(1)}, u32[]{:S(2)}, u32[]{:S(2)}) %collective-permute-start.8) | collective-permute-done | bytes 393248 | tf_op jit(solution)/shard_map/ppermute | solution.py:263
  109.5 3.6 %finish.1 = (bf16[256,384]{1,0:T(8,128)(2,1)S(1)}, bf16[256,384]{1,0:T(8,128)(2,1)}) custom-call(s32[1]{0:T(128)} %bitcast.1.frame_ref, s32[96]{0:T(128)S(1)} %copy-done, s32[96]{0:T(128)S(1)} %copy-done.1, bf16[512,384]{1,0:T(8,128)(2,1)} %q_ref.1, bf16[512,384]{1,0:T(8,128)(2,1)S(1)} %collective-permute-done.7.k_ref, ...), custom_call_target="tpu_custom_call" | custom-call | flops 1 | bytes 1 | tf_op jit(solution)/shard_map/finish/pallas_call | solution.py:163
  113.1 4.6 %collective-permute-start.14 = (bf16[256,384]{1,0:T(8,128)(2,1)S(1)}, bf16[256,384]{1,0:T(8,128)(2,1)S(1)}, u32[]{:S(2)}, u32[]{:S(2)}) collective-permute-start(bf16[256,384]{1,0:T(8,128)(2,1)S(1)} %get-tuple-element.65.refs_0_), channel_id=1, source_target_pairs={{0,1},{1,2},{2,3},{3,4},{4,5},{5,6},{6,7},{7,0},{8,9},{9,10},{10,1... | collective-permute-start | bytes 589832 | tf_op jit(solution)/shard_map/ppermute | solution.py:263
  119.6 5.1 %collective-permute-start.10 = (bf16[256,384]{1,0:T(8,128)(2,1)}, bf16[256,384]{1,0:T(8,128)(2,1)S(1)}, u32[]{:S(2)}, u32[]{:S(2)}) collective-permute-start(bf16[256,384]{1,0:T(8,128)(2,1)} %get-tuple-element.64.refs_1_), channel_id=1, source_target_pairs={{0,1},{1,2},{2,3},{3,4},{4,5},{5,6},{6,7},{7,0},{8,9},{9,10},{10,1... | collective-permute-start | bytes 589832 | tf_op jit(solution)/shard_map/ppermute | solution.py:263
  124.8 1.9 %collective-permute-start.15 = (bf16[256,384]{1,0:T(8,128)(2,1)S(1)}, bf16[256,384]{1,0:T(8,128)(2,1)S(1)}, u32[]{:S(2)}, u32[]{:S(2)}) collective-permute-start(bf16[256,384]{1,0:T(8,128)(2,1)S(1)} %get-tuple-element.65.refs_0_), channel_id=1, source_target_pairs={{0,7},{1,0},{2,1},{3,2},{4,3},{5,4},{6,5},{7,6},{8,15},{9,8},{10,9... | collective-permute-start | bytes 589832 | tf_op jit(solution)/shard_map/ppermute | solution.py:263
  126.7 5.1 %collective-permute-start.18 = (bf16[256,384]{1,0:T(8,128)(2,1)S(1)}, bf16[256,384]{1,0:T(8,128)(2,1)S(1)}, u32[]{:S(2)}, u32[]{:S(2)}) collective-permute-start(bf16[256,384]{1,0:T(8,128)(2,1)S(1)} %collective-permute-done.14.refs_1_), channel_id=1, source_target_pairs={{0,1},{1,2},{2,3},{3,4},{4,5},{5,6},{6,7},{7,0},{8,9},{9,10},{10,1... | collective-permute-start | bytes 589832 | tf_op jit(solution)/shard_map/ppermute | solution.py:263
  133.2 2.6 %collective-permute-start.12 = (bf16[256,384]{1,0:T(8,128)(2,1)S(1)}, bf16[256,384]{1,0:T(8,128)(2,1)S(1)}, u32[]{:S(2)}, u32[]{:S(2)}) collective-permute-start(bf16[256,384]{1,0:T(8,128)(2,1)S(1)} %collective-permute-done.10.refs_2_), channel_id=1, source_target_pairs={{0,1},{1,2},{2,3},{3,4},{4,5},{5,6},{6,7},{7,0},{8,9},{9,10},{10,1... | collective-permute-start | bytes 589832 | tf_op jit(solution)/shard_map/ppermute | solution.py:263
  135.8 3.3 %collective-permute-start.13 = (bf16[256,384]{1,0:T(8,128)(2,1)S(1)}, bf16[256,384]{1,0:T(8,128)(2,1)S(1)}, u32[]{:S(2)}, u32[]{:S(2)}) collective-permute-start(bf16[256,384]{1,0:T(8,128)(2,1)S(1)} %collective-permute-done.11.refs_4_), channel_id=1, source_target_pairs={{0,7},{1,0},{2,1},{3,2},{4,3},{5,4},{6,5},{7,6},{8,15},{9,8},{10,9... | collective-permute-start | bytes 589832 | tf_op jit(solution)/shard_map/ppermute | solution.py:263
  139.1 1.9 %collective-permute-start.19 = (bf16[256,384]{1,0:T(8,128)(2,1)S(1)}, bf16[256,384]{1,0:T(8,128)(2,1)S(1)}, u32[]{:S(2)}, u32[]{:S(2)}) collective-permute-start(bf16[256,384]{1,0:T(8,128)(2,1)S(1)} %collective-permute-done.15.refs_3_), channel_id=1, source_target_pairs={{0,7},{1,0},{2,1},{3,2},{4,3},{5,4},{6,5},{7,6},{8,15},{9,8},{10,9... | collective-permute-start | bytes 589832 | tf_op jit(solution)/shard_map/ppermute | solution.py:263
  141.0 5.1 %collective-permute-start.20 = (bf16[256,384]{1,0:T(8,128)(2,1)S(1)}, bf16[256,384]{1,0:T(8,128)(2,1)S(1)}, u32[]{:S(2)}, u32[]{:S(2)}) collective-permute-start(bf16[256,384]{1,0:T(8,128)(2,1)S(1)} %collective-permute-done.18.refs_1_), channel_id=1, source_target_pairs={{0,1},{1,2},{2,3},{3,4},{4,5},{5,6},{6,7},{7,0},{8,9},{9,10},{10,1... | collective-permute-start | bytes 589832 | tf_op jit(solution)/shard_map/ppermute | solution.py:263
  146.8 2.6 %collective-permute-start.16 = (bf16[256,384]{1,0:T(8,128)(2,1)S(1)}, bf16[256,384]{1,0:T(8,128)(2,1)S(1)}, u32[]{:S(2)}, u32[]{:S(2)}) collective-permute-start(bf16[256,384]{1,0:T(8,128)(2,1)S(1)} %collective-permute-done.12.refs_2_), channel_id=1, source_target_pairs={{0,1},{1,2},{2,3},{3,4},{4,5},{5,6},{6,7},{7,0},{8,9},{9,10},{10,1... | collective-permute-start | bytes 589832 | tf_op jit(solution)/shard_map/ppermute | solution.py:263
  149.4 3.3 %collective-permute-start.17 = (bf16[256,384]{1,0:T(8,128)(2,1)S(1)}, bf16[256,384]{1,0:T(8,128)(2,1)S(1)}, u32[]{:S(2)}, u32[]{:S(2)}) collective-permute-start(bf16[256,384]{1,0:T(8,128)(2,1)S(1)} %collective-permute-done.13.refs_4_), channel_id=1, source_target_pairs={{0,7},{1,0},{2,1},{3,2},{4,3},{5,4},{6,5},{7,6},{8,15},{9,8},{10,9... | collective-permute-start | bytes 589832 | tf_op jit(solution)/shard_map/ppermute | solution.py:263
  152.7 1.9 %collective-permute-start.21 = (bf16[256,384]{1,0:T(8,128)(2,1)S(1)}, bf16[256,384]{1,0:T(8,128)(2,1)S(1)}, u32[]{:S(2)}, u32[]{:S(2)}) collective-permute-start(bf16[256,384]{1,0:T(8,128)(2,1)S(1)} %collective-permute-done.19.refs_3_), channel_id=1, source_target_pairs={{0,7},{1,0},{2,1},{3,2},{4,3},{5,4},{6,5},{7,6},{8,15},{9,8},{10,9... | collective-permute-start | bytes 589832 | tf_op jit(solution)/shard_map/ppermute | solution.py:263
  154.6 5.1 %collective-permute-start.22 = (bf16[256,384]{1,0:T(8,128)(2,1)S(1)}, bf16[256,384]{1,0:T(8,128)(2,1)S(1)}, u32[]{:S(2)}, u32[]{:S(2)}) collective-permute-start(bf16[256,384]{1,0:T(8,128)(2,1)S(1)} %collective-permute-done.20.refs_1_), channel_id=1, source_target_pairs={{0,1},{1,2},{2,3},{3,4},{4,5},{5,6},{6,7},{7,0},{8,9},{9,10},{10,1... | collective-permute-start | bytes 589832 | tf_op jit(solution)/shard_map/ppermute | solution.py:263
  160.4 1.9 %collective-permute-start.23 = (bf16[256,384]{1,0:T(8,128)(2,1)S(1)}, bf16[256,384]{1,0:T(8,128)(2,1)S(1)}, u32[]{:S(2)}, u32[]{:S(2)}) collective-permute-start(bf16[256,384]{1,0:T(8,128)(2,1)S(1)} %collective-permute-done.17.refs_4_), channel_id=1, source_target_pairs={{0,7},{1,0},{2,1},{3,2},{4,3},{5,4},{6,5},{7,6},{8,15},{9,8},{10,9... | collective-permute-start | bytes 589832 | tf_op jit(solution)/shard_map/ppermute | solution.py:263
  163.0 6.2 %collective-permute-done.23.refs_2_ = bf16[256,384]{1,0:T(8,128)(2,1)S(1)} collective-permute-done((bf16[256,384]{1,0:T(8,128)(2,1)S(1)}, bf16[256,384]{1,0:T(8,128)(2,1)S(1)}, u32[]{:S(2)}, u32[]{:S(2)}) %collective-permute-start.23) | collective-permute-done | bytes 196640 | tf_op jit(solution)/shard_map/ppermute | solution.py:263
  (32 shorter events, 16.6 us)
Async XLA Ops:
  0.0 23.9 %collective-permute-start.2 = (bf16[512,384]{1,0:T(8,128)(2,1)}, bf16[512,384]{1,0:T(8,128)(2,1)S(1)}, u32[]{:S(2)}, u32[]{:S(2)}) collective-permute-start(bf16[512,384]{1,0:T(8,128)(2,1)} %refs_3_.1), channel_id=1, source_target_pairs={{0,16},{8,24},{16,32},{24,40},{32,48},{40,56},{48,64},{56,72},{64,... | collective-permute-start | bytes 1179656 | tf_op jit(solution)/shard_map/ppermute | solution.py:263
  7.1 41.9 %copy-start = (s32[96]{0:T(128)S(1)}, s32[96]{0:T(128)}, u32[]{:S(2)}) copy-start(s32[96]{0:T(128)} %span_ref.7) | copy-start | bytes 1156
  7.1 41.9 %copy-start.1 = (s32[96]{0:T(128)S(1)}, s32[96]{0:T(128)}, u32[]{:S(2)}) copy-start(s32[96]{0:T(128)} %counts_ref.7) | copy-start | bytes 1156
  23.9 108.0 %all-to-all-start = ((bf16[8,384,384]{2,1,0:T(8,128)(2,1)}), bf16[8,384,384]{2,1,0:T(8,128)(2,1)S(1)}, u32[]{:S(2)}, u32[]{:S(2)}) async-start(bf16[8,384,384]{2,1,0:T(8,128)(2,1)} %column_blocks.1), calls=%async_computation | async-start | bytes 4718592 | tf_op jit(solution)/shard_map/all_to_all | solution.py:273
  31.2 13.9 %collective-permute-start = (bf16[512,384]{1,0:T(8,128)(2,1)}, bf16[512,384]{1,0:T(8,128)(2,1)S(1)}, u32[]{:S(2)}, u32[]{:S(2)}) collective-permute-start(bf16[512,384]{1,0:T(8,128)(2,1)} %refs_2_.1), channel_id=1, source_target_pairs={{0,16},{8,24},{16,32},{24,40},{32,48},{40,56},{48,64},{56,72},{64,... | collective-permute-start | bytes 1179656 | tf_op jit(solution)/shard_map/ppermute | solution.py:263
  33.1 15.9 %collective-permute-start.4 = (bf16[512,384]{1,0:T(8,128)(2,1)}, bf16[512,384]{1,0:T(8,128)(2,1)S(1)}, u32[]{:S(2)}, u32[]{:S(2)}) collective-permute-start(bf16[512,384]{1,0:T(8,128)(2,1)} %q_ref.1), channel_id=1, source_target_pairs={{0,8},{8,0},{16,24},{24,16},{32,40},{40,32},{48,56},{56,48},{64,72... | collective-permute-start | bytes 1179656 | tf_op jit(solution)/shard_map/ppermute | solution.py:263
  45.1 16.1 %collective-permute-start.1 = (bf16[512,384]{1,0:T(8,128)(2,1)S(1)}, bf16[512,384]{1,0:T(8,128)(2,1)}, u32[]{:S(2)}, u32[]{:S(2)}) collective-permute-start(bf16[512,384]{1,0:T(8,128)(2,1)S(1)} %collective-permute-done.refs_4_), channel_id=1, source_target_pairs={{0,16},{8,24},{16,32},{24,40},{32,48},{40,56},{48,64},{56,72},{64,... | collective-permute-start | bytes 1179656 | tf_op jit(solution)/shard_map/ppermute | solution.py:263
  47.0 19.4 %collective-permute-start.3 = (bf16[512,384]{1,0:T(8,128)(2,1)S(1)}, bf16[512,384]{1,0:T(8,128)(2,1)}, u32[]{:S(2)}, u32[]{:S(2)}) collective-permute-start(bf16[512,384]{1,0:T(8,128)(2,1)S(1)} %collective-permute-done.2.refs_5_), channel_id=1, source_target_pairs={{0,16},{8,24},{16,32},{24,40},{32,48},{40,56},{48,64},{56,72},{64,... | collective-permute-start | bytes 1179656 | tf_op jit(solution)/shard_map/ppermute | solution.py:263
  66.5 16.3 %collective-permute-start.5 = (bf16[512,384]{1,0:T(8,128)(2,1)}, bf16[512,384]{1,0:T(8,128)(2,1)S(1)}, u32[]{:S(2)}, u32[]{:S(2)}) collective-permute-start(bf16[512,384]{1,0:T(8,128)(2,1)} %collective-permute-done.1.refs_2_), channel_id=1, source_target_pairs={{0,16},{8,24},{16,32},{24,40},{32,48},{40,56},{48,64},{56,72},{64,... | collective-permute-start | bytes 1179656 | tf_op jit(solution)/shard_map/ppermute | solution.py:263
  68.4 18.6 %collective-permute-start.6 = (bf16[512,384]{1,0:T(8,128)(2,1)}, bf16[512,384]{1,0:T(8,128)(2,1)S(1)}, u32[]{:S(2)}, u32[]{:S(2)}) collective-permute-start(bf16[512,384]{1,0:T(8,128)(2,1)} %collective-permute-done.3.refs_3_), channel_id=1, source_target_pairs={{0,16},{8,24},{16,32},{24,40},{32,48},{40,56},{48,64},{56,72},{64,... | collective-permute-start | bytes 1179656 | tf_op jit(solution)/shard_map/ppermute | solution.py:263
  92.2 17.4 %collective-permute-start.9 = (f32[3,512,256]{2,1,0:T(8,128)S(1)}, f32[3,512,256]{2,1,0:T(8,128)S(1)}, u32[]{:S(2)}, u32[]{:S(2)}) collective-permute-start(f32[3,512,256]{2,1,0:T(8,128)S(1)} %get-tuple-element.63), channel_id=1, source_target_pairs={{0,8},{8,0},{16,24},{24,16},{32,40},{40,32},{48,56},{56,48},{64,72... | collective-permute-start | bytes 4718600 | tf_op jit(solution)/shard_map/ppermute | solution.py:263
  94.1 11.2 %collective-permute-start.7 = (bf16[512,384]{1,0:T(8,128)(2,1)S(1)}, bf16[512,384]{1,0:T(8,128)(2,1)S(1)}, u32[]{:S(2)}, u32[]{:S(2)}) collective-permute-start(bf16[512,384]{1,0:T(8,128)(2,1)S(1)} %collective-permute-done.5.refs_2_), channel_id=1, source_target_pairs={{8,16},{24,32},{40,48},{56,64},{72,80},{88,96},{104,112},{120,128}... | collective-permute-start | bytes 1179656 | tf_op jit(solution)/shard_map/ppermute | solution.py:263
  95.4 14.1 %collective-permute-start.8 = (bf16[512,384]{1,0:T(8,128)(2,1)S(1)}, bf16[512,384]{1,0:T(8,128)(2,1)S(1)}, u32[]{:S(2)}, u32[]{:S(2)}) collective-permute-start(bf16[512,384]{1,0:T(8,128)(2,1)S(1)} %collective-permute-done.6.refs_3_), channel_id=1, source_target_pairs={{8,16},{24,32},{40,48},{56,64},{72,80},{88,96},{104,112},{120,128}... | collective-permute-start | bytes 1179656 | tf_op jit(solution)/shard_map/ppermute | solution.py:263
  113.1 13.6 %collective-permute-start.14 = (bf16[256,384]{1,0:T(8,128)(2,1)S(1)}, bf16[256,384]{1,0:T(8,128)(2,1)S(1)}, u32[]{:S(2)}, u32[]{:S(2)}) collective-permute-start(bf16[256,384]{1,0:T(8,128)(2,1)S(1)} %get-tuple-element.65.refs_0_), channel_id=1, source_target_pairs={{0,1},{1,2},{2,3},{3,4},{4,5},{5,6},{6,7},{7,0},{8,9},{9,10},{10,1... | collective-permute-start | bytes 589832 | tf_op jit(solution)/shard_map/ppermute | solution.py:263
  117.7 15.5 %collective-permute-start.11 = (bf16[256,384]{1,0:T(8,128)(2,1)}, bf16[256,384]{1,0:T(8,128)(2,1)S(1)}, u32[]{:S(2)}, u32[]{:S(2)}) collective-permute-start(bf16[256,384]{1,0:T(8,128)(2,1)} %get-tuple-element.64.refs_1_), channel_id=1, source_target_pairs={{0,7},{1,0},{2,1},{3,2},{4,3},{5,4},{6,5},{7,6},{8,15},{9,8},{10,9... | collective-permute-start | bytes 589832 | tf_op jit(solution)/shard_map/ppermute | solution.py:263
  119.6 13.6 %collective-permute-start.10 = (bf16[256,384]{1,0:T(8,128)(2,1)}, bf16[256,384]{1,0:T(8,128)(2,1)S(1)}, u32[]{:S(2)}, u32[]{:S(2)}) collective-permute-start(bf16[256,384]{1,0:T(8,128)(2,1)} %get-tuple-element.64.refs_1_), channel_id=1, source_target_pairs={{0,1},{1,2},{2,3},{3,4},{4,5},{5,6},{6,7},{7,0},{8,9},{9,10},{10,1... | collective-permute-start | bytes 589832 | tf_op jit(solution)/shard_map/ppermute | solution.py:263
  124.8 14.3 %collective-permute-start.15 = (bf16[256,384]{1,0:T(8,128)(2,1)S(1)}, bf16[256,384]{1,0:T(8,128)(2,1)S(1)}, u32[]{:S(2)}, u32[]{:S(2)}) collective-permute-start(bf16[256,384]{1,0:T(8,128)(2,1)S(1)} %get-tuple-element.65.refs_0_), channel_id=1, source_target_pairs={{0,7},{1,0},{2,1},{3,2},{4,3},{5,4},{6,5},{7,6},{8,15},{9,8},{10,9... | collective-permute-start | bytes 589832 | tf_op jit(solution)/shard_map/ppermute | solution.py:263
  126.7 14.3 %collective-permute-start.18 = (bf16[256,384]{1,0:T(8,128)(2,1)S(1)}, bf16[256,384]{1,0:T(8,128)(2,1)S(1)}, u32[]{:S(2)}, u32[]{:S(2)}) collective-permute-start(bf16[256,384]{1,0:T(8,128)(2,1)S(1)} %collective-permute-done.14.refs_1_), channel_id=1, source_target_pairs={{0,1},{1,2},{2,3},{3,4},{4,5},{5,6},{6,7},{7,0},{8,9},{9,10},{10,1... | collective-permute-start | bytes 589832 | tf_op jit(solution)/shard_map/ppermute | solution.py:263
  133.2 13.6 %collective-permute-start.12 = (bf16[256,384]{1,0:T(8,128)(2,1)S(1)}, bf16[256,384]{1,0:T(8,128)(2,1)S(1)}, u32[]{:S(2)}, u32[]{:S(2)}) collective-permute-start(bf16[256,384]{1,0:T(8,128)(2,1)S(1)} %collective-permute-done.10.refs_2_), channel_id=1, source_target_pairs={{0,1},{1,2},{2,3},{3,4},{4,5},{5,6},{6,7},{7,0},{8,9},{9,10},{10,1... | collective-permute-start | bytes 589832 | tf_op jit(solution)/shard_map/ppermute | solution.py:263
  135.8 11.0 %collective-permute-start.13 = (bf16[256,384]{1,0:T(8,128)(2,1)S(1)}, bf16[256,384]{1,0:T(8,128)(2,1)S(1)}, u32[]{:S(2)}, u32[]{:S(2)}) collective-permute-start(bf16[256,384]{1,0:T(8,128)(2,1)S(1)} %collective-permute-done.11.refs_4_), channel_id=1, source_target_pairs={{0,7},{1,0},{2,1},{3,2},{4,3},{5,4},{6,5},{7,6},{8,15},{9,8},{10,9... | collective-permute-start | bytes 589832 | tf_op jit(solution)/shard_map/ppermute | solution.py:263
  139.1 13.6 %collective-permute-start.19 = (bf16[256,384]{1,0:T(8,128)(2,1)S(1)}, bf16[256,384]{1,0:T(8,128)(2,1)S(1)}, u32[]{:S(2)}, u32[]{:S(2)}) collective-permute-start(bf16[256,384]{1,0:T(8,128)(2,1)S(1)} %collective-permute-done.15.refs_3_), channel_id=1, source_target_pairs={{0,7},{1,0},{2,1},{3,2},{4,3},{5,4},{6,5},{7,6},{8,15},{9,8},{10,9... | collective-permute-start | bytes 589832 | tf_op jit(solution)/shard_map/ppermute | solution.py:263
  141.0 13.6 %collective-permute-start.20 = (bf16[256,384]{1,0:T(8,128)(2,1)S(1)}, bf16[256,384]{1,0:T(8,128)(2,1)S(1)}, u32[]{:S(2)}, u32[]{:S(2)}) collective-permute-start(bf16[256,384]{1,0:T(8,128)(2,1)S(1)} %collective-permute-done.18.refs_1_), channel_id=1, source_target_pairs={{0,1},{1,2},{2,3},{3,4},{4,5},{5,6},{6,7},{7,0},{8,9},{9,10},{10,1... | collective-permute-start | bytes 589832 | tf_op jit(solution)/shard_map/ppermute | solution.py:263
  146.8 13.6 %collective-permute-start.16 = (bf16[256,384]{1,0:T(8,128)(2,1)S(1)}, bf16[256,384]{1,0:T(8,128)(2,1)S(1)}, u32[]{:S(2)}, u32[]{:S(2)}) collective-permute-start(bf16[256,384]{1,0:T(8,128)(2,1)S(1)} %collective-permute-done.12.refs_2_), channel_id=1, source_target_pairs={{0,1},{1,2},{2,3},{3,4},{4,5},{5,6},{6,7},{7,0},{8,9},{9,10},{10,1... | collective-permute-start | bytes 589832 | tf_op jit(solution)/shard_map/ppermute | solution.py:263
  149.4 11.0 %collective-permute-start.17 = (bf16[256,384]{1,0:T(8,128)(2,1)S(1)}, bf16[256,384]{1,0:T(8,128)(2,1)S(1)}, u32[]{:S(2)}, u32[]{:S(2)}) collective-permute-start(bf16[256,384]{1,0:T(8,128)(2,1)S(1)} %collective-permute-done.13.refs_4_), channel_id=1, source_target_pairs={{0,7},{1,0},{2,1},{3,2},{4,3},{5,4},{6,5},{7,6},{8,15},{9,8},{10,9... | collective-permute-start | bytes 589832 | tf_op jit(solution)/shard_map/ppermute | solution.py:263
  152.7 9.7 %collective-permute-start.21 = (bf16[256,384]{1,0:T(8,128)(2,1)S(1)}, bf16[256,384]{1,0:T(8,128)(2,1)S(1)}, u32[]{:S(2)}, u32[]{:S(2)}) collective-permute-start(bf16[256,384]{1,0:T(8,128)(2,1)S(1)} %collective-permute-done.19.refs_3_), channel_id=1, source_target_pairs={{0,7},{1,0},{2,1},{3,2},{4,3},{5,4},{6,5},{7,6},{8,15},{9,8},{10,9... | collective-permute-start | bytes 589832 | tf_op jit(solution)/shard_map/ppermute | solution.py:263
  154.6 8.4 %collective-permute-start.22 = (bf16[256,384]{1,0:T(8,128)(2,1)S(1)}, bf16[256,384]{1,0:T(8,128)(2,1)S(1)}, u32[]{:S(2)}, u32[]{:S(2)}) collective-permute-start(bf16[256,384]{1,0:T(8,128)(2,1)S(1)} %collective-permute-done.20.refs_1_), channel_id=1, source_target_pairs={{0,1},{1,2},{2,3},{3,4},{4,5},{5,6},{6,7},{7,0},{8,9},{9,10},{10,1... | collective-permute-start | bytes 589832 | tf_op jit(solution)/shard_map/ppermute | solution.py:263
  160.4 8.8 %collective-permute-start.23 = (bf16[256,384]{1,0:T(8,128)(2,1)S(1)}, bf16[256,384]{1,0:T(8,128)(2,1)S(1)}, u32[]{:S(2)}, u32[]{:S(2)}) collective-permute-start(bf16[256,384]{1,0:T(8,128)(2,1)S(1)} %collective-permute-done.17.refs_4_), channel_id=1, source_target_pairs={{0,7},{1,0},{2,1},{3,2},{4,3},{5,4},{6,5},{7,6},{8,15},{9,8},{10,9... | collective-permute-start | bytes 589832 | tf_op jit(solution)/shard_map/ppermute | solution.py:263

commit v3 on v2

--- a/solution.py
+++ b/solution.py
@@ -13,6 +13,7 @@
 SMALL_VMEM = 16 << 20
 LARGE_VMEM = 24 << 20
 BRIEF = pl.CostEstimate(flops=1, transcendentals=0, bytes_accessed=1)
+LONG = pl.CostEstimate(flops=1 << 34, transcendentals=0, bytes_accessed=1)
 
 
 def _attend(limit, q_ref, k_ref, v_ref, acc_ref, top_ref):
@@ -53,137 +54,107 @@
     return pltpu.with_memory_space_constraint(array, pltpu.HBM)
 
 
-def _start(acc, top):
-    acc[...] = jnp.zeros_like(acc)
-    top[...] = jnp.full_like(top, NEG)
-
-
-def _attention_body(hops, first, hand_over):
+def _unpack(packed, acc, top):
+    acc[0, :, :HD] = packed[0, :, :HD]
+    acc[0, :, HD:] = jnp.broadcast_to(packed[0, :, 2 * HD - 1 :], (acc.shape[1], HD))
+    top[0] = jnp.broadcast_to(packed[0, :, HD : HD + 1], (acc.shape[1], HD))
+
+
+def _attention_body(sides, hops, first):
     def body(frame_ref, span_ref, counts_ref, *refs):
         refs = list(refs)
-        q_refs = [refs.pop(0), refs.pop(0)]
-        kv_refs = [(refs.pop(0), refs.pop(0)) for _ in hops]
-        if first:
-            state_in = None
-        else:
-            state_in = [refs.pop(0) for _ in range(4)]
-        if hand_over:
-            own_acc, own_top, packed, other_acc, other_top = refs
-        else:
-            own_acc, own_top, other_acc, other_top = refs
-        state = (own_acc, own_top, other_acc, other_top)
-        if first:
-            _start(own_acc, own_top)
-            _start(other_acc, other_top)
-        else:
-            for ref, ref_in in zip(state, state_in):
-                ref[...] = ref_in[...]
+        take = lambda n: [refs.pop(0) for _ in range(n)]
+        q_refs = take(len(sides))
+        kv_refs = [take(2) for _ in hops]
+        state_refs = [None] * len(sides) if first else take(len(sides))
+        out_refs = take(len(sides))
+        scratch = [take(2) for _ in sides]
         frame = frame_ref[0]
+        for state, (acc, top) in zip(state_refs, scratch):
+            if first:
+                acc[...] = jnp.zeros_like(acc)
+                top[...] = jnp.full_like(top, NEG)
+            else:
+                _unpack(state, acc, top)
         for hop, (k_ref, v_ref) in zip(hops, kv_refs):
-            for side in (0, 1):
+            for side, q_ref, (acc, top) in zip(sides, q_refs, scratch):
                 limit = _visible(frame, side, 2 * hop, span_ref, counts_ref)
-                _attend(limit, q_refs[side], k_ref, v_ref, state[2 * side], state[2 * side + 1])
-        if hand_over:
-            lane = lax.broadcasted_iota(jnp.int32, (1, HD), 1)
-            packed[0, :, :HD] = other_acc[0, :, :HD]
-            packed[0, :, HD:] = jnp.where(lane < HD // 2, other_top[0], other_acc[0, :, HD:])
+                _attend(limit, q_ref, k_ref, v_ref, acc, top)
+        lane = lax.broadcasted_iota(jnp.int32, (1, HD), 1)
+        for out, (acc, top) in zip(out_refs, scratch):
+            out[0, :, :HD] = acc[0, :, :HD]
+            out[0, :, HD:] = jnp.where(lane < HD // 2, top[0], acc[0, :, HD:])
 
     return body
 
 
-def attention_call(scalars, q_own, q_other, sources, hops, state, hand_over, name):
-    per_frame, width = q_own.shape
+def _specs(per_frame):
+    column = pl.BlockSpec((per_frame, HD), lambda h, *_: (0, h))
+    packed = pl.BlockSpec((1, per_frame, 2 * HD), lambda h, *_: (h, 0, 0))
+    scratch = [pltpu.VMEM((1, per_frame, 2 * HD), jnp.float32), pltpu.VMEM((1, per_frame, HD), jnp.float32)]
+    return column, packed, scratch
+
+
+def attention_call(scalars, queries, sources, sides, hops, states, name, cost):
+    per_frame, width = queries[0].shape
     heads = width // HD
-    first = state is None
-    column = pl.BlockSpec((per_frame, HD), lambda h, *_: (0, h))
-    acc_spec = pl.BlockSpec((1, per_frame, 2 * HD), lambda h, *_: (h, 0, 0))
-    top_spec = pl.BlockSpec((1, per_frame, HD), lambda h, *_: (h, 0, 0))
-    in_specs = [column, column]
-    operands = [q_own, q_other]
-    for keys_and_values in sources:
-        in_specs += [column, column]
-        operands += keys_and_values
-    if not first:
-        in_specs += [acc_spec, top_spec] * 2
-        operands += [in_hbm(x) for x in state]
-    acc_shape = jax.ShapeDtypeStruct((heads, per_frame, 2 * HD), jnp.float32)
-    top_shape = jax.ShapeDtypeStruct((heads, per_frame, HD), jnp.float32)
-    scratch = []
-    if hand_over:
-        out_specs = [acc_spec, top_spec, acc_spec]
-        out_shape = [acc_shape, top_shape, acc_shape]
-        scratch = [
-            pltpu.VMEM((1, per_frame, 2 * HD), jnp.float32),
-            pltpu.VMEM((1, per_frame, HD), jnp.float32),
-        ]
-    else:
-        out_specs = [acc_spec, top_spec] * 2
-        out_shape = [pltpu.HBM(s.shape, s.dtype) for s in [acc_shape, top_shape] * 2]
-    return pl.pallas_call(
-        _attention_body(hops, first, hand_over),
-        out_shape=out_shape,
+    column, packed, scratch = _specs(per_frame)
+    operands = list(queries) + [array for pair in sources for array in pair] + list(states or ())
+    return pl.pallas_call(
+        _attention_body(sides, hops, states is None),
+        out_shape=[jax.ShapeDtypeStruct((heads, per_frame, 2 * HD), jnp.float32)] * len(sides),
         grid_spec=pltpu.PrefetchScalarGridSpec(
             num_scalar_prefetch=3,
             grid=(heads,),
-            in_specs=in_specs,
-            out_specs=out_specs,
-            scratch_shapes=scratch,
-        ),
-        cost_estimate=BRIEF,
+            in_specs=[column] * (len(sides) + 2 * len(hops)) + [packed] * len(states or ()),
+            out_specs=[packed] * len(sides),
+            scratch_shapes=scratch * len(sides),
+        ),
+        cost_estimate=cost,
         compiler_params=pltpu.CompilerParams(vmem_limit_bytes=SMALL_VMEM),
         name=name,
     )(*scalars, *operands)
 
 
-def _finish_body(frame_ref, span_ref, counts_ref, q_ref, k_ref, v_ref, acc_in, top_in, packed, upper_ref, lower_ref, acc, top):
-    acc[...] = acc_in[...]
-    top[...] = top_in[...]
+def _finish_body(frame_ref, span_ref, counts_ref, q_ref, k_ref, v_ref, own, other, upper_ref, lower_ref, acc, top):
+    _unpack(own, acc, top)
     limit = _visible(frame_ref[0], 0, WIN - 1, span_ref, counts_ref)
     limit = jnp.where(frame_ref[0] % 2 == 0, limit, 0)
     _attend(limit, q_ref, k_ref, v_ref, acc, top)
-    own_top, other_top = top[0], packed[0, :, HD : HD + 1]
-    own_total, other_total = acc[0, :, HD:], packed[0, :, 2 * HD - 1 :]
+    own_top, other_top = top[0], other[0, :, HD : HD + 1]
+    own_total, other_total = acc[0, :, HD:], other[0, :, 2 * HD - 1 :]
     both_top = jnp.maximum(own_top, other_top)
     own_part = jnp.exp2((own_top - both_top) * EXP2_SCALE)
     other_part = jnp.exp2((other_top - both_top) * EXP2_SCALE)
     total = own_total * own_part + other_total * other_part
-    mixed = acc[0, :, :HD] * own_part + packed[0, :, :HD] * other_part
+    mixed = acc[0, :, :HD] * own_part + other[0, :, :HD] * other_part
     mixed = (mixed / total).astype(jnp.bfloat16)
     half = upper_ref.shape[0]
     upper_ref[...] = mixed[:half]
     lower_ref[...] = mixed[half:]
 
 
-def finish_call(scalars, q_own, keys, values, state, packed, name):
-    per_frame, width = q_own.shape
-    heads = width // HD
-    column = pl.BlockSpec((per_frame, HD), lambda h, *_: (0, h))
-    acc_spec = pl.BlockSpec((1, per_frame, 2 * HD), lambda h, *_: (h, 0, 0))
-    top_spec = pl.BlockSpec((1, per_frame, HD), lambda h, *_: (h, 0, 0))
+def finish_call(scalars, queries, keys, values, own, other, name):
+    per_frame, width = queries.shape
+    column, packed, scratch = _specs(per_frame)
     return pl.pallas_call(
         _finish_body,
         out_shape=[jax.ShapeDtypeStruct((per_frame // 2, width), jnp.bfloat16)] * 2,
         grid_spec=pltpu.PrefetchScalarGridSpec(
             num_scalar_prefetch=3,
-            grid=(heads,),
-            in_specs=[
-                column,
-                column,
-                column,
-                acc_spec,
-                top_spec,
-                acc_spec,
-            ],
+            grid=(width // HD,),
+            in_specs=[column, column, column, packed, packed],
             out_specs=[pl.BlockSpec((per_frame // 2, HD), lambda h, *_: (0, h))] * 2,
-            scratch_shapes=[
-                pltpu.VMEM((1, per_frame, 2 * HD), jnp.float32),
-                pltpu.VMEM((1, per_frame, HD), jnp.float32),
-            ],
+            scratch_shapes=scratch,
         ),
         cost_estimate=BRIEF,
         compiler_params=pltpu.CompilerParams(vmem_limit_bytes=SMALL_VMEM),
         name=name,
-    )(*scalars, q_own, keys, values, *state, packed)
+    )(*scalars, queries, keys, values, own, other)
+
+
+def in_hbm(array):
+    return pltpu.with_memory_space_constraint(array, pltpu.HBM)
 
 
 def _column_blocks_body(w_ref, out_ref):
@@ -262,24 +233,27 @@
     def send(block, route, axis="frame"):
         return lax.ppermute(block, axis, route)
 
-    def attend(sources, hops, state, hand_over, name):
+    def attend(sources, sides, hops, states, name, cost=BRIEF):
+        both = (in_hbm(queries), q_other)
         return attention_call(
-            scalars, in_hbm(queries), q_other, sources, hops, state, hand_over, name
+            scalars, [both[side] for side in sides], sources, sides, hops, states, name, cost
         )
 
     k1, v1 = send(keys, by_chip), send(values, by_chip)
     q_other = send(queries, swap)
-    blocks, v1 = after((column_blocks(out_weight, groups), v1))
+    k2, v2 = send(k1, by_chip), send(v1, by_chip)
+    near = [(in_hbm(keys), in_hbm(values)), (k1, v1)]
+    own, other = attend(near, (0, 1), (0, 1), None, "attend_01", LONG)
+    blocks = column_blocks(out_weight, groups)
     weight = lax.all_to_all(blocks, "head", split_axis=0, concat_axis=0, tiled=True)
-    k2, v2 = send(k1, by_chip), send(v1, by_chip)
-    state = attend([(in_hbm(keys), in_hbm(values)), (k1, v1)], (0, 1), None, False, "attend_01")
-    k2, v2, state = after((k2, v2, state))
     k3, v3 = send(k2, by_chip), send(v2, by_chip)
-    state = attend([(k2, v2)], (2,), state, False, "attend_2")
-    k3, v3, state = after((k3, v3, state))
+    own, other = attend([(k2, v2)], (0, 1), (2,), [own, other], "attend_2", LONG)
+    k3, v3, own, other = after((k3, v3, own, other))
+    (other,) = attend([(k3, v3)], (1,), (3,), [other], "attend_3_other")
+    from_other = send(other, swap)
     k4, v4 = send(k3, to_even), send(v3, to_even)
-    *own, packed = attend([(k3, v3)], (3,), state, True, "attend_3")
-    attended = finish_call(scalars, in_hbm(queries), k4, v4, own, send(packed, swap), "finish")
+    (own,) = attend([(k3, v3)], (0,), (3,), [own], "attend_3_own", LONG)
+    attended = finish_call(scalars, in_hbm(queries), k4, v4, own, from_other, "finish")
 
     def project(base, pieces, places, dtype, name):
         return project_call(group, weight, base, pieces, places, dtype, name)

time: 171 us -> 143 us (0.84)
  the two profiles are of different devices: /device:TPU:26 before, /device:TPU:30 now
where the time goes in v3:
time: 143 us; the launch traced here: 142 us
  starting transfers between devices  77.1 us (54%)
  waiting for transfers between devices  38.8 us (27%)
  Pallas kernels  25.5 us (18%)
    ppermute x24, starting transfers between devices, send(): return lax.ppermute(block, axis, route)  69.6 us
    ppermute x24, waiting for transfers between devices, send(): return lax.ppermute(block, axis, route)  38.8 us
    pallas_call x4, Pallas kernels, attention_call(): pl.pallas_call(_attention_body(sides, hops, states is None), out_shape=[j...  14.4 us
    all_to_all x1, starting transfers between devices, on_device(): lax.all_to_all(blocks, 'head', split_axis=0, concat_axis=0, tiled=True)  7.45 us
    pallas_call x5, Pallas kernels, project_call(): pl.pallas_call(_project_body(places, base is not None), out_shape=jax.Sha...  4.38 us
    pallas_call x1, Pallas kernels, finish_call(): pl.pallas_call(_finish_body, out_shape=[jax.ShapeDtypeStruct((per_frame /...  3.9 us
  transfers between devices with their start and end apart: 25, of which 8 were waited for; matrix products, arithmetic and copies ran while one was open for 0% of the time, Pallas kernels for 17%

profile of v3, /device:TPU:30, one launch (start us, length us, event | category | flops | bytes accessed | tf_op | source)
XLA Modules:
  0.0 141.7 jit_solution(14556609652164943004)
XLA Ops:
  0.0 4.3 %collective-permute-start = (bf16[512,384]{1,0:T(8,128)(2,1)}, bf16[512,384]{1,0:T(8,128)(2,1)S(1)}, u32[]{:S(2)}, u32[]{:S(2)}) collective-permute-start(bf16[512,384]{1,0:T(8,128)(2,1)} %refs_2_.1), channel_id=1, source_target_pairs={{0,16},{8,24},{16,32},{24,40},{32,48},{40,56},{48,64},{56,72},{64,... | collective-permute-start | bytes 1179656 | tf_op jit(solution)/shard_map/ppermute | solution.py:234
  4.3 4.3 %collective-permute-start.3 = (bf16[512,384]{1,0:T(8,128)(2,1)}, bf16[512,384]{1,0:T(8,128)(2,1)S(1)}, u32[]{:S(2)}, u32[]{:S(2)}) collective-permute-start(bf16[512,384]{1,0:T(8,128)(2,1)} %refs_3_.1), channel_id=1, source_target_pairs={{0,16},{8,24},{16,32},{24,40},{32,48},{40,56},{48,64},{56,72},{64,... | collective-permute-start | bytes 1179656 | tf_op jit(solution)/shard_map/ppermute | solution.py:234
  8.6 1.9 %collective-permute-start.6 = (bf16[512,384]{1,0:T(8,128)(2,1)}, bf16[512,384]{1,0:T(8,128)(2,1)S(1)}, u32[]{:S(2)}, u32[]{:S(2)}) collective-permute-start(bf16[512,384]{1,0:T(8,128)(2,1)} %q_ref.1), channel_id=1, source_target_pairs={{0,8},{8,0},{16,24},{24,16},{32,40},{40,32},{48,56},{56,48},{64,72... | collective-permute-start | bytes 1179656 | tf_op jit(solution)/shard_map/ppermute | solution.py:234
  10.5 2.8 %column_blocks.1 = bf16[8,384,384]{2,1,0:T(8,128)(2,1)} custom-call(bf16[384,3072]{1,0:T(8,128)(2,1)} %w_ref.1), custom_call_target="tpu_custom_call" | custom-call | flops 1 | bytes 1 | tf_op jit(solution)/shard_map/column_blocks/pallas_call | solution.py:169
  13.3 7.5 %all-to-all-start = ((bf16[8,384,384]{2,1,0:T(8,128)(2,1)}), bf16[8,384,384]{2,1,0:T(8,128)(2,1)S(1)}, u32[]{:S(2)}, u32[]{:S(2)}) async-start(bf16[8,384,384]{2,1,0:T(8,128)(2,1)} %column_blocks.1), calls=%async_computation | async-start | bytes 4718592 | tf_op jit(solution)/shard_map/all_to_all | solution.py:248
  20.8 4.2 %collective-permute-done.refs_4_ = bf16[512,384]{1,0:T(8,128)(2,1)S(1)} collective-permute-done((bf16[512,384]{1,0:T(8,128)(2,1)}, bf16[512,384]{1,0:T(8,128)(2,1)S(1)}, u32[]{:S(2)}, u32[]{:S(2)}) %collective-permute-start) | collective-permute-done | bytes 393248 | tf_op jit(solution)/shard_map/ppermute | solution.py:234
  26.9 6.5 %collective-permute-done.3.refs_5_ = bf16[512,384]{1,0:T(8,128)(2,1)S(1)} collective-permute-done((bf16[512,384]{1,0:T(8,128)(2,1)}, bf16[512,384]{1,0:T(8,128)(2,1)S(1)}, u32[]{:S(2)}, u32[]{:S(2)}) %collective-permute-start.3) | collective-permute-done | bytes 393248 | tf_op jit(solution)/shard_map/ppermute | solution.py:234
  35.4 6.6 %attend_01.1 = (f32[3,512,256]{2,1,0:T(8,128)S(1)}, f32[3,512,256]{2,1,0:T(8,128)S(1)}) custom-call(s32[1]{0:T(128)} %bitcast.1.frame_ref, s32[96]{0:T(128)S(1)} %copy-done, s32[96]{0:T(128)S(1)} %copy-done.1, bf16[512,384]{1,0:T(8,128)(2,1)} %q_ref.1, bf16[512,384]{1,0:T(8,128)(2,1)S(1)} %collective-permute-done.6.refs_1_.refs_0_, ...), custom_call_target="tpu_custom_call" | custom-call | flops 17179869184 | bytes 1 | tf_op jit(solution)/shard_map/attend_01/pallas_call | solution.py:103
  41.9 3.6 %collective-permute-start.2 = (bf16[512,384]{1,0:T(8,128)(2,1)S(1)}, bf16[512,384]{1,0:T(8,128)(2,1)S(1)}, u32[]{:S(2)}, u32[]{:S(2)}) collective-permute-start(bf16[512,384]{1,0:T(8,128)(2,1)S(1)} %collective-permute-done.1.refs_2_), channel_id=1, source_target_pairs={{0,16},{8,24},{16,32},{24,40},{32,48},{40,56},{48,64},{56,72},{64,... | collective-permute-start | bytes 1179656 | tf_op jit(solution)/shard_map/ppermute | solution.py:234
  45.6 4.2 %collective-permute-done.4.refs_3_ = bf16[512,384]{1,0:T(8,128)(2,1)S(1)} collective-permute-done((bf16[512,384]{1,0:T(8,128)(2,1)S(1)}, bf16[512,384]{1,0:T(8,128)(2,1)S(1)}, u32[]{:S(2)}, u32[]{:S(2)}) %collective-permute-start.4) | collective-permute-done | bytes 393248 | tf_op jit(solution)/shard_map/ppermute | solution.py:234
  51.7 3.3 %attend_2.1 = (f32[3,512,256]{2,1,0:T(8,128)S(1)}, f32[3,512,256]{2,1,0:T(8,128)S(1)}) custom-call(s32[1]{0:T(128)} %bitcast.1.frame_ref, s32[96]{0:T(128)S(1)} %copy-done, s32[96]{0:T(128)S(1)} %copy-done.1, bf16[512,384]{1,0:T(8,128)(2,1)} %q_ref.1, bf16[512,384]{1,0:T(8,128)(2,1)S(1)} %collective-permute-done.6.refs_1_.refs_0_, ...), custom_call_target="tpu_custom_call" | custom-call | flops 17179869184 | bytes 1 | tf_op jit(solution)/shard_map/attend_2/pallas_call | solution.py:103
  55.0 5.1 %collective-permute-done.2.refs_1_ = bf16[512,384]{1,0:T(8,128)(2,1)S(1)} collective-permute-done((bf16[512,384]{1,0:T(8,128)(2,1)S(1)}, bf16[512,384]{1,0:T(8,128)(2,1)S(1)}, u32[]{:S(2)}, u32[]{:S(2)}) %collective-permute-start.2) | collective-permute-done | bytes 393248 | tf_op jit(solution)/shard_map/ppermute | solution.py:234
  60.1 6.2 %collective-permute-done.5.refs_2_ = bf16[512,384]{1,0:T(8,128)(2,1)S(1)} collective-permute-done((bf16[512,384]{1,0:T(8,128)(2,1)S(1)}, bf16[512,384]{1,0:T(8,128)(2,1)S(1)}, u32[]{:S(2)}, u32[]{:S(2)}) %collective-permute-start.5) | collective-permute-done | bytes 393248 | tf_op jit(solution)/shard_map/ppermute | solution.py:234
  70.5 1.9 %collective-permute-start.9 = (f32[3,512,256]{2,1,0:T(8,128)S(1)}, f32[3,512,256]{2,1,0:T(8,128)S(1)}, u32[]{:S(2)}, u32[]{:S(2)}) collective-permute-start(f32[3,512,256]{2,1,0:T(8,128)S(1)} %attend_3_other.1), channel_id=1, source_target_pairs={{0,8},{8,0},{16,24},{24,16},{32,40},{40,32},{48,56},{56,48},{64,72... | collective-permute-start | bytes 4718600 | tf_op jit(solution)/shard_map/ppermute | solution.py:234
  72.4 2.9 %attend_3_own.1.own = f32[3,512,256]{2,1,0:T(8,128)S(1)} custom-call(s32[1]{0:T(128)} %bitcast.1.frame_ref, s32[96]{0:T(128)S(1)} %copy-done, s32[96]{0:T(128)S(1)} %copy-done.1, bf16[512,384]{1,0:T(8,128)(2,1)} %q_ref.1, bf16[512,384]{1,0:T(8,128)(2,1)S(1)} %collective-permute-done.2.refs_1_, bf16[512,384]{1,0:T(8,128)(2,1)S(1)} %collective-permute-done.5.refs_2_, ...), custom_call_target="tpu_custom_call" | custom-call | flops 17179869184 | bytes 1 | tf_op jit(solution)/shard_map/attend_3_own/pallas_call | solution.py:103
  75.3 2.2 %collective-permute-done.7.k_ref = bf16[512,384]{1,0:T(8,128)(2,1)S(1)} collective-permute-done((bf16[512,384]{1,0:T(8,128)(2,1)S(1)}, bf16[512,384]{1,0:T(8,128)(2,1)S(1)}, u32[]{:S(2)}, u32[]{:S(2)}) %collective-permute-start.7) | collective-permute-done | bytes 393248 | tf_op jit(solution)/shard_map/ppermute | solution.py:234
  77.5 4.2 %collective-permute-done.8.v_ref = bf16[512,384]{1,0:T(8,128)(2,1)S(1)} collective-permute-done((bf16[512,384]{1,0:T(8,128)(2,1)S(1)}, bf16[512,384]{1,0:T(8,128)(2,1)S(1)}, u32[]{:S(2)}, u32[]{:S(2)}) %collective-permute-start.8) | collective-permute-done | bytes 393248 | tf_op jit(solution)/shard_map/ppermute | solution.py:234
  81.7 3.9 %finish.1 = (bf16[256,384]{1,0:T(8,128)(2,1)S(1)}, bf16[256,384]{1,0:T(8,128)(2,1)}) custom-call(s32[1]{0:T(128)} %bitcast.1.frame_ref, s32[96]{0:T(128)S(1)} %copy-done, s32[96]{0:T(128)S(1)} %copy-done.1, bf16[512,384]{1,0:T(8,128)(2,1)} %q_ref.1, bf16[512,384]{1,0:T(8,128)(2,1)S(1)} %collective-permute-done.7.k_ref, ...), custom_call_target="tpu_custom_call" | custom-call | flops 1 | bytes 1 | tf_op jit(solution)/shard_map/finish/pallas_call | solution.py:140
  85.6 4.7 %collective-permute-start.14 = (bf16[256,384]{1,0:T(8,128)(2,1)S(1)}, bf16[256,384]{1,0:T(8,128)(2,1)S(1)}, u32[]{:S(2)}, u32[]{:S(2)}) collective-permute-start(bf16[256,384]{1,0:T(8,128)(2,1)S(1)} %get-tuple-element.32.refs_0_), channel_id=1, source_target_pairs={{0,1},{1,2},{2,3},{3,4},{4,5},{5,6},{6,7},{7,0},{8,9},{9,10},{10,1... | collective-permute-start | bytes 589832 | tf_op jit(solution)/shard_map/ppermute | solution.py:234
  90.3 2.6 %collective-permute-start.10 = (bf16[256,384]{1,0:T(8,128)(2,1)}, bf16[256,384]{1,0:T(8,128)(2,1)S(1)}, u32[]{:S(2)}, u32[]{:S(2)}) collective-permute-start(bf16[256,384]{1,0:T(8,128)(2,1)} %get-tuple-element.31.refs_1_), channel_id=1, source_target_pairs={{0,1},{1,2},{2,3},{3,4},{4,5},{5,6},{6,7},{7,0},{8,9},{9,10},{10,1... | collective-permute-start | bytes 589832 | tf_op jit(solution)/shard_map/ppermute | solution.py:234
  92.9 3.3 %collective-permute-start.11 = (bf16[256,384]{1,0:T(8,128)(2,1)}, bf16[256,384]{1,0:T(8,128)(2,1)S(1)}, u32[]{:S(2)}, u32[]{:S(2)}) collective-permute-start(bf16[256,384]{1,0:T(8,128)(2,1)} %get-tuple-element.31.refs_1_), channel_id=1, source_target_pairs={{0,7},{1,0},{2,1},{3,2},{4,3},{5,4},{6,5},{7,6},{8,15},{9,8},{10,9... | collective-permute-start | bytes 589832 | tf_op jit(solution)/shard_map/ppermute | solution.py:234
  96.1 1.9 %collective-permute-start.15 = (bf16[256,384]{1,0:T(8,128)(2,1)S(1)}, bf16[256,384]{1,0:T(8,128)(2,1)S(1)}, u32[]{:S(2)}, u32[]{:S(2)}) collective-permute-start(bf16[256,384]{1,0:T(8,128)(2,1)S(1)} %get-tuple-element.32.refs_0_), channel_id=1, source_target_pairs={{0,7},{1,0},{2,1},{3,2},{4,3},{5,4},{6,5},{7,6},{8,15},{9,8},{10,9... | collective-permute-start | bytes 589832 | tf_op jit(solution)/shard_map/ppermute | solution.py:234
  98.1 5.1 %collective-permute-start.18 = (bf16[256,384]{1,0:T(8,128)(2,1)S(1)}, bf16[256,384]{1,0:T(8,128)(2,1)S(1)}, u32[]{:S(2)}, u32[]{:S(2)}) collective-permute-start(bf16[256,384]{1,0:T(8,128)(2,1)S(1)} %collective-permute-done.14.refs_1_), channel_id=1, source_target_pairs={{0,1},{1,2},{2,3},{3,4},{4,5},{5,6},{6,7},{7,0},{8,9},{9,10},{10,1... | collective-permute-start | bytes 589832 | tf_op jit(solution)/shard_map/ppermute | solution.py:234
  104.6 2.6 %collective-permute-start.12 = (bf16[256,384]{1,0:T(8,128)(2,1)S(1)}, bf16[256,384]{1,0:T(8,128)(2,1)S(1)}, u32[]{:S(2)}, u32[]{:S(2)}) collective-permute-start(bf16[256,384]{1,0:T(8,128)(2,1)S(1)} %collective-permute-done.10.refs_2_), channel_id=1, source_target_pairs={{0,1},{1,2},{2,3},{3,4},{4,5},{5,6},{6,7},{7,0},{8,9},{9,10},{10,1... | collective-permute-start | bytes 589832 | tf_op jit(solution)/shard_map/ppermute | solution.py:234
  107.2 3.3 %collective-permute-start.13 = (bf16[256,384]{1,0:T(8,128)(2,1)S(1)}, bf16[256,384]{1,0:T(8,128)(2,1)S(1)}, u32[]{:S(2)}, u32[]{:S(2)}) collective-permute-start(bf16[256,384]{1,0:T(8,128)(2,1)S(1)} %collective-permute-done.11.refs_4_), channel_id=1, source_target_pairs={{0,7},{1,0},{2,1},{3,2},{4,3},{5,4},{6,5},{7,6},{8,15},{9,8},{10,9... | collective-permute-start | bytes 589832 | tf_op jit(solution)/shard_map/ppermute | solution.py:234
  110.5 1.9 %collective-permute-start.19 = (bf16[256,384]{1,0:T(8,128)(2,1)S(1)}, bf16[256,384]{1,0:T(8,128)(2,1)S(1)}, u32[]{:S(2)}, u32[]{:S(2)}) collective-permute-start(bf16[256,384]{1,0:T(8,128)(2,1)S(1)} %collective-permute-done.15.refs_3_), channel_id=1, source_target_pairs={{0,7},{1,0},{2,1},{3,2},{4,3},{5,4},{6,5},{7,6},{8,15},{9,8},{10,9... | collective-permute-start | bytes 589832 | tf_op jit(solution)/shard_map/ppermute | solution.py:234
  112.4 5.1 %collective-permute-start.20 = (bf16[256,384]{1,0:T(8,128)(2,1)S(1)}, bf16[256,384]{1,0:T(8,128)(2,1)S(1)}, u32[]{:S(2)}, u32[]{:S(2)}) collective-permute-start(bf16[256,384]{1,0:T(8,128)(2,1)S(1)} %collective-permute-done.18.refs_1_), channel_id=1, source_target_pairs={{0,1},{1,2},{2,3},{3,4},{4,5},{5,6},{6,7},{7,0},{8,9},{9,10},{10,1... | collective-permute-start | bytes 589832 | tf_op jit(solution)/shard_map/ppermute | solution.py:234
  118.2 2.6 %collective-permute-start.16 = (bf16[256,384]{1,0:T(8,128)(2,1)S(1)}, bf16[256,384]{1,0:T(8,128)(2,1)S(1)}, u32[]{:S(2)}, u32[]{:S(2)}) collective-permute-start(bf16[256,384]{1,0:T(8,128)(2,1)S(1)} %collective-permute-done.12.refs_2_), channel_id=1, source_target_pairs={{0,1},{1,2},{2,3},{3,4},{4,5},{5,6},{6,7},{7,0},{8,9},{9,10},{10,1... | collective-permute-start | bytes 589832 | tf_op jit(solution)/shard_map/ppermute | solution.py:234
  120.8 3.3 %collective-permute-start.17 = (bf16[256,384]{1,0:T(8,128)(2,1)S(1)}, bf16[256,384]{1,0:T(8,128)(2,1)S(1)}, u32[]{:S(2)}, u32[]{:S(2)}) collective-permute-start(bf16[256,384]{1,0:T(8,128)(2,1)S(1)} %collective-permute-done.13.refs_4_), channel_id=1, source_target_pairs={{0,7},{1,0},{2,1},{3,2},{4,3},{5,4},{6,5},{7,6},{8,15},{9,8},{10,9... | collective-permute-start | bytes 589832 | tf_op jit(solution)/shard_map/ppermute | solution.py:234
  124.1 1.9 %collective-permute-start.21 = (bf16[256,384]{1,0:T(8,128)(2,1)S(1)}, bf16[256,384]{1,0:T(8,128)(2,1)S(1)}, u32[]{:S(2)}, u32[]{:S(2)}) collective-permute-start(bf16[256,384]{1,0:T(8,128)(2,1)S(1)} %collective-permute-done.19.refs_3_), channel_id=1, source_target_pairs={{0,7},{1,0},{2,1},{3,2},{4,3},{5,4},{6,5},{7,6},{8,15},{9,8},{10,9... | collective-permute-start | bytes 589832 | tf_op jit(solution)/shard_map/ppermute | solution.py:234
  126.0 5.1 %collective-permute-start.22 = (bf16[256,384]{1,0:T(8,128)(2,1)S(1)}, bf16[256,384]{1,0:T(8,128)(2,1)S(1)}, u32[]{:S(2)}, u32[]{:S(2)}) collective-permute-start(bf16[256,384]{1,0:T(8,128)(2,1)S(1)} %collective-permute-done.20.refs_1_), channel_id=1, source_target_pairs={{0,1},{1,2},{2,3},{3,4},{4,5},{5,6},{6,7},{7,0},{8,9},{9,10},{10,1... | collective-permute-start | bytes 589832 | tf_op jit(solution)/shard_map/ppermute | solution.py:234
  134.4 6.2 %collective-permute-done.23.refs_2_ = bf16[256,384]{1,0:T(8,128)(2,1)S(1)} collective-permute-done((bf16[256,384]{1,0:T(8,128)(2,1)S(1)}, bf16[256,384]{1,0:T(8,128)(2,1)S(1)}, u32[]{:S(2)}, u32[]{:S(2)}) %collective-permute-start.23) | collective-permute-done | bytes 196640 | tf_op jit(solution)/shard_map/ppermute | solution.py:234
  (33 shorter events, 16.2 us)
Async XLA Ops:
  0.0 25.0 %collective-permute-start = (bf16[512,384]{1,0:T(8,128)(2,1)}, bf16[512,384]{1,0:T(8,128)(2,1)S(1)}, u32[]{:S(2)}, u32[]{:S(2)}) collective-permute-start(bf16[512,384]{1,0:T(8,128)(2,1)} %refs_2_.1), channel_id=1, source_target_pairs={{0,16},{8,24},{16,32},{24,40},{32,48},{40,56},{48,64},{56,72},{64,... | collective-permute-start | bytes 1179656 | tf_op jit(solution)/shard_map/ppermute | solution.py:234
  4.3 29.1 %collective-permute-start.3 = (bf16[512,384]{1,0:T(8,128)(2,1)}, bf16[512,384]{1,0:T(8,128)(2,1)S(1)}, u32[]{:S(2)}, u32[]{:S(2)}) collective-permute-start(bf16[512,384]{1,0:T(8,128)(2,1)} %refs_3_.1), channel_id=1, source_target_pairs={{0,16},{8,24},{16,32},{24,40},{32,48},{40,56},{48,64},{56,72},{64,... | collective-permute-start | bytes 1179656 | tf_op jit(solution)/shard_map/ppermute | solution.py:234
  8.6 26.8 %collective-permute-start.6 = (bf16[512,384]{1,0:T(8,128)(2,1)}, bf16[512,384]{1,0:T(8,128)(2,1)S(1)}, u32[]{:S(2)}, u32[]{:S(2)}) collective-permute-start(bf16[512,384]{1,0:T(8,128)(2,1)} %q_ref.1), channel_id=1, source_target_pairs={{0,8},{8,0},{16,24},{24,16},{32,40},{40,32},{48,56},{56,48},{64,72... | collective-permute-start | bytes 1179656 | tf_op jit(solution)/shard_map/ppermute | solution.py:234
  13.3 22.0 %copy-start = (s32[96]{0:T(128)S(1)}, s32[96]{0:T(128)}, u32[]{:S(2)}) copy-start(s32[96]{0:T(128)} %span_ref.9) | copy-start | bytes 1156
  13.3 22.0 %copy-start.1 = (s32[96]{0:T(128)S(1)}, s32[96]{0:T(128)}, u32[]{:S(2)}) copy-start(s32[96]{0:T(128)} %counts_ref.9) | copy-start | bytes 1156
  13.3 89.9 %all-to-all-start = ((bf16[8,384,384]{2,1,0:T(8,128)(2,1)}), bf16[8,384,384]{2,1,0:T(8,128)(2,1)S(1)}, u32[]{:S(2)}, u32[]{:S(2)}) async-start(bf16[8,384,384]{2,1,0:T(8,128)(2,1)} %column_blocks.1), calls=%async_computation | async-start | bytes 4718592 | tf_op jit(solution)/shard_map/all_to_all | solution.py:248
  25.0 16.9 %collective-permute-start.1 = (bf16[512,384]{1,0:T(8,128)(2,1)S(1)}, bf16[512,384]{1,0:T(8,128)(2,1)S(1)}, u32[]{:S(2)}, u32[]{:S(2)}) collective-permute-start(bf16[512,384]{1,0:T(8,128)(2,1)S(1)} %collective-permute-done.refs_4_), channel_id=1, source_target_pairs={{0,16},{8,24},{16,32},{24,40},{32,48},{40,56},{48,64},{56,72},{64,... | collective-permute-start | bytes 1179656 | tf_op jit(solution)/shard_map/ppermute | solution.py:234
  33.4 16.3 %collective-permute-start.4 = (bf16[512,384]{1,0:T(8,128)(2,1)S(1)}, bf16[512,384]{1,0:T(8,128)(2,1)S(1)}, u32[]{:S(2)}, u32[]{:S(2)}) collective-permute-start(bf16[512,384]{1,0:T(8,128)(2,1)S(1)} %collective-permute-done.3.refs_5_), channel_id=1, source_target_pairs={{0,16},{8,24},{16,32},{24,40},{32,48},{40,56},{48,64},{56,72},{64,... | collective-permute-start | bytes 1179656 | tf_op jit(solution)/shard_map/ppermute | solution.py:234
  41.9 18.1 %collective-permute-start.2 = (bf16[512,384]{1,0:T(8,128)(2,1)S(1)}, bf16[512,384]{1,0:T(8,128)(2,1)S(1)}, u32[]{:S(2)}, u32[]{:S(2)}) collective-permute-start(bf16[512,384]{1,0:T(8,128)(2,1)S(1)} %collective-permute-done.1.refs_2_), channel_id=1, source_target_pairs={{0,16},{8,24},{16,32},{24,40},{32,48},{40,56},{48,64},{56,72},{64,... | collective-permute-start | bytes 1179656 | tf_op jit(solution)/shard_map/ppermute | solution.py:234
  49.7 16.5 %collective-permute-start.5 = (bf16[512,384]{1,0:T(8,128)(2,1)S(1)}, bf16[512,384]{1,0:T(8,128)(2,1)S(1)}, u32[]{:S(2)}, u32[]{:S(2)}) collective-permute-start(bf16[512,384]{1,0:T(8,128)(2,1)S(1)} %collective-permute-done.4.refs_3_), channel_id=1, source_target_pairs={{0,16},{8,24},{16,32},{24,40},{32,48},{40,56},{48,64},{56,72},{64,... | collective-permute-start | bytes 1179656 | tf_op jit(solution)/shard_map/ppermute | solution.py:234
  66.3 11.2 %collective-permute-start.7 = (bf16[512,384]{1,0:T(8,128)(2,1)S(1)}, bf16[512,384]{1,0:T(8,128)(2,1)S(1)}, u32[]{:S(2)}, u32[]{:S(2)}) collective-permute-start(bf16[512,384]{1,0:T(8,128)(2,1)S(1)} %collective-permute-done.2.refs_1_), channel_id=1, source_target_pairs={{8,16},{24,32},{40,48},{56,64},{72,80},{88,96},{104,112},{120,128}... | collective-permute-start | bytes 1179656 | tf_op jit(solution)/shard_map/ppermute | solution.py:234
  67.6 14.1 %collective-permute-start.8 = (bf16[512,384]{1,0:T(8,128)(2,1)S(1)}, bf16[512,384]{1,0:T(8,128)(2,1)S(1)}, u32[]{:S(2)}, u32[]{:S(2)}) collective-permute-start(bf16[512,384]{1,0:T(8,128)(2,1)S(1)} %collective-permute-done.5.refs_2_), channel_id=1, source_target_pairs={{8,16},{24,32},{40,48},{56,64},{72,80},{88,96},{104,112},{120,128}... | collective-permute-start | bytes 1179656 | tf_op jit(solution)/shard_map/ppermute | solution.py:234
  70.5 11.2 %collective-permute-start.9 = (f32[3,512,256]{2,1,0:T(8,128)S(1)}, f32[3,512,256]{2,1,0:T(8,128)S(1)}, u32[]{:S(2)}, u32[]{:S(2)}) collective-permute-start(f32[3,512,256]{2,1,0:T(8,128)S(1)} %attend_3_other.1), channel_id=1, source_target_pairs={{0,8},{8,0},{16,24},{24,16},{32,40},{40,32},{48,56},{56,48},{64,72... | collective-permute-start | bytes 4718600 | tf_op jit(solution)/shard_map/ppermute | solution.py:234
  85.6 12.5 %collective-permute-start.14 = (bf16[256,384]{1,0:T(8,128)(2,1)S(1)}, bf16[256,384]{1,0:T(8,128)(2,1)S(1)}, u32[]{:S(2)}, u32[]{:S(2)}) collective-permute-start(bf16[256,384]{1,0:T(8,128)(2,1)S(1)} %get-tuple-element.32.refs_0_), channel_id=1, source_target_pairs={{0,1},{1,2},{2,3},{3,4},{4,5},{5,6},{6,7},{7,0},{8,9},{9,10},{10,1... | collective-permute-start | bytes 589832 | tf_op jit(solution)/shard_map/ppermute | solution.py:234
  90.3 14.3 %collective-permute-start.10 = (bf16[256,384]{1,0:T(8,128)(2,1)}, bf16[256,384]{1,0:T(8,128)(2,1)S(1)}, u32[]{:S(2)}, u32[]{:S(2)}) collective-permute-start(bf16[256,384]{1,0:T(8,128)(2,1)} %get-tuple-element.31.refs_1_), channel_id=1, source_target_pairs={{0,1},{1,2},{2,3},{3,4},{4,5},{5,6},{6,7},{7,0},{8,9},{9,10},{10,1... | collective-permute-start | bytes 589832 | tf_op jit(solution)/shard_map/ppermute | solution.py:234
  92.9 11.7 %collective-permute-start.11 = (bf16[256,384]{1,0:T(8,128)(2,1)}, bf16[256,384]{1,0:T(8,128)(2,1)S(1)}, u32[]{:S(2)}, u32[]{:S(2)}) collective-permute-start(bf16[256,384]{1,0:T(8,128)(2,1)} %get-tuple-element.31.refs_1_), channel_id=1, source_target_pairs={{0,7},{1,0},{2,1},{3,2},{4,3},{5,4},{6,5},{7,6},{8,15},{9,8},{10,9... | collective-permute-start | bytes 589832 | tf_op jit(solution)/shard_map/ppermute | solution.py:234
  96.1 14.3 %collective-permute-start.15 = (bf16[256,384]{1,0:T(8,128)(2,1)S(1)}, bf16[256,384]{1,0:T(8,128)(2,1)S(1)}, u32[]{:S(2)}, u32[]{:S(2)}) collective-permute-start(bf16[256,384]{1,0:T(8,128)(2,1)S(1)} %get-tuple-element.32.refs_0_), channel_id=1, source_target_pairs={{0,7},{1,0},{2,1},{3,2},{4,3},{5,4},{6,5},{7,6},{8,15},{9,8},{10,9... | collective-permute-start | bytes 589832 | tf_op jit(solution)/shard_map/ppermute | solution.py:234
  98.1 14.3 %collective-permute-start.18 = (bf16[256,384]{1,0:T(8,128)(2,1)S(1)}, bf16[256,384]{1,0:T(8,128)(2,1)S(1)}, u32[]{:S(2)}, u32[]{:S(2)}) collective-permute-start(bf16[256,384]{1,0:T(8,128)(2,1)S(1)} %collective-permute-done.14.refs_1_), channel_id=1, source_target_pairs={{0,1},{1,2},{2,3},{3,4},{4,5},{5,6},{6,7},{7,0},{8,9},{9,10},{10,1... | collective-permute-start | bytes 589832 | tf_op jit(solution)/shard_map/ppermute | solution.py:234
  104.6 13.6 %collective-permute-start.12 = (bf16[256,384]{1,0:T(8,128)(2,1)S(1)}, bf16[256,384]{1,0:T(8,128)(2,1)S(1)}, u32[]{:S(2)}, u32[]{:S(2)}) collective-permute-start(bf16[256,384]{1,0:T(8,128)(2,1)S(1)} %collective-permute-done.10.refs_2_), channel_id=1, source_target_pairs={{0,1},{1,2},{2,3},{3,4},{4,5},{5,6},{6,7},{7,0},{8,9},{9,10},{10,1... | collective-permute-start | bytes 589832 | tf_op jit(solution)/shard_map/ppermute | solution.py:234
  107.2 11.0 %collective-permute-start.13 = (bf16[256,384]{1,0:T(8,128)(2,1)S(1)}, bf16[256,384]{1,0:T(8,128)(2,1)S(1)}, u32[]{:S(2)}, u32[]{:S(2)}) collective-permute-start(bf16[256,384]{1,0:T(8,128)(2,1)S(1)} %collective-permute-done.11.refs_4_), channel_id=1, source_target_pairs={{0,7},{1,0},{2,1},{3,2},{4,3},{5,4},{6,5},{7,6},{8,15},{9,8},{10,9... | collective-permute-start | bytes 589832 | tf_op jit(solution)/shard_map/ppermute | solution.py:234
  110.5 13.6 %collective-permute-start.19 = (bf16[256,384]{1,0:T(8,128)(2,1)S(1)}, bf16[256,384]{1,0:T(8,128)(2,1)S(1)}, u32[]{:S(2)}, u32[]{:S(2)}) collective-permute-start(bf16[256,384]{1,0:T(8,128)(2,1)S(1)} %collective-permute-done.15.refs_3_), channel_id=1, source_target_pairs={{0,7},{1,0},{2,1},{3,2},{4,3},{5,4},{6,5},{7,6},{8,15},{9,8},{10,9... | collective-permute-start | bytes 589832 | tf_op jit(solution)/shard_map/ppermute | solution.py:234
  112.4 13.6 %collective-permute-start.20 = (bf16[256,384]{1,0:T(8,128)(2,1)S(1)}, bf16[256,384]{1,0:T(8,128)(2,1)S(1)}, u32[]{:S(2)}, u32[]{:S(2)}) collective-permute-start(bf16[256,384]{1,0:T(8,128)(2,1)S(1)} %collective-permute-done.18.refs_1_), channel_id=1, source_target_pairs={{0,1},{1,2},{2,3},{3,4},{4,5},{5,6},{6,7},{7,0},{8,9},{9,10},{10,1... | collective-permute-start | bytes 589832 | tf_op jit(solution)/shard_map/ppermute | solution.py:234
  118.2 13.6 %collective-permute-start.16 = (bf16[256,384]{1,0:T(8,128)(2,1)S(1)}, bf16[256,384]{1,0:T(8,128)(2,1)S(1)}, u32[]{:S(2)}, u32[]{:S(2)}) collective-permute-start(bf16[256,384]{1,0:T(8,128)(2,1)S(1)} %collective-permute-done.12.refs_2_), channel_id=1, source_target_pairs={{0,1},{1,2},{2,3},{3,4},{4,5},{5,6},{6,7},{7,0},{8,9},{9,10},{10,1... | collective-permute-start | bytes 589832 | tf_op jit(solution)/shard_map/ppermute | solution.py:234
  120.8 11.0 %collective-permute-start.17 = (bf16[256,384]{1,0:T(8,128)(2,1)S(1)}, bf16[256,384]{1,0:T(8,128)(2,1)S(1)}, u32[]{:S(2)}, u32[]{:S(2)}) collective-permute-start(bf16[256,384]{1,0:T(8,128)(2,1)S(1)} %collective-permute-done.13.refs_4_), channel_id=1, source_target_pairs={{0,7},{1,0},{2,1},{3,2},{4,3},{5,4},{6,5},{7,6},{8,15},{9,8},{10,9... | collective-permute-start | bytes 589832 | tf_op jit(solution)/shard_map/ppermute | solution.py:234
  124.1 9.7 %collective-permute-start.21 = (bf16[256,384]{1,0:T(8,128)(2,1)S(1)}, bf16[256,384]{1,0:T(8,128)(2,1)S(1)}, u32[]{:S(2)}, u32[]{:S(2)}) collective-permute-start(bf16[256,384]{1,0:T(8,128)(2,1)S(1)} %collective-permute-done.19.refs_3_), channel_id=1, source_target_pairs={{0,7},{1,0},{2,1},{3,2},{4,3},{5,4},{6,5},{7,6},{8,15},{9,8},{10,9... | collective-permute-start | bytes 589832 | tf_op jit(solution)/shard_map/ppermute | solution.py:234
  126.0 8.4 %collective-permute-start.22 = (bf16[256,384]{1,0:T(8,128)(2,1)S(1)}, bf16[256,384]{1,0:T(8,128)(2,1)S(1)}, u32[]{:S(2)}, u32[]{:S(2)}) collective-permute-start(bf16[256,384]{1,0:T(8,128)(2,1)S(1)} %collective-permute-done.20.refs_1_), channel_id=1, source_target_pairs={{0,1},{1,2},{2,3},{3,4},{4,5},{5,6},{6,7},{7,0},{8,9},{9,10},{10,1... | collective-permute-start | bytes 589832 | tf_op jit(solution)/shard_map/ppermute | solution.py:234
  131.8 8.8 %collective-permute-start.23 = (bf16[256,384]{1,0:T(8,128)(2,1)S(1)}, bf16[256,384]{1,0:T(8,128)(2,1)S(1)}, u32[]{:S(2)}, u32[]{:S(2)}) collective-permute-start(bf16[256,384]{1,0:T(8,128)(2,1)S(1)} %collective-permute-done.17.refs_4_), channel_id=1, source_target_pairs={{0,7},{1,0},{2,1},{3,2},{4,3},{5,4},{6,5},{7,6},{8,15},{9,8},{10,9... | collective-permute-start | bytes 589832 | tf_op jit(solution)/shard_map/ppermute | solution.py:234

commit v4 on v3

--- a/solution.py
+++ b/solution.py
@@ -48,10 +48,6 @@
     back = query - source
     seen = (source >= 0) & (back >= 0) & (back < span_ref[query])
     return jnp.where(seen, counts_ref[jnp.maximum(source, 0)], 0)
-
-
-def in_hbm(array):
-    return pltpu.with_memory_space_constraint(array, pltpu.HBM)
 
 
 def _unpack(packed, acc, top):
@@ -88,25 +84,31 @@
     return body
 
 
-def _specs(per_frame):
-    column = pl.BlockSpec((per_frame, HD), lambda h, *_: (0, h))
+def _plane(array, plane):
+    if array.ndim == 2:
+        return pl.BlockSpec((array.shape[0], HD), lambda h, *_: (0, h))
+    return pl.BlockSpec((None, array.shape[1], HD), lambda h, *_: (plane, 0, h))
+
+
+def _specs(per_frame, head0):
+    column = pl.BlockSpec((per_frame, HD), lambda h, *_: (0, head0 + h))
     packed = pl.BlockSpec((1, per_frame, 2 * HD), lambda h, *_: (h, 0, 0))
     scratch = [pltpu.VMEM((1, per_frame, 2 * HD), jnp.float32), pltpu.VMEM((1, per_frame, HD), jnp.float32)]
     return column, packed, scratch
 
 
-def attention_call(scalars, queries, sources, sides, hops, states, name, cost):
-    per_frame, width = queries[0].shape
-    heads = width // HD
-    column, packed, scratch = _specs(per_frame)
-    operands = list(queries) + [array for pair in sources for array in pair] + list(states or ())
+def attention_call(scalars, queries, head0, heads, sources, sides, hops, states, name, cost):
+    per_frame = queries[0].shape[0]
+    column, packed, scratch = _specs(per_frame, head0)
+    operands = list(queries) + [source for source in sources for _ in (0, 1)] + list(states or ())
+    planes = [_plane(source, plane) for source in sources for plane in (0, 1)]
     return pl.pallas_call(
         _attention_body(sides, hops, states is None),
         out_shape=[jax.ShapeDtypeStruct((heads, per_frame, 2 * HD), jnp.float32)] * len(sides),
         grid_spec=pltpu.PrefetchScalarGridSpec(
             num_scalar_prefetch=3,
             grid=(heads,),
-            in_specs=[column] * (len(sides) + 2 * len(hops)) + [packed] * len(states or ()),
+            in_specs=[column] * len(sides) + planes + [packed] * len(states or ()),
             out_specs=[packed] * len(sides),
             scratch_shapes=scratch * len(sides),
         ),
@@ -116,7 +118,7 @@
     )(*scalars, *operands)
 
 
-def _finish_body(frame_ref, span_ref, counts_ref, q_ref, k_ref, v_ref, own, other, upper_ref, lower_ref, acc, top):
+def _finish_body(frame_ref, span_ref, counts_ref, q_ref, k_ref, v_ref, own, other, out_ref, acc, top):
     _unpack(own, acc, top)
     limit = _visible(frame_ref[0], 0, WIN - 1, span_ref, counts_ref)
     limit = jnp.where(frame_ref[0] % 2 == 0, limit, 0)
@@ -128,29 +130,46 @@
     other_part = jnp.exp2((other_top - both_top) * EXP2_SCALE)
     total = own_total * own_part + other_total * other_part
     mixed = acc[0, :, :HD] * own_part + other[0, :, :HD] * other_part
-    mixed = (mixed / total).astype(jnp.bfloat16)
-    half = upper_ref.shape[0]
-    upper_ref[...] = mixed[:half]
-    lower_ref[...] = mixed[half:]
-
-
-def finish_call(scalars, queries, keys, values, own, other, name):
-    per_frame, width = queries.shape
-    column, packed, scratch = _specs(per_frame)
+    out_ref[...] = (mixed / total).astype(jnp.bfloat16)
+
+
+def finish_call(scalars, queries, head0, keys, values, own, other, name):
+    heads, per_frame, _ = own.shape
+    column, packed, scratch = _specs(per_frame, head0)
     return pl.pallas_call(
         _finish_body,
-        out_shape=[jax.ShapeDtypeStruct((per_frame // 2, width), jnp.bfloat16)] * 2,
+        out_shape=jax.ShapeDtypeStruct((per_frame, heads * HD), jnp.bfloat16),
         grid_spec=pltpu.PrefetchScalarGridSpec(
             num_scalar_prefetch=3,
-            grid=(width // HD,),
-            in_specs=[column, column, column, packed, packed],
-            out_specs=[pl.BlockSpec((per_frame // 2, HD), lambda h, *_: (0, h))] * 2,
+            grid=(heads,),
+            in_specs=[column, _plane(keys, 0), _plane(values, 1), packed, packed],
+            out_specs=pl.BlockSpec((per_frame, HD), lambda h, *_: (0, h)),
             scratch_shapes=scratch,
         ),
         cost_estimate=BRIEF,
         compiler_params=pltpu.CompilerParams(vmem_limit_bytes=SMALL_VMEM),
         name=name,
     )(*scalars, queries, keys, values, own, other)
+
+
+def _pack_body(first, k_ref, v_ref, a_ref, b_ref):
+    for plane, ref in enumerate((k_ref, v_ref)):
+        a_ref[plane] = ref[:, :first]
+        b_ref[plane] = ref[:, first:]
+
+
+def pack_call(keys, values, first):
+    per_frame, width = keys.shape
+    return pl.pallas_call(
+        lambda *refs: _pack_body(first, *refs),
+        out_shape=[
+            jax.ShapeDtypeStruct((2, per_frame, first), keys.dtype),
+            jax.ShapeDtypeStruct((2, per_frame, width - first), keys.dtype),
+        ],
+        cost_estimate=BRIEF,
+        compiler_params=pltpu.CompilerParams(vmem_limit_bytes=SMALL_VMEM),
+        name="pack",
+    )(keys, values)
 
 
 def in_hbm(array):
@@ -178,38 +197,45 @@
     )(in_hbm(weight))
 
 
-def _project_body(places, has_base):
+def _project_body(places, row0, has_base, has_gathered):
     def body(group_ref, *refs):
         out_ref, w_ref = refs[-1], refs[-2]
+        gathered_ref = refs[has_base] if has_gathered else None
+        pieces = refs[has_base + has_gathered : -2]
         groups, half = w_ref.shape[0], out_ref.shape[0] // 2
         for part in (0, 1):
             rows = pl.ds(part * half, half)
-            total = refs[0][rows, :] if has_base else None
-            for (place, offset), ref in zip(places, refs[has_base:-2], strict=True):
-                if place == part:
+            total = refs[0][rows, :] if has_base else jnp.zeros((half, out_ref.shape[1]), jnp.float32)
+            if has_gathered:
+                for source in range(groups):
+                    total += jnp.dot(
+                        gathered_ref[source, rows, :], w_ref[source, :row0, :], preferred_element_type=jnp.float32
+                    )
+            for (place, offset), ref in zip(places, pieces, strict=True):
+                if place in (part, None):
                     source = lax.rem(group_ref[0] + offset, groups)
-                    product = jnp.dot(ref[...], w_ref[source], preferred_element_type=jnp.float32)
-                    total = product if total is None else total + product
+                    piece = ref[rows, :] if place is None else ref[...]
+                    total += jnp.dot(piece, w_ref[source, row0:, :], preferred_element_type=jnp.float32)
             out_ref[rows, :] = total.astype(out_ref.dtype)
 
     return body
 
 
-def project_call(group, weight, base, pieces, places, dtype, name):
-    groups, height, columns = weight.shape
-    half = pieces[0].shape[0]
-    operands = ([] if base is None else [base]) + list(pieces) + [weight]
-    return pl.pallas_call(
-        _project_body(places, base is not None),
-        out_shape=jax.ShapeDtypeStruct((2 * half, columns), dtype),
+def project_call(group, weight, row0, base, gathered, pieces, places, dtype, name):
+    groups, _, columns = weight.shape
+    per_frame = pieces[0].shape[0] * (1 if places[0][0] is None else 2)
+    operands = [x for x in (base, gathered) if x is not None] + list(pieces) + [weight]
+    return pl.pallas_call(
+        _project_body(places, row0, base is not None, gathered is not None),
+        out_shape=jax.ShapeDtypeStruct((per_frame, columns), dtype),
         grid_spec=pltpu.PrefetchScalarGridSpec(
             num_scalar_prefetch=1,
             grid=(1,),
             in_specs=[pl.BlockSpec(x.shape, lambda i, g, n=x.ndim: (0,) * n) for x in operands],
-            out_specs=pl.BlockSpec((2 * half, columns), lambda i, g: (0, 0)),
+            out_specs=pl.BlockSpec((per_frame, columns), lambda i, g: (0, 0)),
         ),
         cost_estimate=pl.CostEstimate(
-            flops=2 * len(pieces) * half * height * columns, transcendentals=0, bytes_accessed=4 << 20
+            flops=len(pieces) * per_frame * weight.shape[1] * columns, transcendentals=0, bytes_accessed=4 << 20
         ),
         compiler_params=pltpu.CompilerParams(vmem_limit_bytes=LARGE_VMEM),
         name=name,
@@ -233,43 +259,58 @@
     def send(block, route, axis="frame"):
         return lax.ppermute(block, axis, route)
 
-    def attend(sources, sides, hops, states, name, cost=BRIEF):
+    def attend(head0, heads, sources, sides, hops, states, name, cost):
         both = (in_hbm(queries), q_other)
         return attention_call(
-            scalars, [both[side] for side in sides], sources, sides, hops, states, name, cost
+            scalars, [both[side] for side in sides], head0, heads, sources, sides, hops, states, name, cost
         )
 
-    k1, v1 = send(keys, by_chip), send(values, by_chip)
+    a0, b0 = pack_call(keys, values, HD)
+    a1, b1 = send(a0, by_chip), send(b0, by_chip)
     q_other = send(queries, swap)
-    k2, v2 = send(k1, by_chip), send(v1, by_chip)
-    near = [(in_hbm(keys), in_hbm(values)), (k1, v1)]
-    own, other = attend(near, (0, 1), (0, 1), None, "attend_01", LONG)
-    blocks = column_blocks(out_weight, groups)
-    weight = lax.all_to_all(blocks, "head", split_axis=0, concat_axis=0, tiled=True)
-    k3, v3 = send(k2, by_chip), send(v2, by_chip)
-    own, other = attend([(k2, v2)], (0, 1), (2,), [own, other], "attend_2", LONG)
-    k3, v3, own, other = after((k3, v3, own, other))
-    (other,) = attend([(k3, v3)], (1,), (3,), [other], "attend_3_other")
-    from_other = send(other, swap)
-    k4, v4 = send(k3, to_even), send(v3, to_even)
-    (own,) = attend([(k3, v3)], (0,), (3,), [own], "attend_3_own", LONG)
-    attended = finish_call(scalars, in_hbm(queries), k4, v4, own, from_other, "finish")
-
-    def project(base, pieces, places, dtype, name):
-        return project_call(group, weight, base, pieces, places, dtype, name)
-
-    up, down = list(attended), list(attended)
-    held, places, total = list(attended), ((0, 0), (1, 0)), None
-    for step in (1, 2, 3):
-        up = [send(block, upward, "head") for block in up]
-        down = [send(block, downward, "head") for block in down]
-        total = project(total, held, places, jnp.float32, f"project_{step - 1}")
-        held = up + down
-        places = ((0, groups - step), (1, groups - step), (0, step), (1, step))
-        up[1], down[1], total = after((up[1], down[1], total))
-    far = [send(up[0], upward, "head"), send(down[1], downward, "head")]
-    total = project(total, held, places, jnp.float32, "project_3")
-    return project(total, far, ((0, 4), (1, 4)), jnp.bfloat16, "project_4")
+    weight = lax.all_to_all(
+        column_blocks(out_weight, groups), "head", split_axis=0, concat_axis=0, tiled=True
+    )
+    a2 = send(a1, by_chip)
+    a2, b1 = after((a2, b1))
+    a3, b2 = send(a2, by_chip), send(b1, by_chip)
+    states_b = attend(1, 2, [b0, b1], (0, 1), (0, 1), None, "attend_b01", LONG)
+    a4 = send(a3, to_even)
+    own_a, other_a = attend(0, 1, [a0, a1, a2, a3], (0, 1), (0, 1, 2, 3), None, "attend_a0123", LONG)
+    b2, a4, own_a, other_a, states_b = after((b2, a4, own_a, other_a, states_b))
+    b3 = send(b2, by_chip)
+    from_other_a = send(other_a, swap)
+    own_b, other_b = attend(1, 2, [b2], (0, 1), (2,), states_b, "attend_b2", LONG)
+    attended_a = finish_call(scalars, in_hbm(queries), 0, a4, a4, own_a, from_other_a, "finish_a")
+    gathered_a = lax.all_to_all(
+        jnp.broadcast_to(attended_a[None], (groups, per_frame, HD)),
+        "head", split_axis=0, concat_axis=0, tiled=True,
+    )
+    b3, own_b, other_b, attended_a = after((b3, own_b, other_b, attended_a))
+    b4_keys, b4_values = send(b3[0], to_even), send(b3[1], to_even)
+    (other_b,) = attend(1, 2, [b3], (1,), (3,), [other_b], "attend_b3_other", BRIEF)
+    from_other_b = send(other_b, swap)
+    (own_b,) = attend(1, 2, [b3], (0,), (3,), [own_b], "attend_b3_own", BRIEF)
+    attended = finish_call(scalars, in_hbm(queries), 1, b4_keys, b4_values, own_b, from_other_b, "finish_b")
+
+    def project(base, gathered, pieces, places, dtype, name):
+        return project_call(group, weight, HD, base, gathered, pieces, places, dtype, name)
+
+    half = per_frame // 2
+    f32 = jnp.float32
+    up1, down1 = send(attended, upward, "head"), send(attended, downward, "head")
+    total = project(None, None, [attended], ((None, 0),), f32, "project_0")
+    up2, down2 = send(up1, upward, "head"), send(down1, downward, "head")
+    total = project(total, gathered_a, [up1, down1], ((None, groups - 1), (None, 1)), f32, "project_1")
+    up3 = send(up2, upward, "head")
+    down2, total = after((down2, total))
+    down3 = send(down2, downward, "head")
+    total = project(total, None, [up2, down2], ((None, groups - 2), (None, 2)), f32, "project_2")
+    up4 = send(up3[:half], upward, "head")
+    down3, total = after((down3, total))
+    down4 = send(down3[half:], downward, "head")
+    total = project(total, None, [up3, down3], ((None, groups - 3), (None, 3)), f32, "project_3")
+    return project(total, None, [up4, down4], ((0, 4), (1, 4)), jnp.bfloat16, "project_4")
 
 
 def solution(mesh):

time: 143 us -> 167 us (1.17)
  the two profiles are of different devices: /device:TPU:30 before, /device:TPU:26 now
where the time goes in v4:
time: 167 us; the launch traced here: 166 us
  starting transfers between devices  73 us (44%)
  waiting for transfers between devices  47.6 us (29%)
  Pallas kernels  35.2 us (21%)
  local copies, waits for them, and re-layouts  10.1 us (6%)
    ppermute x20, starting transfers between devices, send(): return lax.ppermute(block, axis, route)  55.7 us
    ppermute x20, waiting for transfers between devices, send(): return lax.ppermute(block, axis, route)  44.8 us
    pallas_call x5, Pallas kernels, attention_call(): pl.pallas_call(_attention_body(sides, hops, states is None), out_shape=[j...  20.4 us
    all_to_all x1, starting transfers between devices, on_device(): lax.all_to_all(jnp.broadcast_to(attended_a[None], (groups, per_frame, HD)...  9.92 us
    unnamed x20, local copies, waits for them, and re-layouts  8.02 us
    all_to_all x1, starting transfers between devices, on_device(): lax.all_to_all(column_blocks(out_weight, groups), 'head', split_axis=0, c...  7.45 us
    pallas_call x5, Pallas kernels, project_call(): pl.pallas_call(_project_body(places, row0, base is not None, gathered is...  6.68 us
    pallas_call x2, Pallas kernels, finish_call(): pl.pallas_call(_finish_body, out_shape=jax.ShapeDtypeStruct((per_frame, h...  4.31 us
  transfers between devices with their start and end apart: 22, of which 11 were waited for; matrix products, arithmetic and copies ran while one was open for 1% of the time, Pallas kernels for 20%

profile of v4, /device:TPU:26, one launch (start us, length us, event | category | flops | bytes accessed | tf_op | source)
XLA Modules:
  0.0 166.3 jit_solution(14862583239366142176)
XLA Ops:
  3.0 4.3 %collective-permute-start = (bf16[2,512,128]{2,1,0:T(8,128)(2,1)}, bf16[2,512,128]{2,1,0:T(8,128)(2,1)}, u32[]{:S(2)}, u32[]{:S(2)}) collective-permute-start(bf16[2,512,128]{2,1,0:T(8,128)(2,1)} %get-tuple-element.28.refs_2_.refs_3_), channel_id=1, source_target_pairs={{0,16},{8,24},{16,32},{24,40},{32,48},{40,56},{48,64},{56,72},{64,... | collective-permute-start | bytes 786440 | tf_op jit(solution)/shard_map/ppermute | solution.py:260
  7.2 4.3 %collective-permute-start.2 = (bf16[2,512,256]{2,1,0:T(8,128)(2,1)}, bf16[2,512,256]{2,1,0:T(8,128)(2,1)S(1)}, u32[]{:S(2)}, u32[]{:S(2)}) collective-permute-start(bf16[2,512,256]{2,1,0:T(8,128)(2,1)} %get-tuple-element.29.refs_2_.refs_3_), channel_id=1, source_target_pairs={{0,16},{8,24},{16,32},{24,40},{32,48},{40,56},{48,64},{56,72},{64,... | collective-permute-start | bytes 1572872 | tf_op jit(solution)/shard_map/ppermute | solution.py:260
  11.5 1.9 %collective-permute-start.6 = (bf16[512,384]{1,0:T(8,128)(2,1)}, bf16[512,384]{1,0:T(8,128)(2,1)S(1)}, u32[]{:S(2)}, u32[]{:S(2)}) collective-permute-start(bf16[512,384]{1,0:T(8,128)(2,1)} %q_ref.3), channel_id=1, source_target_pairs={{0,8},{8,0},{16,24},{24,16},{32,40},{40,32},{48,56},{56,48},{64,72... | collective-permute-start | bytes 1179656 | tf_op jit(solution)/shard_map/ppermute | solution.py:260
  13.5 2.8 %column_blocks.1 = bf16[8,384,384]{2,1,0:T(8,128)(2,1)} custom-call(bf16[384,3072]{1,0:T(8,128)(2,1)} %w_ref.1), custom_call_target="tpu_custom_call" | custom-call | flops 1 | bytes 1 | tf_op jit(solution)/shard_map/column_blocks/pallas_call | solution.py:188
  16.3 7.5 %all-to-all-start = ((bf16[8,384,384]{2,1,0:T(8,128)(2,1)}), bf16[8,384,384]{2,1,0:T(8,128)(2,1)S(1)}, u32[]{:S(2)}, u32[]{:S(2)}) async-start(bf16[8,384,384]{2,1,0:T(8,128)(2,1)} %column_blocks.1), calls=%async_computation | async-start | bytes 4718592 | tf_op jit(solution)/shard_map/all_to_all | solution.py:271
  24.9 3.1 %collective-permute-start.1 = (bf16[2,512,128]{2,1,0:T(8,128)(2,1)}, bf16[2,512,128]{2,1,0:T(8,128)(2,1)}, u32[]{:S(2)}, u32[]{:S(2)}) collective-permute-start(bf16[2,512,128]{2,1,0:T(8,128)(2,1)} %collective-permute-done.refs_4_.refs_5_), channel_id=1, source_target_pairs={{0,16},{8,24},{16,32},{24,40},{32,48},{40,56},{48,64},{56,72},{64,... | collective-permute-start | bytes 786440 | tf_op jit(solution)/shard_map/ppermute | solution.py:260
  28.0 12.9 %collective-permute-done.1.refs_6_.refs_7_ = bf16[2,512,128]{2,1,0:T(8,128)(2,1)} collective-permute-done((bf16[2,512,128]{2,1,0:T(8,128)(2,1)}, bf16[2,512,128]{2,1,0:T(8,128)(2,1)}, u32[]{:S(2)}, u32[]{:S(2)}) %collective-permute-start.1) | collective-permute-done | bytes 262176 | tf_op jit(solution)/shard_map/ppermute | solution.py:260
  42.9 1.9 %collective-permute-start.3 = (bf16[2,512,256]{2,1,0:T(8,128)(2,1)S(1)}, bf16[2,512,256]{2,1,0:T(8,128)(2,1)}, u32[]{:S(2)}, u32[]{:S(2)}) collective-permute-start(bf16[2,512,256]{2,1,0:T(8,128)(2,1)S(1)} %collective-permute-done.2.refs_4_.refs_5_), channel_id=1, source_target_pairs={{0,16},{8,24},{16,32},{24,40},{32,48},{40,56},{48,64},{56,72},{64,... | collective-permute-start | bytes 1572872 | tf_op jit(solution)/shard_map/ppermute | solution.py:260
  44.9 6.3 %attend_b01.1 = (f32[2,512,256]{2,1,0:T(8,128)S(1)}, f32[2,512,256]{2,1,0:T(8,128)S(1)}) custom-call(s32[1]{0:T(128)} %bitcast.1.frame_ref, s32[96]{0:T(128)S(1)} %copy-done.4, s32[96]{0:T(128)S(1)} %copy-done.5, bf16[512,384]{1,0:T(8,128)(2,1)} %q_ref.3, bf16[512,384]{1,0:T(8,128)(2,1)S(1)} %collective-permute-done.6.refs_1_.refs_0_, ...), custom_call_target="tpu_custom_call" | custom-call | flops 17179869184 | bytes 1 | tf_op jit(solution)/shard_map/attend_b01/pallas_call | solution.py:105
  55.7 5.5 %attend_a0123.1 = (f32[1,512,256]{2,1,0:T(8,128)S(1)}, f32[1,512,256]{2,1,0:T(8,128)S(1)}) custom-call(s32[1]{0:T(128)} %bitcast.1.frame_ref, s32[96]{0:T(128)S(1)} %copy-done.4, s32[96]{0:T(128)S(1)} %copy-done.5, bf16[512,384]{1,0:T(8,128)(2,1)} %q_ref.3, bf16[512,384]{1,0:T(8,128)(2,1)S(1)} %collective-permute-done.6.refs_1_.refs_0_, ...), custom_call_target="tpu_custom_call" | custom-call | flops 17179869184 | bytes 1 | tf_op jit(solution)/shard_map/attend_a0123/pallas_call | solution.py:105
  61.2 5.7 %collective-permute-done.5.k_ref.v_ref = bf16[2,512,128]{2,1,0:T(8,128)(2,1)S(1)} collective-permute-done((bf16[2,512,128]{2,1,0:T(8,128)(2,1)S(1)}, bf16[2,512,128]{2,1,0:T(8,128)(2,1)S(1)}, u32[]{:S(2)}, u32[]{:S(2)}) %collective-permute-start.5) | collective-permute-done | bytes 262176 | tf_op jit(solution)/shard_map/ppermute | solution.py:260
  68.9 1.9 %collective-permute-start.7 = (bf16[2,512,256]{2,1,0:T(8,128)(2,1)}, bf16[2,512,256]{2,1,0:T(8,128)(2,1)S(1)}, u32[]{:S(2)}, u32[]{:S(2)}) collective-permute-start(bf16[2,512,256]{2,1,0:T(8,128)(2,1)} %collective-permute-done.3.refs_2_.refs_3_), channel_id=1, source_target_pairs={{0,16},{8,24},{16,32},{24,40},{32,48},{40,56},{48,64},{56,72},{64,... | collective-permute-start | bytes 1572872 | tf_op jit(solution)/shard_map/ppermute | solution.py:260
  72.7 2.8 %all-to-all-done.refs_1_.refs_4_.refs_3_ = bf16[8,384,384]{2,1,0:T(8,128)(2,1)S(1)} async-done(((bf16[8,384,384]{2,1,0:T(8,128)(2,1)}), bf16[8,384,384]{2,1,0:T(8,128)(2,1)S(1)}, u32[]{:S(2)}, u32[]{:S(2)}) %all-to-all-start) | async-done | bytes 2359328 | tf_op jit(solution)/shard_map/all_to_all | solution.py:271
  76.6 9.9 %all-to-all-start.1 = ((bf16[8,512,128]{2,1,0:T(8,128)(2,1)}), bf16[8,512,128]{2,1,0:T(8,128)(2,1)}, u32[]{:S(2)}, u32[]{:S(2)}) async-start(bf16[8,512,128]{2,1,0:T(8,128)(2,1)} %broadcast_in_dim.2), calls=%async_computation.1 | async-start | bytes 2097152 | tf_op jit(solution)/shard_map/all_to_all | solution.py:285
  89.0 4.0 %attend_b2.1 = (f32[2,512,256]{2,1,0:T(8,128)S(1)}, f32[2,512,256]{2,1,0:T(8,128)S(1)}) custom-call(s32[1]{0:T(128)} %bitcast.1.frame_ref, s32[96]{0:T(128)S(1)} %copy-done.4, s32[96]{0:T(128)S(1)} %copy-done.5, bf16[512,384]{1,0:T(8,128)(2,1)} %q_ref.3, bf16[512,384]{1,0:T(8,128)(2,1)S(1)} %collective-permute-done.6.refs_1_.refs_0_, ...), custom_call_target="tpu_custom_call" | custom-call | flops 17179869184 | bytes 1 | tf_op jit(solution)/shard_map/attend_b2/pallas_call | solution.py:105
  93.0 2.6 %attend_b3_other.1 = f32[2,512,256]{2,1,0:T(8,128)S(1)} custom-call(s32[1]{0:T(128)} %bitcast.1.frame_ref, s32[96]{0:T(128)S(1)} %copy-done.4, s32[96]{0:T(128)S(1)} %copy-done.5, bf16[512,384]{1,0:T(8,128)(2,1)S(1)} %collective-permute-done.6.refs_1_.refs_0_, bf16[2,512,256]{2,1,0:T(8,128)(2,1)S(1)} %collective-permute-done.7.refs_1_.refs_2_, ...), custom_call_target="tpu_custom_call" | custom-call | flops 1 | bytes 1 | tf_op jit(solution)/shard_map/attend_b3_other/pallas_call | solution.py:105
  95.6 1.9 %collective-permute-start.11 = (f32[2,512,256]{2,1,0:T(8,128)S(1)}, f32[2,512,256]{2,1,0:T(8,128)S(1)}, u32[]{:S(2)}, u32[]{:S(2)}) collective-permute-start(f32[2,512,256]{2,1,0:T(8,128)S(1)} %attend_b3_other.1), channel_id=1, source_target_pairs={{0,8},{8,0},{16,24},{24,16},{32,40},{40,32},{48,56},{56,48},{64,72... | collective-permute-start | bytes 3145736 | tf_op jit(solution)/shard_map/ppermute | solution.py:260
  100.2 2.0 %attend_b3_own.1.own = f32[2,512,256]{2,1,0:T(8,128)S(1)} custom-call(s32[1]{0:T(128)} %bitcast.1.frame_ref, s32[96]{0:T(128)S(1)} %copy-done.4, s32[96]{0:T(128)S(1)} %copy-done.5, bf16[512,384]{1,0:T(8,128)(2,1)} %q_ref.3, bf16[2,512,256]{2,1,0:T(8,128)(2,1)S(1)} %collective-permute-done.7.refs_1_.refs_2_, ...), custom_call_target="tpu_custom_call" | custom-call | flops 1 | bytes 1 | tf_op jit(solution)/shard_map/attend_b3_own/pallas_call | solution.py:105
  102.3 8.0 %collective-permute-done.10.v_ref = bf16[512,256]{1,0:T(8,128)(2,1)S(1)} collective-permute-done((bf16[512,256]{1,0:T(8,128)(2,1)S(1)}, bf16[512,256]{1,0:T(8,128)(2,1)S(1)}, u32[]{:S(2)}, u32[]{:S(2)}) %collective-permute-start.10) | collective-permute-done | bytes 262176 | tf_op jit(solution)/shard_map/ppermute | solution.py:260
  110.2 2.8 %collective-permute-done.9.k_ref = bf16[512,256]{1,0:T(8,128)(2,1)S(1)} collective-permute-done((bf16[512,256]{1,0:T(8,128)(2,1)S(1)}, bf16[512,256]{1,0:T(8,128)(2,1)S(1)}, u32[]{:S(2)}, u32[]{:S(2)}) %collective-permute-start.9) | collective-permute-done | bytes 262176 | tf_op jit(solution)/shard_map/ppermute | solution.py:260
  113.1 2.4 %finish_b.1.refs_0_ = bf16[512,256]{1,0:T(8,128)(2,1)S(1)} custom-call(s32[1]{0:T(128)} %bitcast.1.frame_ref, s32[96]{0:T(128)S(1)} %copy-done.4, s32[96]{0:T(128)S(1)} %copy-done.5, bf16[512,384]{1,0:T(8,128)(2,1)} %q_ref.3, bf16[512,256]{1,0:T(8,128)(2,1)S(1)} %collective-permute-done.9.k_ref, bf16[512,256]{1,0:T(8,128)(2,1)S(1)} %collective-permute-done.10.v_ref, ...), custom_call_target="tpu_custom_call" | custom-call | flops 1 | bytes 1 | tf_op jit(solution)/shard_map/finish_b/pallas_call | solution.py:139
  115.5 4.6 %collective-permute-start.14 = (bf16[512,256]{1,0:T(8,128)(2,1)S(1)}, bf16[512,256]{1,0:T(8,128)(2,1)S(1)}, u32[]{:S(2)}, u32[]{:S(2)}) collective-permute-start(bf16[512,256]{1,0:T(8,128)(2,1)S(1)} %finish_b.1.refs_0_), channel_id=1, source_target_pairs={{0,1},{1,2},{2,3},{3,4},{4,5},{5,6},{6,7},{7,0},{8,9},{9,10},{10,1... | collective-permute-start | bytes 786440 | tf_op jit(solution)/shard_map/ppermute | solution.py:260
  120.1 1.9 %collective-permute-start.12 = (bf16[512,256]{1,0:T(8,128)(2,1)S(1)}, bf16[512,256]{1,0:T(8,128)(2,1)}, u32[]{:S(2)}, u32[]{:S(2)}) collective-permute-start(bf16[512,256]{1,0:T(8,128)(2,1)S(1)} %finish_b.1.refs_0_), channel_id=1, source_target_pairs={{0,7},{1,0},{2,1},{3,2},{4,3},{5,4},{6,5},{7,6},{8,15},{9,8},{10,9... | collective-permute-start | bytes 786440 | tf_op jit(solution)/shard_map/ppermute | solution.py:260
  122.0 4.6 %collective-permute-done.14.refs_2_ = bf16[512,256]{1,0:T(8,128)(2,1)S(1)} collective-permute-done((bf16[512,256]{1,0:T(8,128)(2,1)S(1)}, bf16[512,256]{1,0:T(8,128)(2,1)S(1)}, u32[]{:S(2)}, u32[]{:S(2)}) %collective-permute-start.14) | collective-permute-done | bytes 262176 | tf_op jit(solution)/shard_map/ppermute | solution.py:260
  126.6 5.6 %collective-permute-start.16 = (bf16[512,256]{1,0:T(8,128)(2,1)S(1)}, bf16[512,256]{1,0:T(8,128)(2,1)}, u32[]{:S(2)}, u32[]{:S(2)}) collective-permute-start(bf16[512,256]{1,0:T(8,128)(2,1)S(1)} %collective-permute-done.14.refs_2_), channel_id=1, source_target_pairs={{0,1},{1,2},{2,3},{3,4},{4,5},{5,6},{6,7},{7,0},{8,9},{9,10},{10,1... | collective-permute-start | bytes 786440 | tf_op jit(solution)/shard_map/ppermute | solution.py:260
  134.8 3.2 %collective-permute-done.16.refs_1_ = bf16[512,256]{1,0:T(8,128)(2,1)} collective-permute-done((bf16[512,256]{1,0:T(8,128)(2,1)S(1)}, bf16[512,256]{1,0:T(8,128)(2,1)}, u32[]{:S(2)}, u32[]{:S(2)}) %collective-permute-start.16) | collective-permute-done | bytes 262176 | tf_op jit(solution)/shard_map/ppermute | solution.py:260
  138.0 5.7 %collective-permute-start.17 = (bf16[512,256]{1,0:T(8,128)(2,1)}, bf16[512,256]{1,0:T(8,128)(2,1)}, u32[]{:S(2)}, u32[]{:S(2)}) collective-permute-start(bf16[512,256]{1,0:T(8,128)(2,1)} %collective-permute-done.16.refs_1_), channel_id=1, source_target_pairs={{0,1},{1,2},{2,3},{3,4},{4,5},{5,6},{6,7},{7,0},{8,9},{9,10},{10,1... | collective-permute-start | bytes 786440 | tf_op jit(solution)/shard_map/ppermute | solution.py:260
  145.0 2.5 %project_1.1.refs_0_ = f32[512,384]{1,0:T(8,128)S(1)} custom-call(s32[1]{0:T(128)} %bitcast.group_ref, f32[512,384]{1,0:T(8,128)S(1)} %project_0.1.refs_0_, bf16[8,512,128]{2,1,0:T(8,128)(2,1)} %all-to-all-done.1.refs_1_, bf16[512,256]{1,0:T(8,128)(2,1)S(1)} %copy-done.3, bf16[512,256]{1,0:T(8,128)(2,1)} %collective-permute-done.12.refs_3_, ...), custom_call_target="tpu_custom_call" | custom-call | flops 150994944 | bytes 4194304 | tf_op jit(solution)/shard_map/project_1/pallas_call | solution.py:228
  147.5 1.9 %collective-permute-start.15 = (bf16[512,256]{1,0:T(8,128)(2,1)}, bf16[512,256]{1,0:T(8,128)(2,1)S(1)}, u32[]{:S(2)}, u32[]{:S(2)}) collective-permute-start(bf16[512,256]{1,0:T(8,128)(2,1)} %collective-permute-done.13.refs_2_), channel_id=1, source_target_pairs={{0,7},{1,0},{2,1},{3,2},{4,3},{5,4},{6,5},{7,6},{8,15},{9,8},{10,9... | collective-permute-start | bytes 786440 | tf_op jit(solution)/shard_map/ppermute | solution.py:260
  150.4 5.1 %collective-permute-start.18 = (bf16[256,256]{1,0:T(8,128)(2,1)S(1)}, bf16[256,256]{1,0:T(8,128)(2,1)S(1)}, u32[]{:S(2)}, u32[]{:S(2)}) collective-permute-start(bf16[256,256]{1,0:T(8,128)(2,1)S(1)} %slice.16), channel_id=1, source_target_pairs={{0,1},{1,2},{2,3},{3,4},{4,5},{5,6},{6,7},{7,0},{8,9},{9,10},{10,1... | collective-permute-start | bytes 393224 | tf_op jit(solution)/shard_map/ppermute | solution.py:260
  157.2 1.9 %collective-permute-start.19 = (bf16[256,256]{1,0:T(8,128)(2,1)S(1)}, bf16[256,256]{1,0:T(8,128)(2,1)S(1)}, u32[]{:S(2)}, u32[]{:S(2)}) collective-permute-start(bf16[256,256]{1,0:T(8,128)(2,1)S(1)} %slice.15), channel_id=1, source_target_pairs={{0,7},{1,0},{2,1},{3,2},{4,3},{5,4},{6,5},{7,6},{8,15},{9,8},{10,9... | collective-permute-start | bytes 393224 | tf_op jit(solution)/shard_map/ppermute | solution.py:260
  160.5 4.7 %collective-permute-done.19.refs_2_ = bf16[256,256]{1,0:T(8,128)(2,1)S(1)} collective-permute-done((bf16[256,256]{1,0:T(8,128)(2,1)S(1)}, bf16[256,256]{1,0:T(8,128)(2,1)S(1)}, u32[]{:S(2)}, u32[]{:S(2)}) %collective-permute-start.19) | collective-permute-done | bytes 131104 | tf_op jit(solution)/shard_map/ppermute | solution.py:260
  (50 shorter events, 29.5 us)
Async XLA Ops:
  0.0 1.0 copy-start
  1.0 1.0 copy-start.1
  3.0 22.0 %collective-permute-start = (bf16[2,512,128]{2,1,0:T(8,128)(2,1)}, bf16[2,512,128]{2,1,0:T(8,128)(2,1)}, u32[]{:S(2)}, u32[]{:S(2)}) collective-permute-start(bf16[2,512,128]{2,1,0:T(8,128)(2,1)} %get-tuple-element.28.refs_2_.refs_3_), channel_id=1, source_target_pairs={{0,16},{8,24},{16,32},{24,40},{32,48},{40,56},{48,64},{56,72},{64,... | collective-permute-start | bytes 786440 | tf_op jit(solution)/shard_map/ppermute | solution.py:260
  7.2 33.7 %collective-permute-start.2 = (bf16[2,512,256]{2,1,0:T(8,128)(2,1)}, bf16[2,512,256]{2,1,0:T(8,128)(2,1)S(1)}, u32[]{:S(2)}, u32[]{:S(2)}) collective-permute-start(bf16[2,512,256]{2,1,0:T(8,128)(2,1)} %get-tuple-element.29.refs_2_.refs_3_), channel_id=1, source_target_pairs={{0,16},{8,24},{16,32},{24,40},{32,48},{40,56},{48,64},{56,72},{64,... | collective-permute-start | bytes 1572872 | tf_op jit(solution)/shard_map/ppermute | solution.py:260
  11.5 33.3 %collective-permute-start.6 = (bf16[512,384]{1,0:T(8,128)(2,1)}, bf16[512,384]{1,0:T(8,128)(2,1)S(1)}, u32[]{:S(2)}, u32[]{:S(2)}) collective-permute-start(bf16[512,384]{1,0:T(8,128)(2,1)} %q_ref.3), channel_id=1, source_target_pairs={{0,8},{8,0},{16,24},{24,16},{32,40},{40,32},{48,56},{56,48},{64,72... | collective-permute-start | bytes 1179656 | tf_op jit(solution)/shard_map/ppermute | solution.py:260
  16.3 28.5 %copy-start.4 = (s32[96]{0:T(128)S(1)}, s32[96]{0:T(128)}, u32[]{:S(2)}) copy-start(s32[96]{0:T(128)} %span_ref.13) | copy-start | bytes 1156
  16.3 28.6 %copy-start.5 = (s32[96]{0:T(128)S(1)}, s32[96]{0:T(128)}, u32[]{:S(2)}) copy-start(s32[96]{0:T(128)} %counts_ref.13) | copy-start | bytes 1156
  16.3 59.2 %all-to-all-start = ((bf16[8,384,384]{2,1,0:T(8,128)(2,1)}), bf16[8,384,384]{2,1,0:T(8,128)(2,1)S(1)}, u32[]{:S(2)}, u32[]{:S(2)}) async-start(bf16[8,384,384]{2,1,0:T(8,128)(2,1)} %column_blocks.1), calls=%async_computation | async-start | bytes 4718592 | tf_op jit(solution)/shard_map/all_to_all | solution.py:271
  24.9 16.0 %collective-permute-start.1 = (bf16[2,512,128]{2,1,0:T(8,128)(2,1)}, bf16[2,512,128]{2,1,0:T(8,128)(2,1)}, u32[]{:S(2)}, u32[]{:S(2)}) collective-permute-start(bf16[2,512,128]{2,1,0:T(8,128)(2,1)} %collective-permute-done.refs_4_.refs_5_), channel_id=1, source_target_pairs={{0,16},{8,24},{16,32},{24,40},{32,48},{40,56},{48,64},{56,72},{64,... | collective-permute-start | bytes 786440 | tf_op jit(solution)/shard_map/ppermute | solution.py:260
  41.0 13.4 %collective-permute-start.4 = (bf16[2,512,128]{2,1,0:T(8,128)(2,1)}, bf16[2,512,128]{2,1,0:T(8,128)(2,1)S(1)}, u32[]{:S(2)}, u32[]{:S(2)}) collective-permute-start(bf16[2,512,128]{2,1,0:T(8,128)(2,1)} %collective-permute-done.1.refs_6_.refs_7_), channel_id=1, source_target_pairs={{0,16},{8,24},{16,32},{24,40},{32,48},{40,56},{48,64},{56,72},{64,... | collective-permute-start | bytes 786440 | tf_op jit(solution)/shard_map/ppermute | solution.py:260
  42.9 24.0 %collective-permute-start.3 = (bf16[2,512,256]{2,1,0:T(8,128)(2,1)S(1)}, bf16[2,512,256]{2,1,0:T(8,128)(2,1)}, u32[]{:S(2)}, u32[]{:S(2)}) collective-permute-start(bf16[2,512,256]{2,1,0:T(8,128)(2,1)S(1)} %collective-permute-done.2.refs_4_.refs_5_), channel_id=1, source_target_pairs={{0,16},{8,24},{16,32},{24,40},{32,48},{40,56},{48,64},{56,72},{64,... | collective-permute-start | bytes 1572872 | tf_op jit(solution)/shard_map/ppermute | solution.py:260
  51.1 1.0 copy-start.6
  52.1 1.0 copy-start.8
  54.4 12.5 %collective-permute-start.5 = (bf16[2,512,128]{2,1,0:T(8,128)(2,1)S(1)}, bf16[2,512,128]{2,1,0:T(8,128)(2,1)S(1)}, u32[]{:S(2)}, u32[]{:S(2)}) collective-permute-start(bf16[2,512,128]{2,1,0:T(8,128)(2,1)S(1)} %collective-permute-done.4.refs_8_.refs_9_), channel_id=1, source_target_pairs={{8,16},{24,32},{40,48},{56,64},{72,80},{88,96},{104,112},{120,128}... | collective-permute-start | bytes 786440 | tf_op jit(solution)/shard_map/ppermute | solution.py:260
  66.9 3.8 %collective-permute-start.8 = (f32[1,512,256]{2,1,0:T(8,128)S(1)}, f32[1,512,256]{2,1,0:T(8,128)S(1)}, u32[]{:S(2)}, u32[]{:S(2)}) collective-permute-start(f32[1,512,256]{2,1,0:T(8,128)S(1)} %get-tuple-element.43), channel_id=1, source_target_pairs={{0,8},{8,0},{16,24},{24,16},{32,40},{40,32},{48,56},{56,48},{64,72... | collective-permute-start | bytes 1572872 | tf_op jit(solution)/shard_map/ppermute | solution.py:260
  68.9 24.1 %collective-permute-start.7 = (bf16[2,512,256]{2,1,0:T(8,128)(2,1)}, bf16[2,512,256]{2,1,0:T(8,128)(2,1)S(1)}, u32[]{:S(2)}, u32[]{:S(2)}) collective-permute-start(bf16[2,512,256]{2,1,0:T(8,128)(2,1)} %collective-permute-done.3.refs_2_.refs_3_), channel_id=1, source_target_pairs={{0,16},{8,24},{16,32},{24,40},{32,48},{40,56},{48,64},{56,72},{64,... | collective-permute-start | bytes 1572872 | tf_op jit(solution)/shard_map/ppermute | solution.py:260
  76.6 67.4 %all-to-all-start.1 = ((bf16[8,512,128]{2,1,0:T(8,128)(2,1)}), bf16[8,512,128]{2,1,0:T(8,128)(2,1)}, u32[]{:S(2)}, u32[]{:S(2)}) async-start(bf16[8,512,128]{2,1,0:T(8,128)(2,1)} %broadcast_in_dim.2), calls=%async_computation.1 | async-start | bytes 2097152 | tf_op jit(solution)/shard_map/all_to_all | solution.py:285
  86.5 1.2 copy-start.7
  87.8 1.2 copy-start.9
  95.6 17.4 %collective-permute-start.11 = (f32[2,512,256]{2,1,0:T(8,128)S(1)}, f32[2,512,256]{2,1,0:T(8,128)S(1)}, u32[]{:S(2)}, u32[]{:S(2)}) collective-permute-start(f32[2,512,256]{2,1,0:T(8,128)S(1)} %attend_b3_other.1), channel_id=1, source_target_pairs={{0,8},{8,0},{16,24},{24,16},{32,40},{40,32},{48,56},{56,48},{64,72... | collective-permute-start | bytes 3145736 | tf_op jit(solution)/shard_map/ppermute | solution.py:260
  97.6 12.6 %collective-permute-start.10 = (bf16[512,256]{1,0:T(8,128)(2,1)S(1)}, bf16[512,256]{1,0:T(8,128)(2,1)S(1)}, u32[]{:S(2)}, u32[]{:S(2)}) collective-permute-start(bf16[512,256]{1,0:T(8,128)(2,1)S(1)} %get-tuple-element.51), channel_id=1, source_target_pairs={{8,16},{24,32},{40,48},{56,64},{72,80},{88,96},{104,112},{120,128}... | collective-permute-start | bytes 786440 | tf_op jit(solution)/shard_map/ppermute | solution.py:260
  98.9 14.1 %collective-permute-start.9 = (bf16[512,256]{1,0:T(8,128)(2,1)S(1)}, bf16[512,256]{1,0:T(8,128)(2,1)S(1)}, u32[]{:S(2)}, u32[]{:S(2)}) collective-permute-start(bf16[512,256]{1,0:T(8,128)(2,1)S(1)} %get-tuple-element.52), channel_id=1, source_target_pairs={{8,16},{24,32},{40,48},{56,64},{72,80},{88,96},{104,112},{120,128}... | collective-permute-start | bytes 786440 | tf_op jit(solution)/shard_map/ppermute | solution.py:260
  115.5 11.1 %collective-permute-start.14 = (bf16[512,256]{1,0:T(8,128)(2,1)S(1)}, bf16[512,256]{1,0:T(8,128)(2,1)S(1)}, u32[]{:S(2)}, u32[]{:S(2)}) collective-permute-start(bf16[512,256]{1,0:T(8,128)(2,1)S(1)} %finish_b.1.refs_0_), channel_id=1, source_target_pairs={{0,1},{1,2},{2,3},{3,4},{4,5},{5,6},{6,7},{7,0},{8,9},{9,10},{10,1... | collective-permute-start | bytes 786440 | tf_op jit(solution)/shard_map/ppermute | solution.py:260
  120.1 12.8 %collective-permute-start.12 = (bf16[512,256]{1,0:T(8,128)(2,1)S(1)}, bf16[512,256]{1,0:T(8,128)(2,1)}, u32[]{:S(2)}, u32[]{:S(2)}) collective-permute-start(bf16[512,256]{1,0:T(8,128)(2,1)S(1)} %finish_b.1.refs_0_), channel_id=1, source_target_pairs={{0,7},{1,0},{2,1},{3,2},{4,3},{5,4},{6,5},{7,6},{8,15},{9,8},{10,9... | collective-permute-start | bytes 786440 | tf_op jit(solution)/shard_map/ppermute | solution.py:260
  126.6 11.4 %collective-permute-start.16 = (bf16[512,256]{1,0:T(8,128)(2,1)S(1)}, bf16[512,256]{1,0:T(8,128)(2,1)}, u32[]{:S(2)}, u32[]{:S(2)}) collective-permute-start(bf16[512,256]{1,0:T(8,128)(2,1)S(1)} %collective-permute-done.14.refs_2_), channel_id=1, source_target_pairs={{0,1},{1,2},{2,3},{3,4},{4,5},{5,6},{6,7},{7,0},{8,9},{9,10},{10,1... | collective-permute-start | bytes 786440 | tf_op jit(solution)/shard_map/ppermute | solution.py:260
  132.2 0.7 copy-start.2
  132.9 14.6 %collective-permute-start.13 = (bf16[512,256]{1,0:T(8,128)(2,1)}, bf16[512,256]{1,0:T(8,128)(2,1)}, u32[]{:S(2)}, u32[]{:S(2)}) collective-permute-start(bf16[512,256]{1,0:T(8,128)(2,1)} %collective-permute-done.12.refs_3_), channel_id=1, source_target_pairs={{0,7},{1,0},{2,1},{3,2},{4,3},{5,4},{6,5},{7,6},{8,15},{9,8},{10,9... | collective-permute-start | bytes 786440 | tf_op jit(solution)/shard_map/ppermute | solution.py:260
  138.0 11.4 %collective-permute-start.17 = (bf16[512,256]{1,0:T(8,128)(2,1)}, bf16[512,256]{1,0:T(8,128)(2,1)}, u32[]{:S(2)}, u32[]{:S(2)}) collective-permute-start(bf16[512,256]{1,0:T(8,128)(2,1)} %collective-permute-done.16.refs_1_), channel_id=1, source_target_pairs={{0,1},{1,2},{2,3},{3,4},{4,5},{5,6},{6,7},{7,0},{8,9},{9,10},{10,1... | collective-permute-start | bytes 786440 | tf_op jit(solution)/shard_map/ppermute | solution.py:260
  144.0 1.0 copy-start.3
  147.5 9.7 %collective-permute-start.15 = (bf16[512,256]{1,0:T(8,128)(2,1)}, bf16[512,256]{1,0:T(8,128)(2,1)S(1)}, u32[]{:S(2)}, u32[]{:S(2)}) collective-permute-start(bf16[512,256]{1,0:T(8,128)(2,1)} %collective-permute-done.13.refs_2_), channel_id=1, source_target_pairs={{0,7},{1,0},{2,1},{3,2},{4,3},{5,4},{6,5},{7,6},{8,15},{9,8},{10,9... | collective-permute-start | bytes 786440 | tf_op jit(solution)/shard_map/ppermute | solution.py:260
  150.4 10.2 %collective-permute-start.18 = (bf16[256,256]{1,0:T(8,128)(2,1)S(1)}, bf16[256,256]{1,0:T(8,128)(2,1)S(1)}, u32[]{:S(2)}, u32[]{:S(2)}) collective-permute-start(bf16[256,256]{1,0:T(8,128)(2,1)S(1)} %slice.16), channel_id=1, source_target_pairs={{0,1},{1,2},{2,3},{3,4},{4,5},{5,6},{6,7},{7,0},{8,9},{9,10},{10,1... | collective-permute-start | bytes 393224 | tf_op jit(solution)/shard_map/ppermute | solution.py:260
  157.2 8.1 %collective-permute-start.19 = (bf16[256,256]{1,0:T(8,128)(2,1)S(1)}, bf16[256,256]{1,0:T(8,128)(2,1)S(1)}, u32[]{:S(2)}, u32[]{:S(2)}) collective-permute-start(bf16[256,256]{1,0:T(8,128)(2,1)S(1)} %slice.15), channel_id=1, source_target_pairs={{0,7},{1,0},{2,1},{3,2},{4,3},{5,4},{6,5},{7,6},{8,15},{9,8},{10,9... | collective-permute-start | bytes 393224 | tf_op jit(solution)/shard_map/ppermute | solution.py:260

commit v5 on v3

--- a/solution.py
+++ b/solution.py
@@ -50,14 +50,19 @@
     return jnp.where(seen, counts_ref[jnp.maximum(source, 0)], 0)
 
 
-def in_hbm(array):
-    return pltpu.with_memory_space_constraint(array, pltpu.HBM)
-
-
 def _unpack(packed, acc, top):
     acc[0, :, :HD] = packed[0, :, :HD]
     acc[0, :, HD:] = jnp.broadcast_to(packed[0, :, 2 * HD - 1 :], (acc.shape[1], HD))
     top[0] = jnp.broadcast_to(packed[0, :, HD : HD + 1], (acc.shape[1], HD))
+
+
+def _join(packed, acc, top):
+    new_top = jnp.maximum(top[0], packed[0, :, HD : HD + 1])
+    own_part = jnp.exp2((top[0] - new_top) * EXP2_SCALE)
+    other_part = jnp.exp2((packed[0, :, HD : HD + 1] - new_top) * EXP2_SCALE)
+    acc[0, :, :HD] = acc[0, :, :HD] * own_part + packed[0, :, :HD] * other_part
+    acc[0, :, HD:] = acc[0, :, HD:] * own_part + packed[0, :, 2 * HD - 1 :] * other_part
+    top[0] = new_top
 
 
 def _attention_body(sides, hops, first):
@@ -95,7 +100,7 @@
     return column, packed, scratch
 
 
-def attention_call(scalars, queries, sources, sides, hops, states, name, cost):
+def attention_call(scalars, queries, sources, sides, hops, states, name):
     per_frame, width = queries[0].shape
     heads = width // HD
     column, packed, scratch = _specs(per_frame)
@@ -110,28 +115,19 @@
             out_specs=[packed] * len(sides),
             scratch_shapes=scratch * len(sides),
         ),
-        cost_estimate=cost,
+        cost_estimate=LONG,
         compiler_params=pltpu.CompilerParams(vmem_limit_bytes=SMALL_VMEM),
         name=name,
     )(*scalars, *operands)
 
 
-def _finish_body(frame_ref, span_ref, counts_ref, q_ref, k_ref, v_ref, own, other, upper_ref, lower_ref, acc, top):
+def _finish_body(frame_ref, span_ref, counts_ref, q_ref, k_ref, v_ref, own, other, out_ref, acc, top):
     _unpack(own, acc, top)
     limit = _visible(frame_ref[0], 0, WIN - 1, span_ref, counts_ref)
     limit = jnp.where(frame_ref[0] % 2 == 0, limit, 0)
     _attend(limit, q_ref, k_ref, v_ref, acc, top)
-    own_top, other_top = top[0], other[0, :, HD : HD + 1]
-    own_total, other_total = acc[0, :, HD:], other[0, :, 2 * HD - 1 :]
-    both_top = jnp.maximum(own_top, other_top)
-    own_part = jnp.exp2((own_top - both_top) * EXP2_SCALE)
-    other_part = jnp.exp2((other_top - both_top) * EXP2_SCALE)
-    total = own_total * own_part + other_total * other_part
-    mixed = acc[0, :, :HD] * own_part + other[0, :, :HD] * other_part
-    mixed = (mixed / total).astype(jnp.bfloat16)
-    half = upper_ref.shape[0]
-    upper_ref[...] = mixed[:half]
-    lower_ref[...] = mixed[half:]
+    _join(other, acc, top)
+    out_ref[...] = (acc[0, :, :HD] / acc[0, :, HD:]).astype(jnp.bfloat16)
 
 
 def finish_call(scalars, queries, keys, values, own, other, name):
@@ -139,12 +135,12 @@
     column, packed, scratch = _specs(per_frame)
     return pl.pallas_call(
         _finish_body,
-        out_shape=[jax.ShapeDtypeStruct((per_frame // 2, width), jnp.bfloat16)] * 2,
+        out_shape=jax.ShapeDtypeStruct((per_frame, width), jnp.bfloat16),
         grid_spec=pltpu.PrefetchScalarGridSpec(
             num_scalar_prefetch=3,
             grid=(width // HD,),
             in_specs=[column, column, column, packed, packed],
-            out_specs=[pl.BlockSpec((per_frame // 2, HD), lambda h, *_: (0, h))] * 2,
+            out_specs=column,
             scratch_shapes=scratch,
         ),
         cost_estimate=BRIEF,
@@ -184,32 +180,32 @@
         groups, half = w_ref.shape[0], out_ref.shape[0] // 2
         for part in (0, 1):
             rows = pl.ds(part * half, half)
-            total = refs[0][rows, :] if has_base else None
+            total = refs[0][rows, :] if has_base else jnp.zeros((half, out_ref.shape[1]), jnp.float32)
             for (place, offset), ref in zip(places, refs[has_base:-2], strict=True):
-                if place == part:
+                if place in (part, None):
                     source = lax.rem(group_ref[0] + offset, groups)
-                    product = jnp.dot(ref[...], w_ref[source], preferred_element_type=jnp.float32)
-                    total = product if total is None else total + product
+                    piece = ref[rows, :] if place is None else ref[...]
+                    total += jnp.dot(piece, w_ref[source], preferred_element_type=jnp.float32)
             out_ref[rows, :] = total.astype(out_ref.dtype)
 
     return body
 
 
 def project_call(group, weight, base, pieces, places, dtype, name):
-    groups, height, columns = weight.shape
-    half = pieces[0].shape[0]
+    groups, _, columns = weight.shape
+    per_frame = pieces[0].shape[0] * (1 if places[0][0] is None else 2)
     operands = ([] if base is None else [base]) + list(pieces) + [weight]
     return pl.pallas_call(
         _project_body(places, base is not None),
-        out_shape=jax.ShapeDtypeStruct((2 * half, columns), dtype),
+        out_shape=jax.ShapeDtypeStruct((per_frame, columns), dtype),
         grid_spec=pltpu.PrefetchScalarGridSpec(
             num_scalar_prefetch=1,
             grid=(1,),
             in_specs=[pl.BlockSpec(x.shape, lambda i, g, n=x.ndim: (0,) * n) for x in operands],
-            out_specs=pl.BlockSpec((2 * half, columns), lambda i, g: (0, 0)),
+            out_specs=pl.BlockSpec((per_frame, columns), lambda i, g: (0, 0)),
         ),
         cost_estimate=pl.CostEstimate(
-            flops=2 * len(pieces) * half * height * columns, transcendentals=0, bytes_accessed=4 << 20
+            flops=len(pieces) * per_frame * weight.shape[1] * columns, transcendentals=0, bytes_accessed=4 << 20
         ),
         compiler_params=pltpu.CompilerParams(vmem_limit_bytes=LARGE_VMEM),
         name=name,
@@ -233,43 +229,44 @@
     def send(block, route, axis="frame"):
         return lax.ppermute(block, axis, route)
 
-    def attend(sources, sides, hops, states, name, cost=BRIEF):
+    def attend(sources, sides, hops, states, name):
         both = (in_hbm(queries), q_other)
         return attention_call(
-            scalars, [both[side] for side in sides], sources, sides, hops, states, name, cost
+            scalars, [both[side] for side in sides], sources, sides, hops, states, name
         )
 
     k1, v1 = send(keys, by_chip), send(values, by_chip)
     q_other = send(queries, swap)
-    k2, v2 = send(k1, by_chip), send(v1, by_chip)
-    near = [(in_hbm(keys), in_hbm(values)), (k1, v1)]
-    own, other = attend(near, (0, 1), (0, 1), None, "attend_01", LONG)
     blocks = column_blocks(out_weight, groups)
     weight = lax.all_to_all(blocks, "head", split_axis=0, concat_axis=0, tiled=True)
+    parts = attend([(in_hbm(keys), in_hbm(values))], (0, 1), (0,), None, "attend_0")
+    k1, parts = after((k1, parts))
+    k2, v2 = send(k1, by_chip), send(v1, by_chip)
+    parts = attend([(k1, v1)], (0, 1), (1,), parts, "attend_1")
+    k2, parts = after((k2, parts))
     k3, v3 = send(k2, by_chip), send(v2, by_chip)
-    own, other = attend([(k2, v2)], (0, 1), (2,), [own, other], "attend_2", LONG)
+    own, other = attend([(k2, v2)], (0, 1), (2,), parts, "attend_2")
     k3, v3, own, other = after((k3, v3, own, other))
     (other,) = attend([(k3, v3)], (1,), (3,), [other], "attend_3_other")
     from_other = send(other, swap)
     k4, v4 = send(k3, to_even), send(v3, to_even)
-    (own,) = attend([(k3, v3)], (0,), (3,), [own], "attend_3_own", LONG)
+    (own,) = attend([(k3, v3)], (0,), (3,), [own], "attend_3_own")
     attended = finish_call(scalars, in_hbm(queries), k4, v4, own, from_other, "finish")
 
     def project(base, pieces, places, dtype, name):
         return project_call(group, weight, base, pieces, places, dtype, name)
 
-    up, down = list(attended), list(attended)
-    held, places, total = list(attended), ((0, 0), (1, 0)), None
+    half = per_frame // 2
+    up, down = attended, attended
+    held, places, total = [attended], [(None, 0)], None
     for step in (1, 2, 3):
-        up = [send(block, upward, "head") for block in up]
-        down = [send(block, downward, "head") for block in down]
+        up, down = send(up, upward, "head"), send(down, downward, "head")
         total = project(total, held, places, jnp.float32, f"project_{step - 1}")
-        held = up + down
-        places = ((0, groups - step), (1, groups - step), (0, step), (1, step))
-        up[1], down[1], total = after((up[1], down[1], total))
-    far = [send(up[0], upward, "head"), send(down[1], downward, "head")]
+        held, places = [up, down], [(None, groups - step), (None, step)]
+        down, total = after((down, total))
+    far = [send(up[:half], upward, "head"), send(down[half:], downward, "head")]
     total = project(total, held, places, jnp.float32, "project_3")
-    return project(total, far, ((0, 4), (1, 4)), jnp.bfloat16, "project_4")
+    return project(total, far, [(0, 4), (1, 4)], jnp.bfloat16, "project_4")
 
 
 def solution(mesh):

time: 143 us -> 142 us (level); the launches traced: 142 us -> 143 us
  starting transfers between devices: 77.1 us -> 60.9 us
  waiting for transfers between devices: 38.8 us -> 51.6 us
  Pallas kernels: 25.5 us -> 29.8 us
    ppermute x24 -> x18, starting transfers between devices: 69.6 us -> 53.5 us  [send(): return lax.ppermute(block, axis, route)]
    ppermute x24 -> x18, waiting for transfers between devices: 38.8 us -> 51.6 us  [send(): return lax.ppermute(block, axis, route)]
    pallas_call x4 -> x5, Pallas kernels: 14.4 us -> 19.3 us  [attention_call(): pl.pallas_call(_attention_body(sides, hops, states is None), out_shape=[j...]
  transfers between devices with their start and end apart: 25 -> 19, of which waited for: 8 -> 12; matrix products, arithmetic and copies ran while one was open for 0% -> 0% of each run, Pallas kernels for 17% -> 20%
where the time goes in v5:
time: 142 us; the launch traced here: 143 us
  starting transfers between devices  60.9 us (43%)
  waiting for transfers between devices  51.6 us (36%)
  Pallas kernels  29.8 us (21%)
    ppermute x18, starting transfers between devices, send(): return lax.ppermute(block, axis, route)  53.5 us
    ppermute x18, waiting for transfers between devices, send(): return lax.ppermute(block, axis, route)  51.6 us
    pallas_call x5, Pallas kernels, attention_call(): pl.pallas_call(_attention_body(sides, hops, states is None), out_shape=[j...  19.3 us
    all_to_all x1, starting transfers between devices, on_device(): lax.all_to_all(blocks, 'head', split_axis=0, concat_axis=0, tiled=True)  7.45 us
    pallas_call x5, Pallas kernels, project_call(): pl.pallas_call(_project_body(places, base is not None), out_shape=jax.Sha...  4.45 us
    pallas_call x1, Pallas kernels, finish_call(): pl.pallas_call(_finish_body, out_shape=jax.ShapeDtypeStruct((per_frame, w...  3.28 us
  transfers between devices with their start and end apart: 19, of which 12 were waited for; matrix products, arithmetic and copies ran while one was open for 0% of the time, Pallas kernels for 20%

profile of v5, /device:TPU:30, one launch (start us, length us, event | category | flops | bytes accessed | tf_op | source)
XLA Modules:
  0.0 142.7 jit_solution(8957208737353112525)
XLA Ops:
  0.0 1.9 %collective-permute-start.1 = (bf16[512,384]{1,0:T(8,128)(2,1)}, bf16[512,384]{1,0:T(8,128)(2,1)S(1)}, u32[]{:S(2)}, u32[]{:S(2)}) collective-permute-start(bf16[512,384]{1,0:T(8,128)(2,1)} %q_ref.1), channel_id=1, source_target_pairs={{0,8},{8,0},{16,24},{24,16},{32,40},{40,32},{48,56},{56,48},{64,72... | collective-permute-start | bytes 1179656 | tf_op jit(solution)/shard_map/ppermute | solution.py:230
  1.9 4.3 %collective-permute-start = (bf16[512,384]{1,0:T(8,128)(2,1)}, bf16[512,384]{1,0:T(8,128)(2,1)S(1)}, u32[]{:S(2)}, u32[]{:S(2)}) collective-permute-start(bf16[512,384]{1,0:T(8,128)(2,1)} %refs_2_.1), channel_id=1, source_target_pairs={{0,16},{8,24},{16,32},{24,40},{32,48},{40,56},{48,64},{56,72},{64,... | collective-permute-start | bytes 1179656 | tf_op jit(solution)/shard_map/ppermute | solution.py:230
  6.2 4.3 %collective-permute-start.3 = (bf16[512,384]{1,0:T(8,128)(2,1)}, bf16[512,384]{1,0:T(8,128)(2,1)S(1)}, u32[]{:S(2)}, u32[]{:S(2)}) collective-permute-start(bf16[512,384]{1,0:T(8,128)(2,1)} %refs_3_.1), channel_id=1, source_target_pairs={{0,16},{8,24},{16,32},{24,40},{32,48},{40,56},{48,64},{56,72},{64,... | collective-permute-start | bytes 1179656 | tf_op jit(solution)/shard_map/ppermute | solution.py:230
  10.5 2.8 %column_blocks.1 = bf16[8,384,384]{2,1,0:T(8,128)(2,1)} custom-call(bf16[384,3072]{1,0:T(8,128)(2,1)} %w_ref.1), custom_call_target="tpu_custom_call" | custom-call | flops 1 | bytes 1 | tf_op jit(solution)/shard_map/column_blocks/pallas_call | solution.py:165
  13.3 7.5 %all-to-all-start = ((bf16[8,384,384]{2,1,0:T(8,128)(2,1)}), bf16[8,384,384]{2,1,0:T(8,128)(2,1)S(1)}, u32[]{:S(2)}, u32[]{:S(2)}) async-start(bf16[8,384,384]{2,1,0:T(8,128)(2,1)} %column_blocks.1), calls=%async_computation | async-start | bytes 4718592 | tf_op jit(solution)/shard_map/all_to_all | solution.py:241
  20.7 6.5 %attend_0.1 = (f32[3,512,256]{2,1,0:T(8,128)S(1)}, f32[3,512,256]{2,1,0:T(8,128)S(1)}) custom-call(s32[1]{0:T(128)} %bitcast.1.frame_ref, s32[96]{0:T(128)S(1)} %copy-done, s32[96]{0:T(128)S(1)} %copy-done.1, bf16[512,384]{1,0:T(8,128)(2,1)} %q_ref.1, bf16[512,384]{1,0:T(8,128)(2,1)S(1)} %collective-permute-done.1.refs_1_.refs_0_, bf16[512,384]{1,0:T(8,128)(2,1)} %refs_2_.1, ...), custom_call_target="tpu_custom_call" | custom-call | flops 17179869184 | bytes 1 | tf_op jit(solution)/shard_map/attend_0/pallas_call | solution.py:108
  27.2 4.3 %collective-permute-start.2 = (bf16[512,384]{1,0:T(8,128)(2,1)S(1)}, bf16[512,384]{1,0:T(8,128)(2,1)S(1)}, u32[]{:S(2)}, u32[]{:S(2)}) collective-permute-start(bf16[512,384]{1,0:T(8,128)(2,1)S(1)} %collective-permute-done.refs_2_), channel_id=1, source_target_pairs={{0,16},{8,24},{16,32},{24,40},{32,48},{40,56},{48,64},{56,72},{64,... | collective-permute-start | bytes 1179656 | tf_op jit(solution)/shard_map/ppermute | solution.py:230
  31.5 3.7 %collective-permute-done.3.refs_3_ = bf16[512,384]{1,0:T(8,128)(2,1)S(1)} collective-permute-done((bf16[512,384]{1,0:T(8,128)(2,1)}, bf16[512,384]{1,0:T(8,128)(2,1)S(1)}, u32[]{:S(2)}, u32[]{:S(2)}) %collective-permute-start.3) | collective-permute-done | bytes 393248 | tf_op jit(solution)/shard_map/ppermute | solution.py:230
  35.2 1.9 %collective-permute-start.5 = (bf16[512,384]{1,0:T(8,128)(2,1)S(1)}, bf16[512,384]{1,0:T(8,128)(2,1)S(1)}, u32[]{:S(2)}, u32[]{:S(2)}) collective-permute-start(bf16[512,384]{1,0:T(8,128)(2,1)S(1)} %collective-permute-done.3.refs_3_), channel_id=1, source_target_pairs={{0,16},{8,24},{16,32},{24,40},{32,48},{40,56},{48,64},{56,72},{64,... | collective-permute-start | bytes 1179656 | tf_op jit(solution)/shard_map/ppermute | solution.py:230
  37.1 5.1 %attend_1.1 = (f32[3,512,256]{2,1,0:T(8,128)S(1)}, f32[3,512,256]{2,1,0:T(8,128)S(1)}) custom-call(s32[1]{0:T(128)} %bitcast.1.frame_ref, s32[96]{0:T(128)S(1)} %copy-done, s32[96]{0:T(128)S(1)} %copy-done.1, bf16[512,384]{1,0:T(8,128)(2,1)} %q_ref.1, bf16[512,384]{1,0:T(8,128)(2,1)S(1)} %collective-permute-done.1.refs_1_.refs_0_, ...), custom_call_target="tpu_custom_call" | custom-call | flops 17179869184 | bytes 1 | tf_op jit(solution)/shard_map/attend_1/pallas_call | solution.py:108
  42.2 5.2 %collective-permute-done.2.refs_2_ = bf16[512,384]{1,0:T(8,128)(2,1)S(1)} collective-permute-done((bf16[512,384]{1,0:T(8,128)(2,1)S(1)}, bf16[512,384]{1,0:T(8,128)(2,1)S(1)}, u32[]{:S(2)}, u32[]{:S(2)}) %collective-permute-start.2) | collective-permute-done | bytes 393248 | tf_op jit(solution)/shard_map/ppermute | solution.py:230
  49.3 5.8 %collective-permute-done.5.refs_3_ = bf16[512,384]{1,0:T(8,128)(2,1)S(1)} collective-permute-done((bf16[512,384]{1,0:T(8,128)(2,1)S(1)}, bf16[512,384]{1,0:T(8,128)(2,1)S(1)}, u32[]{:S(2)}, u32[]{:S(2)}) %collective-permute-start.5) | collective-permute-done | bytes 393248 | tf_op jit(solution)/shard_map/ppermute | solution.py:230
  57.0 3.3 %attend_2.1 = (f32[3,512,256]{2,1,0:T(8,128)S(1)}, f32[3,512,256]{2,1,0:T(8,128)S(1)}) custom-call(s32[1]{0:T(128)} %bitcast.1.frame_ref, s32[96]{0:T(128)S(1)} %copy-done, s32[96]{0:T(128)S(1)} %copy-done.1, bf16[512,384]{1,0:T(8,128)(2,1)} %q_ref.1, bf16[512,384]{1,0:T(8,128)(2,1)S(1)} %collective-permute-done.1.refs_1_.refs_0_, ...), custom_call_target="tpu_custom_call" | custom-call | flops 17179869184 | bytes 1 | tf_op jit(solution)/shard_map/attend_2/pallas_call | solution.py:108
  60.4 3.2 %collective-permute-done.4.refs_1_ = bf16[512,384]{1,0:T(8,128)(2,1)S(1)} collective-permute-done((bf16[512,384]{1,0:T(8,128)(2,1)S(1)}, bf16[512,384]{1,0:T(8,128)(2,1)S(1)}, u32[]{:S(2)}, u32[]{:S(2)}) %collective-permute-start.4) | collective-permute-done | bytes 393248 | tf_op jit(solution)/shard_map/ppermute | solution.py:230
  63.5 6.3 %collective-permute-done.6.refs_2_ = bf16[512,384]{1,0:T(8,128)(2,1)S(1)} collective-permute-done((bf16[512,384]{1,0:T(8,128)(2,1)S(1)}, bf16[512,384]{1,0:T(8,128)(2,1)S(1)}, u32[]{:S(2)}, u32[]{:S(2)}) %collective-permute-start.6) | collective-permute-done | bytes 393248 | tf_op jit(solution)/shard_map/ppermute | solution.py:230
  74.0 1.9 %collective-permute-start.9 = (f32[3,512,256]{2,1,0:T(8,128)S(1)}, f32[3,512,256]{2,1,0:T(8,128)S(1)}, u32[]{:S(2)}, u32[]{:S(2)}) collective-permute-start(f32[3,512,256]{2,1,0:T(8,128)S(1)} %attend_3_other.1), channel_id=1, source_target_pairs={{0,8},{8,0},{16,24},{24,16},{32,40},{40,32},{48,56},{56,48},{64,72... | collective-permute-start | bytes 4718600 | tf_op jit(solution)/shard_map/ppermute | solution.py:230
  75.9 2.9 %attend_3_own.1.own = f32[3,512,256]{2,1,0:T(8,128)S(1)} custom-call(s32[1]{0:T(128)} %bitcast.1.frame_ref, s32[96]{0:T(128)S(1)} %copy-done, s32[96]{0:T(128)S(1)} %copy-done.1, bf16[512,384]{1,0:T(8,128)(2,1)} %q_ref.1, bf16[512,384]{1,0:T(8,128)(2,1)S(1)} %collective-permute-done.4.refs_1_, bf16[512,384]{1,0:T(8,128)(2,1)S(1)} %collective-permute-done.6.refs_2_, ...), custom_call_target="tpu_custom_call" | custom-call | flops 17179869184 | bytes 1 | tf_op jit(solution)/shard_map/attend_3_own/pallas_call | solution.py:108
  78.9 2.2 %collective-permute-done.7.k_ref = bf16[512,384]{1,0:T(8,128)(2,1)S(1)} collective-permute-done((bf16[512,384]{1,0:T(8,128)(2,1)S(1)}, bf16[512,384]{1,0:T(8,128)(2,1)S(1)}, u32[]{:S(2)}, u32[]{:S(2)}) %collective-permute-start.7) | collective-permute-done | bytes 393248 | tf_op jit(solution)/shard_map/ppermute | solution.py:230
  81.0 4.2 %collective-permute-done.8.v_ref = bf16[512,384]{1,0:T(8,128)(2,1)S(1)} collective-permute-done((bf16[512,384]{1,0:T(8,128)(2,1)S(1)}, bf16[512,384]{1,0:T(8,128)(2,1)S(1)}, u32[]{:S(2)}, u32[]{:S(2)}) %collective-permute-start.8) | collective-permute-done | bytes 393248 | tf_op jit(solution)/shard_map/ppermute | solution.py:230
  85.3 3.3 %finish.1.refs_0_ = bf16[512,384]{1,0:T(8,128)(2,1)S(1)} custom-call(s32[1]{0:T(128)} %bitcast.1.frame_ref, s32[96]{0:T(128)S(1)} %copy-done, s32[96]{0:T(128)S(1)} %copy-done.1, bf16[512,384]{1,0:T(8,128)(2,1)} %q_ref.1, bf16[512,384]{1,0:T(8,128)(2,1)S(1)} %collective-permute-done.7.k_ref, bf16[512,384]{1,0:T(8,128)(2,1)S(1)} %collective-permute-done.8.v_ref, ...), custom_call_target="tpu_custom_call" | custom-call | flops 1 | bytes 1 | tf_op jit(solution)/shard_map/finish/pallas_call | solution.py:136
  88.5 4.6 %collective-permute-start.12 = (bf16[512,384]{1,0:T(8,128)(2,1)S(1)}, bf16[512,384]{1,0:T(8,128)(2,1)S(1)}, u32[]{:S(2)}, u32[]{:S(2)}) collective-permute-start(bf16[512,384]{1,0:T(8,128)(2,1)S(1)} %finish.1.refs_0_), channel_id=1, source_target_pairs={{0,1},{1,2},{2,3},{3,4},{4,5},{5,6},{6,7},{7,0},{8,9},{9,10},{10,1... | collective-permute-start | bytes 1179656 | tf_op jit(solution)/shard_map/ppermute | solution.py:230
  93.1 1.9 %collective-permute-start.10 = (bf16[512,384]{1,0:T(8,128)(2,1)S(1)}, bf16[512,384]{1,0:T(8,128)(2,1)}, u32[]{:S(2)}, u32[]{:S(2)}) collective-permute-start(bf16[512,384]{1,0:T(8,128)(2,1)S(1)} %finish.1.refs_0_), channel_id=1, source_target_pairs={{0,7},{1,0},{2,1},{3,2},{4,3},{5,4},{6,5},{7,6},{8,15},{9,8},{10,9... | collective-permute-start | bytes 1179656 | tf_op jit(solution)/shard_map/ppermute | solution.py:230
  95.1 5.1 %collective-permute-done.12.refs_1_ = bf16[512,384]{1,0:T(8,128)(2,1)S(1)} collective-permute-done((bf16[512,384]{1,0:T(8,128)(2,1)S(1)}, bf16[512,384]{1,0:T(8,128)(2,1)S(1)}, u32[]{:S(2)}, u32[]{:S(2)}) %collective-permute-start.12) | collective-permute-done | bytes 393248 | tf_op jit(solution)/shard_map/ppermute | solution.py:230
  100.1 5.1 %collective-permute-start.14 = (bf16[512,384]{1,0:T(8,128)(2,1)S(1)}, bf16[512,384]{1,0:T(8,128)(2,1)S(1)}, u32[]{:S(2)}, u32[]{:S(2)}) collective-permute-start(bf16[512,384]{1,0:T(8,128)(2,1)S(1)} %collective-permute-done.12.refs_1_), channel_id=1, source_target_pairs={{0,1},{1,2},{2,3},{3,4},{4,5},{5,6},{6,7},{7,0},{8,9},{9,10},{10,1... | collective-permute-start | bytes 1179656 | tf_op jit(solution)/shard_map/ppermute | solution.py:230
  105.6 1.9 %collective-permute-start.11 = (bf16[512,384]{1,0:T(8,128)(2,1)}, bf16[512,384]{1,0:T(8,128)(2,1)S(1)}, u32[]{:S(2)}, u32[]{:S(2)}) collective-permute-start(bf16[512,384]{1,0:T(8,128)(2,1)} %collective-permute-done.10.refs_2_), channel_id=1, source_target_pairs={{0,7},{1,0},{2,1},{3,2},{4,3},{5,4},{6,5},{7,6},{8,15},{9,8},{10,9... | collective-permute-start | bytes 1179656 | tf_op jit(solution)/shard_map/ppermute | solution.py:230
  107.6 5.2 %collective-permute-done.14.refs_1_ = bf16[512,384]{1,0:T(8,128)(2,1)S(1)} collective-permute-done((bf16[512,384]{1,0:T(8,128)(2,1)S(1)}, bf16[512,384]{1,0:T(8,128)(2,1)S(1)}, u32[]{:S(2)}, u32[]{:S(2)}) %collective-permute-start.14) | collective-permute-done | bytes 393248 | tf_op jit(solution)/shard_map/ppermute | solution.py:230
  112.8 5.6 %collective-permute-start.15 = (bf16[512,384]{1,0:T(8,128)(2,1)S(1)}, bf16[512,384]{1,0:T(8,128)(2,1)S(1)}, u32[]{:S(2)}, u32[]{:S(2)}) collective-permute-start(bf16[512,384]{1,0:T(8,128)(2,1)S(1)} %collective-permute-done.14.refs_1_), channel_id=1, source_target_pairs={{0,1},{1,2},{2,3},{3,4},{4,5},{5,6},{6,7},{7,0},{8,9},{9,10},{10,1... | collective-permute-start | bytes 1179656 | tf_op jit(solution)/shard_map/ppermute | solution.py:230
  120.0 1.9 %collective-permute-start.13 = (bf16[512,384]{1,0:T(8,128)(2,1)S(1)}, bf16[512,384]{1,0:T(8,128)(2,1)S(1)}, u32[]{:S(2)}, u32[]{:S(2)}) collective-permute-start(bf16[512,384]{1,0:T(8,128)(2,1)S(1)} %collective-permute-done.11.refs_2_), channel_id=1, source_target_pairs={{0,7},{1,0},{2,1},{3,2},{4,3},{5,4},{6,5},{7,6},{8,15},{9,8},{10,9... | collective-permute-start | bytes 1179656 | tf_op jit(solution)/shard_map/ppermute | solution.py:230
  121.9 3.8 %collective-permute-done.15.refs_1_ = bf16[512,384]{1,0:T(8,128)(2,1)S(1)} collective-permute-done((bf16[512,384]{1,0:T(8,128)(2,1)S(1)}, bf16[512,384]{1,0:T(8,128)(2,1)S(1)}, u32[]{:S(2)}, u32[]{:S(2)}) %collective-permute-start.15) | collective-permute-done | bytes 393248 | tf_op jit(solution)/shard_map/ppermute | solution.py:230
  125.8 5.6 %collective-permute-start.16 = (bf16[256,384]{1,0:T(8,128)(2,1)S(1)}, bf16[256,384]{1,0:T(8,128)(2,1)S(1)}, u32[]{:S(2)}, u32[]{:S(2)}) collective-permute-start(bf16[256,384]{1,0:T(8,128)(2,1)S(1)} %slice.8), channel_id=1, source_target_pairs={{0,1},{1,2},{2,3},{3,4},{4,5},{5,6},{6,7},{7,0},{8,9},{9,10},{10,1... | collective-permute-start | bytes 589832 | tf_op jit(solution)/shard_map/ppermute | solution.py:230
  132.8 1.9 %collective-permute-start.17 = (bf16[256,384]{1,0:T(8,128)(2,1)S(1)}, bf16[256,384]{1,0:T(8,128)(2,1)S(1)}, u32[]{:S(2)}, u32[]{:S(2)}) collective-permute-start(bf16[256,384]{1,0:T(8,128)(2,1)S(1)} %slice.7), channel_id=1, source_target_pairs={{0,7},{1,0},{2,1},{3,2},{4,3},{5,4},{6,5},{7,6},{8,15},{9,8},{10,9... | collective-permute-start | bytes 589832 | tf_op jit(solution)/shard_map/ppermute | solution.py:230
  135.4 6.2 %collective-permute-done.17.refs_2_ = bf16[256,384]{1,0:T(8,128)(2,1)S(1)} collective-permute-done((bf16[256,384]{1,0:T(8,128)(2,1)S(1)}, bf16[256,384]{1,0:T(8,128)(2,1)S(1)}, u32[]{:S(2)}, u32[]{:S(2)}) %collective-permute-start.17) | collective-permute-done | bytes 196640 | tf_op jit(solution)/shard_map/ppermute | solution.py:230
  (24 shorter events, 13.2 us)
Async XLA Ops:
  0.0 20.7 %collective-permute-start.1 = (bf16[512,384]{1,0:T(8,128)(2,1)}, bf16[512,384]{1,0:T(8,128)(2,1)S(1)}, u32[]{:S(2)}, u32[]{:S(2)}) collective-permute-start(bf16[512,384]{1,0:T(8,128)(2,1)} %q_ref.1), channel_id=1, source_target_pairs={{0,8},{8,0},{16,24},{24,16},{32,40},{40,32},{48,56},{56,48},{64,72... | collective-permute-start | bytes 1179656 | tf_op jit(solution)/shard_map/ppermute | solution.py:230
  1.9 25.3 %collective-permute-start = (bf16[512,384]{1,0:T(8,128)(2,1)}, bf16[512,384]{1,0:T(8,128)(2,1)S(1)}, u32[]{:S(2)}, u32[]{:S(2)}) collective-permute-start(bf16[512,384]{1,0:T(8,128)(2,1)} %refs_2_.1), channel_id=1, source_target_pairs={{0,16},{8,24},{16,32},{24,40},{32,48},{40,56},{48,64},{56,72},{64,... | collective-permute-start | bytes 1179656 | tf_op jit(solution)/shard_map/ppermute | solution.py:230
  6.2 29.0 %collective-permute-start.3 = (bf16[512,384]{1,0:T(8,128)(2,1)}, bf16[512,384]{1,0:T(8,128)(2,1)S(1)}, u32[]{:S(2)}, u32[]{:S(2)}) collective-permute-start(bf16[512,384]{1,0:T(8,128)(2,1)} %refs_3_.1), channel_id=1, source_target_pairs={{0,16},{8,24},{16,32},{24,40},{32,48},{40,56},{48,64},{56,72},{64,... | collective-permute-start | bytes 1179656 | tf_op jit(solution)/shard_map/ppermute | solution.py:230
  13.3 7.5 %copy-start = (s32[96]{0:T(128)S(1)}, s32[96]{0:T(128)}, u32[]{:S(2)}) copy-start(s32[96]{0:T(128)} %span_ref.11) | copy-start | bytes 1156
  13.3 7.5 %copy-start.1 = (s32[96]{0:T(128)S(1)}, s32[96]{0:T(128)}, u32[]{:S(2)}) copy-start(s32[96]{0:T(128)} %counts_ref.11) | copy-start | bytes 1156
  13.3 91.9 %all-to-all-start = ((bf16[8,384,384]{2,1,0:T(8,128)(2,1)}), bf16[8,384,384]{2,1,0:T(8,128)(2,1)S(1)}, u32[]{:S(2)}, u32[]{:S(2)}) async-start(bf16[8,384,384]{2,1,0:T(8,128)(2,1)} %column_blocks.1), calls=%async_computation | async-start | bytes 4718592 | tf_op jit(solution)/shard_map/all_to_all | solution.py:241
  27.2 20.2 %collective-permute-start.2 = (bf16[512,384]{1,0:T(8,128)(2,1)S(1)}, bf16[512,384]{1,0:T(8,128)(2,1)S(1)}, u32[]{:S(2)}, u32[]{:S(2)}) collective-permute-start(bf16[512,384]{1,0:T(8,128)(2,1)S(1)} %collective-permute-done.refs_2_), channel_id=1, source_target_pairs={{0,16},{8,24},{16,32},{24,40},{32,48},{40,56},{48,64},{56,72},{64,... | collective-permute-start | bytes 1179656 | tf_op jit(solution)/shard_map/ppermute | solution.py:230
  35.2 19.9 %collective-permute-start.5 = (bf16[512,384]{1,0:T(8,128)(2,1)S(1)}, bf16[512,384]{1,0:T(8,128)(2,1)S(1)}, u32[]{:S(2)}, u32[]{:S(2)}) collective-permute-start(bf16[512,384]{1,0:T(8,128)(2,1)S(1)} %collective-permute-done.3.refs_3_), channel_id=1, source_target_pairs={{0,16},{8,24},{16,32},{24,40},{32,48},{40,56},{48,64},{56,72},{64,... | collective-permute-start | bytes 1179656 | tf_op jit(solution)/shard_map/ppermute | solution.py:230
  47.4 16.2 %collective-permute-start.4 = (bf16[512,384]{1,0:T(8,128)(2,1)S(1)}, bf16[512,384]{1,0:T(8,128)(2,1)S(1)}, u32[]{:S(2)}, u32[]{:S(2)}) collective-permute-start(bf16[512,384]{1,0:T(8,128)(2,1)S(1)} %collective-permute-done.2.refs_2_), channel_id=1, source_target_pairs={{0,16},{8,24},{16,32},{24,40},{32,48},{40,56},{48,64},{56,72},{64,... | collective-permute-start | bytes 1179656 | tf_op jit(solution)/shard_map/ppermute | solution.py:230
  55.1 14.7 %collective-permute-start.6 = (bf16[512,384]{1,0:T(8,128)(2,1)S(1)}, bf16[512,384]{1,0:T(8,128)(2,1)S(1)}, u32[]{:S(2)}, u32[]{:S(2)}) collective-permute-start(bf16[512,384]{1,0:T(8,128)(2,1)S(1)} %collective-permute-done.5.refs_3_), channel_id=1, source_target_pairs={{0,16},{8,24},{16,32},{24,40},{32,48},{40,56},{48,64},{56,72},{64,... | collective-permute-start | bytes 1179656 | tf_op jit(solution)/shard_map/ppermute | solution.py:230
  69.8 11.2 %collective-permute-start.7 = (bf16[512,384]{1,0:T(8,128)(2,1)S(1)}, bf16[512,384]{1,0:T(8,128)(2,1)S(1)}, u32[]{:S(2)}, u32[]{:S(2)}) collective-permute-start(bf16[512,384]{1,0:T(8,128)(2,1)S(1)} %collective-permute-done.4.refs_1_), channel_id=1, source_target_pairs={{8,16},{24,32},{40,48},{56,64},{72,80},{88,96},{104,112},{120,128}... | collective-permute-start | bytes 1179656 | tf_op jit(solution)/shard_map/ppermute | solution.py:230
  71.1 14.1 %collective-permute-start.8 = (bf16[512,384]{1,0:T(8,128)(2,1)S(1)}, bf16[512,384]{1,0:T(8,128)(2,1)S(1)}, u32[]{:S(2)}, u32[]{:S(2)}) collective-permute-start(bf16[512,384]{1,0:T(8,128)(2,1)S(1)} %collective-permute-done.6.refs_2_), channel_id=1, source_target_pairs={{8,16},{24,32},{40,48},{56,64},{72,80},{88,96},{104,112},{120,128}... | collective-permute-start | bytes 1179656 | tf_op jit(solution)/shard_map/ppermute | solution.py:230
  74.0 11.2 %collective-permute-start.9 = (f32[3,512,256]{2,1,0:T(8,128)S(1)}, f32[3,512,256]{2,1,0:T(8,128)S(1)}, u32[]{:S(2)}, u32[]{:S(2)}) collective-permute-start(f32[3,512,256]{2,1,0:T(8,128)S(1)} %attend_3_other.1), channel_id=1, source_target_pairs={{0,8},{8,0},{16,24},{24,16},{32,40},{40,32},{48,56},{56,48},{64,72... | collective-permute-start | bytes 4718600 | tf_op jit(solution)/shard_map/ppermute | solution.py:230
  88.5 11.6 %collective-permute-start.12 = (bf16[512,384]{1,0:T(8,128)(2,1)S(1)}, bf16[512,384]{1,0:T(8,128)(2,1)S(1)}, u32[]{:S(2)}, u32[]{:S(2)}) collective-permute-start(bf16[512,384]{1,0:T(8,128)(2,1)S(1)} %finish.1.refs_0_), channel_id=1, source_target_pairs={{0,1},{1,2},{2,3},{3,4},{4,5},{5,6},{6,7},{7,0},{8,9},{9,10},{10,1... | collective-permute-start | bytes 1179656 | tf_op jit(solution)/shard_map/ppermute | solution.py:230
  93.1 12.5 %collective-permute-start.10 = (bf16[512,384]{1,0:T(8,128)(2,1)S(1)}, bf16[512,384]{1,0:T(8,128)(2,1)}, u32[]{:S(2)}, u32[]{:S(2)}) collective-permute-start(bf16[512,384]{1,0:T(8,128)(2,1)S(1)} %finish.1.refs_0_), channel_id=1, source_target_pairs={{0,7},{1,0},{2,1},{3,2},{4,3},{5,4},{6,5},{7,6},{8,15},{9,8},{10,9... | collective-permute-start | bytes 1179656 | tf_op jit(solution)/shard_map/ppermute | solution.py:230
  100.1 12.6 %collective-permute-start.14 = (bf16[512,384]{1,0:T(8,128)(2,1)S(1)}, bf16[512,384]{1,0:T(8,128)(2,1)S(1)}, u32[]{:S(2)}, u32[]{:S(2)}) collective-permute-start(bf16[512,384]{1,0:T(8,128)(2,1)S(1)} %collective-permute-done.12.refs_1_), channel_id=1, source_target_pairs={{0,1},{1,2},{2,3},{3,4},{4,5},{5,6},{6,7},{7,0},{8,9},{9,10},{10,1... | collective-permute-start | bytes 1179656 | tf_op jit(solution)/shard_map/ppermute | solution.py:230
  105.6 14.4 %collective-permute-start.11 = (bf16[512,384]{1,0:T(8,128)(2,1)}, bf16[512,384]{1,0:T(8,128)(2,1)S(1)}, u32[]{:S(2)}, u32[]{:S(2)}) collective-permute-start(bf16[512,384]{1,0:T(8,128)(2,1)} %collective-permute-done.10.refs_2_), channel_id=1, source_target_pairs={{0,7},{1,0},{2,1},{3,2},{4,3},{5,4},{6,5},{7,6},{8,15},{9,8},{10,9... | collective-permute-start | bytes 1179656 | tf_op jit(solution)/shard_map/ppermute | solution.py:230
  112.8 13.0 %collective-permute-start.15 = (bf16[512,384]{1,0:T(8,128)(2,1)S(1)}, bf16[512,384]{1,0:T(8,128)(2,1)S(1)}, u32[]{:S(2)}, u32[]{:S(2)}) collective-permute-start(bf16[512,384]{1,0:T(8,128)(2,1)S(1)} %collective-permute-done.14.refs_1_), channel_id=1, source_target_pairs={{0,1},{1,2},{2,3},{3,4},{4,5},{5,6},{6,7},{7,0},{8,9},{9,10},{10,1... | collective-permute-start | bytes 1179656 | tf_op jit(solution)/shard_map/ppermute | solution.py:230
  120.0 12.8 %collective-permute-start.13 = (bf16[512,384]{1,0:T(8,128)(2,1)S(1)}, bf16[512,384]{1,0:T(8,128)(2,1)S(1)}, u32[]{:S(2)}, u32[]{:S(2)}) collective-permute-start(bf16[512,384]{1,0:T(8,128)(2,1)S(1)} %collective-permute-done.11.refs_2_), channel_id=1, source_target_pairs={{0,7},{1,0},{2,1},{3,2},{4,3},{5,4},{6,5},{7,6},{8,15},{9,8},{10,9... | collective-permute-start | bytes 1179656 | tf_op jit(solution)/shard_map/ppermute | solution.py:230
  125.8 9.6 %collective-permute-start.16 = (bf16[256,384]{1,0:T(8,128)(2,1)S(1)}, bf16[256,384]{1,0:T(8,128)(2,1)S(1)}, u32[]{:S(2)}, u32[]{:S(2)}) collective-permute-start(bf16[256,384]{1,0:T(8,128)(2,1)S(1)} %slice.8), channel_id=1, source_target_pairs={{0,1},{1,2},{2,3},{3,4},{4,5},{5,6},{6,7},{7,0},{8,9},{9,10},{10,1... | collective-permute-start | bytes 589832 | tf_op jit(solution)/shard_map/ppermute | solution.py:230
  132.8 8.8 %collective-permute-start.17 = (bf16[256,384]{1,0:T(8,128)(2,1)S(1)}, bf16[256,384]{1,0:T(8,128)(2,1)S(1)}, u32[]{:S(2)}, u32[]{:S(2)}) collective-permute-start(bf16[256,384]{1,0:T(8,128)(2,1)S(1)} %slice.7), channel_id=1, source_target_pairs={{0,7},{1,0},{2,1},{3,2},{4,3},{5,4},{6,5},{7,6},{8,15},{9,8},{10,9... | collective-permute-start | bytes 589832 | tf_op jit(solution)/shard_map/ppermute | solution.py:230

commit v6 on v5

--- a/solution.py
+++ b/solution.py
@@ -65,12 +65,12 @@
     top[0] = new_top
 
 
-def _attention_body(sides, hops, first):
+def _attention_body(sides, hop, pieces, first):
     def body(frame_ref, span_ref, counts_ref, *refs):
         refs = list(refs)
         take = lambda n: [refs.pop(0) for _ in range(n)]
         q_refs = take(len(sides))
-        kv_refs = [take(2) for _ in hops]
+        kv_refs = [take(2) for _ in range(pieces)]
         state_refs = [None] * len(sides) if first else take(len(sides))
         out_refs = take(len(sides))
         scratch = [take(2) for _ in sides]
@@ -81,16 +81,22 @@
                 top[...] = jnp.full_like(top, NEG)
             else:
                 _unpack(state, acc, top)
-        for hop, (k_ref, v_ref) in zip(hops, kv_refs):
+        slot0 = 0
+        for k_ref, v_ref in kv_refs:
             for side, q_ref, (acc, top) in zip(sides, q_refs, scratch):
                 limit = _visible(frame, side, 2 * hop, span_ref, counts_ref)
-                _attend(limit, q_ref, k_ref, v_ref, acc, top)
+                _attend(limit - slot0, q_ref, k_ref, v_ref, acc, top)
+            slot0 += k_ref.shape[0]
         lane = lax.broadcasted_iota(jnp.int32, (1, HD), 1)
         for out, (acc, top) in zip(out_refs, scratch):
             out[0, :, :HD] = acc[0, :, :HD]
             out[0, :, HD:] = jnp.where(lane < HD // 2, top[0], acc[0, :, HD:])
 
     return body
+
+
+def _column(array):
+    return pl.BlockSpec((array.shape[0], HD), lambda h, *_: (0, h))
 
 
 def _specs(per_frame):
@@ -100,18 +106,20 @@
     return column, packed, scratch
 
 
-def attention_call(scalars, queries, sources, sides, hops, states, name):
+def attention_call(scalars, queries, sources, sides, hop, states, name):
     per_frame, width = queries[0].shape
     heads = width // HD
     column, packed, scratch = _specs(per_frame)
     operands = list(queries) + [array for pair in sources for array in pair] + list(states or ())
     return pl.pallas_call(
-        _attention_body(sides, hops, states is None),
+        _attention_body(sides, hop, len(sources), states is None),
         out_shape=[jax.ShapeDtypeStruct((heads, per_frame, 2 * HD), jnp.float32)] * len(sides),
         grid_spec=pltpu.PrefetchScalarGridSpec(
             num_scalar_prefetch=3,
             grid=(heads,),
-            in_specs=[column] * (len(sides) + 2 * len(hops)) + [packed] * len(states or ()),
+            in_specs=[column] * len(sides)
+            + [_column(array) for pair in sources for array in pair]
+            + [packed] * len(states or ()),
             out_specs=[packed] * len(sides),
             scratch_shapes=scratch * len(sides),
         ),
@@ -121,16 +129,17 @@
     )(*scalars, *operands)
 
 
-def _finish_body(frame_ref, span_ref, counts_ref, q_ref, k_ref, v_ref, own, other, out_ref, acc, top):
+def _finish_body(frame_ref, span_ref, counts_ref, q_ref, k0_ref, v0_ref, k1_ref, v1_ref, own, other, out_ref, acc, top):
     _unpack(own, acc, top)
     limit = _visible(frame_ref[0], 0, WIN - 1, span_ref, counts_ref)
     limit = jnp.where(frame_ref[0] % 2 == 0, limit, 0)
-    _attend(limit, q_ref, k_ref, v_ref, acc, top)
+    _attend(limit, q_ref, k0_ref, v0_ref, acc, top)
+    _attend(limit - k0_ref.shape[0], q_ref, k1_ref, v1_ref, acc, top)
     _join(other, acc, top)
     out_ref[...] = (acc[0, :, :HD] / acc[0, :, HD:]).astype(jnp.bfloat16)
 
 
-def finish_call(scalars, queries, keys, values, own, other, name):
+def finish_call(scalars, queries, sources, own, other, name):
     per_frame, width = queries.shape
     column, packed, scratch = _specs(per_frame)
     return pl.pallas_call(
@@ -139,14 +148,14 @@
         grid_spec=pltpu.PrefetchScalarGridSpec(
             num_scalar_prefetch=3,
             grid=(width // HD,),
-            in_specs=[column, column, column, packed, packed],
+            in_specs=[column] + [_column(array) for pair in sources for array in pair] + [packed, packed],
             out_specs=column,
             scratch_shapes=scratch,
         ),
         cost_estimate=BRIEF,
         compiler_params=pltpu.CompilerParams(vmem_limit_bytes=SMALL_VMEM),
         name=name,
-    )(*scalars, queries, keys, values, own, other)
+    )(*scalars, queries, *(array for pair in sources for array in pair), own, other)
 
 
 def in_hbm(array):
@@ -229,41 +238,44 @@
     def send(block, route, axis="frame"):
         return lax.ppermute(block, axis, route)
 
-    def attend(sources, sides, hops, states, name):
+    def attend(sources, sides, hop, states, name):
         both = (in_hbm(queries), q_other)
         return attention_call(
-            scalars, [both[side] for side in sides], sources, sides, hops, states, name
+            scalars, [both[side] for side in sides], sources, sides, hop, states, name
         )
 
-    k1, v1 = send(keys, by_chip), send(values, by_chip)
+    def send_all(pieces, route):
+        return [(send(k, route), send(v, route)) for k, v in pieces]
+
+    half = per_frame // 2
+    hop1 = send_all([(keys[:half], values[:half]), (keys[half:], values[half:])], by_chip)
     q_other = send(queries, swap)
     blocks = column_blocks(out_weight, groups)
     weight = lax.all_to_all(blocks, "head", split_axis=0, concat_axis=0, tiled=True)
-    parts = attend([(in_hbm(keys), in_hbm(values))], (0, 1), (0,), None, "attend_0")
-    k1, parts = after((k1, parts))
-    k2, v2 = send(k1, by_chip), send(v1, by_chip)
-    parts = attend([(k1, v1)], (0, 1), (1,), parts, "attend_1")
-    k2, parts = after((k2, parts))
-    k3, v3 = send(k2, by_chip), send(v2, by_chip)
-    own, other = attend([(k2, v2)], (0, 1), (2,), parts, "attend_2")
-    k3, v3, own, other = after((k3, v3, own, other))
-    (other,) = attend([(k3, v3)], (1,), (3,), [other], "attend_3_other")
+    parts = attend([(in_hbm(keys), in_hbm(values))], (0, 1), 0, None, "attend_0")
+    hop1[1], parts = after((hop1[1], parts))
+    hop2 = send_all(hop1, by_chip)
+    parts = attend(hop1, (0, 1), 1, parts, "attend_1")
+    hop2[1], parts = after((hop2[1], parts))
+    hop3 = send_all(hop2, by_chip)
+    own, other = attend(hop2, (0, 1), 2, parts, "attend_2")
+    hop3[1], own, other = after((hop3[1], own, other))
+    hop4 = send_all(hop3, to_even)
+    (other,) = attend(hop3, (1,), 3, [other], "attend_3_other")
     from_other = send(other, swap)
-    k4, v4 = send(k3, to_even), send(v3, to_even)
-    (own,) = attend([(k3, v3)], (0,), (3,), [own], "attend_3_own")
-    attended = finish_call(scalars, in_hbm(queries), k4, v4, own, from_other, "finish")
+    (own,) = attend(hop3, (0,), 3, [own], "attend_3_own")
+    attended = finish_call(scalars, in_hbm(queries), hop4, own, from_other, "finish")
 
     def project(base, pieces, places, dtype, name):
         return project_call(group, weight, base, pieces, places, dtype, name)
 
-    half = per_frame // 2
     up, down = attended, attended
     held, places, total = [attended], [(None, 0)], None
     for step in (1, 2, 3):
         up, down = send(up, upward, "head"), send(down, downward, "head")
         total = project(total, held, places, jnp.float32, f"project_{step - 1}")
         held, places = [up, down], [(None, groups - step), (None, step)]
-        down, total = after((down, total))
+        up, total = after((up, total))
     far = [send(up[:half], upward, "head"), send(down[half:], downward, "head")]
     total = project(total, held, places, jnp.float32, "project_3")
     return project(total, far, [(0, 4), (1, 4)], jnp.bfloat16, "project_4")

time: 142 us -> 160 us (1.13)
  the two profiles are of different devices: /device:TPU:30 before, /device:TPU:4 now
where the time goes in v6:
time: 160 us; the launch traced here: 159 us
  starting transfers between devices  90.9 us (57%)
  Pallas kernels  47.3 us (30%)
  waiting for transfers between devices  16.4 us (10%)
  local copies, waits for them, and re-layouts  3.67 us (2%)
    ppermute x26, starting transfers between devices, send(): return lax.ppermute(block, axis, route)  83.6 us
    pallas_call x5, Pallas kernels, attention_call(): pl.pallas_call(_attention_body(sides, hop, len(sources), states is None),...  34.1 us
    ppermute x26, waiting for transfers between devices, send(): return lax.ppermute(block, axis, route)  16.4 us
    all_to_all x1, starting transfers between devices, on_device(): lax.all_to_all(blocks, 'head', split_axis=0, concat_axis=0, tiled=True)  7.23 us
    pallas_call x1, Pallas kernels, finish_call(): pl.pallas_call(_finish_body, out_shape=jax.ShapeDtypeStruct((per_frame, w...  5.89 us
    pallas_call x5, Pallas kernels, project_call(): pl.pallas_call(_project_body(places, base is not None), out_shape=jax.Sha...  4.48 us
  transfers between devices with their start and end apart: 27, of which 5 were waited for; matrix products, arithmetic and copies ran while one was open for 2% of the time, Pallas kernels for 29%

profile of v6, /device:TPU:4, one launch (start us, length us, event | category | flops | bytes accessed | tf_op | source)
XLA Modules:
  0.0 158.8 jit_solution(5578618535978246377)
XLA Ops:
  3.7 4.3 %collective-permute-start = (bf16[256,384]{1,0:T(8,128)(2,1)}, bf16[256,384]{1,0:T(8,128)(2,1)S(1)}, u32[]{:S(2)}, u32[]{:S(2)}) collective-permute-start(bf16[256,384]{1,0:T(8,128)(2,1)} %get-tuple-element.56), channel_id=1, source_target_pairs={{0,16},{8,24},{16,32},{24,40},{32,48},{40,56},{48,64},{56,72},{64,... | collective-permute-start | bytes 589832 | tf_op jit(solution)/shard_map/ppermute | solution.py:239
  9.8 4.3 %collective-permute-start.4 = (bf16[256,384]{1,0:T(8,128)(2,1)}, bf16[256,384]{1,0:T(8,128)(2,1)S(1)}, u32[]{:S(2)}, u32[]{:S(2)}) collective-permute-start(bf16[256,384]{1,0:T(8,128)(2,1)} %get-tuple-element.54), channel_id=1, source_target_pairs={{0,16},{8,24},{16,32},{24,40},{32,48},{40,56},{48,64},{56,72},{64,... | collective-permute-start | bytes 589832 | tf_op jit(solution)/shard_map/ppermute | solution.py:239
  14.1 4.3 %collective-permute-start.8 = (bf16[256,384]{1,0:T(8,128)(2,1)}, bf16[256,384]{1,0:T(8,128)(2,1)S(1)}, u32[]{:S(2)}, u32[]{:S(2)}) collective-permute-start(bf16[256,384]{1,0:T(8,128)(2,1)} %get-tuple-element.55), channel_id=1, source_target_pairs={{0,16},{8,24},{16,32},{24,40},{32,48},{40,56},{48,64},{56,72},{64,... | collective-permute-start | bytes 589832 | tf_op jit(solution)/shard_map/ppermute | solution.py:239
  18.4 5.5 %collective-permute-start.9 = (bf16[256,384]{1,0:T(8,128)(2,1)}, bf16[256,384]{1,0:T(8,128)(2,1)S(1)}, u32[]{:S(2)}, u32[]{:S(2)}) collective-permute-start(bf16[256,384]{1,0:T(8,128)(2,1)} %get-tuple-element.53), channel_id=1, source_target_pairs={{0,16},{8,24},{16,32},{24,40},{32,48},{40,56},{48,64},{56,72},{64,... | collective-permute-start | bytes 589832 | tf_op jit(solution)/shard_map/ppermute | solution.py:239
  23.9 2.8 %column_blocks.1 = bf16[8,384,384]{2,1,0:T(8,128)(2,1)} custom-call(bf16[384,3072]{1,0:T(8,128)(2,1)} %w_ref.1), custom_call_target="tpu_custom_call" | custom-call | flops 1 | bytes 1 | tf_op jit(solution)/shard_map/column_blocks/pallas_call | solution.py:174
  26.7 7.2 %all-to-all-start = ((bf16[8,384,384]{2,1,0:T(8,128)(2,1)}), bf16[8,384,384]{2,1,0:T(8,128)(2,1)S(1)}, u32[]{:S(2)}, u32[]{:S(2)}) async-start(bf16[8,384,384]{2,1,0:T(8,128)(2,1)} %column_blocks.1), calls=%async_computation | async-start | bytes 4718592 | tf_op jit(solution)/shard_map/all_to_all | solution.py:254
  33.9 4.3 %collective-permute-start.1 = (bf16[256,384]{1,0:T(8,128)(2,1)S(1)}, bf16[256,384]{1,0:T(8,128)(2,1)S(1)}, u32[]{:S(2)}, u32[]{:S(2)}) collective-permute-start(bf16[256,384]{1,0:T(8,128)(2,1)S(1)} %collective-permute-done.refs_2_), channel_id=1, source_target_pairs={{0,16},{8,24},{16,32},{24,40},{32,48},{40,56},{48,64},{56,72},{64,... | collective-permute-start | bytes 589832 | tf_op jit(solution)/shard_map/ppermute | solution.py:239
  38.2 4.3 %collective-permute-start.5 = (bf16[256,384]{1,0:T(8,128)(2,1)S(1)}, bf16[256,384]{1,0:T(8,128)(2,1)S(1)}, u32[]{:S(2)}, u32[]{:S(2)}) collective-permute-start(bf16[256,384]{1,0:T(8,128)(2,1)S(1)} %collective-permute-done.4.refs_3_), channel_id=1, source_target_pairs={{0,16},{8,24},{16,32},{24,40},{32,48},{40,56},{48,64},{56,72},{64,... | collective-permute-start | bytes 589832 | tf_op jit(solution)/shard_map/ppermute | solution.py:239
  42.6 6.5 %attend_0.1 = (f32[3,512,256]{2,1,0:T(8,128)S(1)}, f32[3,512,256]{2,1,0:T(8,128)S(1)}) custom-call(s32[1]{0:T(128)} %bitcast.1.frame_ref, s32[96]{0:T(128)S(1)} %copy-done, s32[96]{0:T(128)S(1)} %copy-done.1, bf16[512,384]{1,0:T(8,128)(2,1)} %q_ref.1, bf16[512,384]{1,0:T(8,128)(2,1)S(1)} %collective-permute-done.10.refs_1_.refs_0_, ...), custom_call_target="tpu_custom_call" | custom-call | flops 17179869184 | bytes 1 | tf_op jit(solution)/shard_map/attend_0/pallas_call | solution.py:114
  49.0 4.0 %collective-permute-start.11 = (bf16[256,384]{1,0:T(8,128)(2,1)S(1)}, bf16[256,384]{1,0:T(8,128)(2,1)S(1)}, u32[]{:S(2)}, u32[]{:S(2)}) collective-permute-start(bf16[256,384]{1,0:T(8,128)(2,1)S(1)} %collective-permute-done.8.refs_4_), channel_id=1, source_target_pairs={{0,16},{8,24},{16,32},{24,40},{32,48},{40,56},{48,64},{56,72},{64,... | collective-permute-start | bytes 589832 | tf_op jit(solution)/shard_map/ppermute | solution.py:239
  53.0 3.4 %collective-permute-start.12 = (bf16[256,384]{1,0:T(8,128)(2,1)S(1)}, bf16[256,384]{1,0:T(8,128)(2,1)S(1)}, u32[]{:S(2)}, u32[]{:S(2)}) collective-permute-start(bf16[256,384]{1,0:T(8,128)(2,1)S(1)} %collective-permute-done.9.refs_5_), channel_id=1, source_target_pairs={{0,16},{8,24},{16,32},{24,40},{32,48},{40,56},{48,64},{56,72},{64,... | collective-permute-start | bytes 589832 | tf_op jit(solution)/shard_map/ppermute | solution.py:239
  56.4 3.4 %collective-permute-start.2 = (bf16[256,384]{1,0:T(8,128)(2,1)S(1)}, bf16[256,384]{1,0:T(8,128)(2,1)S(1)}, u32[]{:S(2)}, u32[]{:S(2)}) collective-permute-start(bf16[256,384]{1,0:T(8,128)(2,1)S(1)} %collective-permute-done.1.refs_2_), channel_id=1, source_target_pairs={{0,16},{8,24},{16,32},{24,40},{32,48},{40,56},{48,64},{56,72},{64,... | collective-permute-start | bytes 589832 | tf_op jit(solution)/shard_map/ppermute | solution.py:239
  59.8 3.4 %collective-permute-start.6 = (bf16[256,384]{1,0:T(8,128)(2,1)S(1)}, bf16[256,384]{1,0:T(8,128)(2,1)S(1)}, u32[]{:S(2)}, u32[]{:S(2)}) collective-permute-start(bf16[256,384]{1,0:T(8,128)(2,1)S(1)} %collective-permute-done.5.refs_3_), channel_id=1, source_target_pairs={{0,16},{8,24},{16,32},{24,40},{32,48},{40,56},{48,64},{56,72},{64,... | collective-permute-start | bytes 589832 | tf_op jit(solution)/shard_map/ppermute | solution.py:239
  63.2 8.9 %attend_1.1 = (f32[3,512,256]{2,1,0:T(8,128)S(1)}, f32[3,512,256]{2,1,0:T(8,128)S(1)}) custom-call(s32[1]{0:T(128)} %bitcast.1.frame_ref, s32[96]{0:T(128)S(1)} %copy-done, s32[96]{0:T(128)S(1)} %copy-done.1, bf16[512,384]{1,0:T(8,128)(2,1)} %q_ref.1, bf16[512,384]{1,0:T(8,128)(2,1)S(1)} %collective-permute-done.10.refs_1_.refs_0_, ...), custom_call_target="tpu_custom_call" | custom-call | flops 17179869184 | bytes 1 | tf_op jit(solution)/shard_map/attend_1/pallas_call | solution.py:114
  72.2 1.9 %collective-permute-start.13 = (bf16[256,384]{1,0:T(8,128)(2,1)S(1)}, bf16[256,384]{1,0:T(8,128)(2,1)S(1)}, u32[]{:S(2)}, u32[]{:S(2)}) collective-permute-start(bf16[256,384]{1,0:T(8,128)(2,1)S(1)} %collective-permute-done.11.refs_4_), channel_id=1, source_target_pairs={{0,16},{8,24},{16,32},{24,40},{32,48},{40,56},{48,64},{56,72},{64,... | collective-permute-start | bytes 589832 | tf_op jit(solution)/shard_map/ppermute | solution.py:239
  74.1 1.9 %collective-permute-start.14 = (bf16[256,384]{1,0:T(8,128)(2,1)S(1)}, bf16[256,384]{1,0:T(8,128)(2,1)S(1)}, u32[]{:S(2)}, u32[]{:S(2)}) collective-permute-start(bf16[256,384]{1,0:T(8,128)(2,1)S(1)} %collective-permute-done.12.refs_5_), channel_id=1, source_target_pairs={{0,16},{8,24},{16,32},{24,40},{32,48},{40,56},{48,64},{56,72},{64,... | collective-permute-start | bytes 589832 | tf_op jit(solution)/shard_map/ppermute | solution.py:239
  78.7 8.9 %attend_2.1 = (f32[3,512,256]{2,1,0:T(8,128)S(1)}, f32[3,512,256]{2,1,0:T(8,128)S(1)}) custom-call(s32[1]{0:T(128)} %bitcast.1.frame_ref, s32[96]{0:T(128)S(1)} %copy-done, s32[96]{0:T(128)S(1)} %copy-done.1, bf16[512,384]{1,0:T(8,128)(2,1)} %q_ref.1, bf16[512,384]{1,0:T(8,128)(2,1)S(1)} %collective-permute-done.10.refs_1_.refs_0_, ...), custom_call_target="tpu_custom_call" | custom-call | flops 17179869184 | bytes 1 | tf_op jit(solution)/shard_map/attend_2/pallas_call | solution.py:114
  90.2 4.5 %attend_3_other.1 = f32[3,512,256]{2,1,0:T(8,128)S(1)} custom-call(s32[1]{0:T(128)} %bitcast.1.frame_ref, s32[96]{0:T(128)S(1)} %copy-done, s32[96]{0:T(128)S(1)} %copy-done.1, bf16[512,384]{1,0:T(8,128)(2,1)S(1)} %collective-permute-done.10.refs_1_.refs_0_, bf16[256,384]{1,0:T(8,128)(2,1)S(1)} %collective-permute-done.2.refs_1_, ...), custom_call_target="tpu_custom_call" | custom-call | flops 17179869184 | bytes 1 | tf_op jit(solution)/shard_map/attend_3_other/pallas_call | solution.py:114
  94.7 1.9 %collective-permute-start.17 = (f32[3,512,256]{2,1,0:T(8,128)S(1)}, f32[3,512,256]{2,1,0:T(8,128)S(1)}, u32[]{:S(2)}, u32[]{:S(2)}) collective-permute-start(f32[3,512,256]{2,1,0:T(8,128)S(1)} %attend_3_other.1), channel_id=1, source_target_pairs={{0,8},{8,0},{16,24},{24,16},{32,40},{40,32},{48,56},{56,48},{64,72... | collective-permute-start | bytes 4718600 | tf_op jit(solution)/shard_map/ppermute | solution.py:239
  96.7 5.3 %attend_3_own.1.own = f32[3,512,256]{2,1,0:T(8,128)S(1)} custom-call(s32[1]{0:T(128)} %bitcast.1.frame_ref, s32[96]{0:T(128)S(1)} %copy-done, s32[96]{0:T(128)S(1)} %copy-done.1, bf16[512,384]{1,0:T(8,128)(2,1)} %q_ref.1, bf16[256,384]{1,0:T(8,128)(2,1)S(1)} %collective-permute-done.2.refs_1_, bf16[256,384]{1,0:T(8,128)(2,1)S(1)} %collective-permute-done.6.refs_2_, ...), custom_call_target="tpu_custom_call" | custom-call | flops 17179869184 | bytes 1 | tf_op jit(solution)/shard_map/attend_3_own/pallas_call | solution.py:114
  102.0 5.9 %finish.1.refs_0_ = bf16[512,384]{1,0:T(8,128)(2,1)S(1)} custom-call(s32[1]{0:T(128)} %bitcast.1.frame_ref, s32[96]{0:T(128)S(1)} %copy-done, s32[96]{0:T(128)S(1)} %copy-done.1, bf16[512,384]{1,0:T(8,128)(2,1)} %q_ref.1, bf16[256,384]{1,0:T(8,128)(2,1)S(1)} %collective-permute-done.3.k0_ref, bf16[256,384]{1,0:T(8,128)(2,1)S(1)} %collective-permute-done.7.v0_ref, ...), custom_call_target="tpu_custom_call" | custom-call | flops 1 | bytes 1 | tf_op jit(solution)/shard_map/finish/pallas_call | solution.py:145
  107.9 5.1 %collective-permute-start.20 = (bf16[512,384]{1,0:T(8,128)(2,1)S(1)}, bf16[512,384]{1,0:T(8,128)(2,1)S(1)}, u32[]{:S(2)}, u32[]{:S(2)}) collective-permute-start(bf16[512,384]{1,0:T(8,128)(2,1)S(1)} %finish.1.refs_0_), channel_id=1, source_target_pairs={{0,7},{1,0},{2,1},{3,2},{4,3},{5,4},{6,5},{7,6},{8,15},{9,8},{10,9... | collective-permute-start | bytes 1179656 | tf_op jit(solution)/shard_map/ppermute | solution.py:239
  113.1 1.9 %collective-permute-start.18 = (bf16[512,384]{1,0:T(8,128)(2,1)S(1)}, bf16[512,384]{1,0:T(8,128)(2,1)}, u32[]{:S(2)}, u32[]{:S(2)}) collective-permute-start(bf16[512,384]{1,0:T(8,128)(2,1)S(1)} %finish.1.refs_0_), channel_id=1, source_target_pairs={{0,1},{1,2},{2,3},{3,4},{4,5},{5,6},{6,7},{7,0},{8,9},{9,10},{10,1... | collective-permute-start | bytes 1179656 | tf_op jit(solution)/shard_map/ppermute | solution.py:239
  115.0 3.3 %collective-permute-done.20.refs_2_ = bf16[512,384]{1,0:T(8,128)(2,1)S(1)} collective-permute-done((bf16[512,384]{1,0:T(8,128)(2,1)S(1)}, bf16[512,384]{1,0:T(8,128)(2,1)S(1)}, u32[]{:S(2)}, u32[]{:S(2)}) %collective-permute-start.20) | collective-permute-done | bytes 393248 | tf_op jit(solution)/shard_map/ppermute | solution.py:239
  118.4 5.8 %collective-permute-start.22 = (bf16[512,384]{1,0:T(8,128)(2,1)S(1)}, bf16[512,384]{1,0:T(8,128)(2,1)S(1)}, u32[]{:S(2)}, u32[]{:S(2)}) collective-permute-start(bf16[512,384]{1,0:T(8,128)(2,1)S(1)} %collective-permute-done.20.refs_2_), channel_id=1, source_target_pairs={{0,7},{1,0},{2,1},{3,2},{4,3},{5,4},{6,5},{7,6},{8,15},{9,8},{10,9... | collective-permute-start | bytes 1179656 | tf_op jit(solution)/shard_map/ppermute | solution.py:239
  126.5 2.7 %collective-permute-done.22.refs_2_ = bf16[512,384]{1,0:T(8,128)(2,1)S(1)} collective-permute-done((bf16[512,384]{1,0:T(8,128)(2,1)S(1)}, bf16[512,384]{1,0:T(8,128)(2,1)S(1)}, u32[]{:S(2)}, u32[]{:S(2)}) %collective-permute-start.22) | collective-permute-done | bytes 393248 | tf_op jit(solution)/shard_map/ppermute | solution.py:239
  129.2 5.6 %collective-permute-start.23 = (bf16[512,384]{1,0:T(8,128)(2,1)S(1)}, bf16[512,384]{1,0:T(8,128)(2,1)S(1)}, u32[]{:S(2)}, u32[]{:S(2)}) collective-permute-start(bf16[512,384]{1,0:T(8,128)(2,1)S(1)} %collective-permute-done.22.refs_2_), channel_id=1, source_target_pairs={{0,7},{1,0},{2,1},{3,2},{4,3},{5,4},{6,5},{7,6},{8,15},{9,8},{10,9... | collective-permute-start | bytes 1179656 | tf_op jit(solution)/shard_map/ppermute | solution.py:239
  136.5 1.9 %collective-permute-start.21 = (bf16[512,384]{1,0:T(8,128)(2,1)S(1)}, bf16[512,384]{1,0:T(8,128)(2,1)S(1)}, u32[]{:S(2)}, u32[]{:S(2)}) collective-permute-start(bf16[512,384]{1,0:T(8,128)(2,1)S(1)} %collective-permute-done.19.refs_1_), channel_id=1, source_target_pairs={{0,1},{1,2},{2,3},{3,4},{4,5},{5,6},{6,7},{7,0},{8,9},{9,10},{10,1... | collective-permute-start | bytes 1179656 | tf_op jit(solution)/shard_map/ppermute | solution.py:239
  138.4 2.8 %collective-permute-done.23.refs_2_ = bf16[512,384]{1,0:T(8,128)(2,1)S(1)} collective-permute-done((bf16[512,384]{1,0:T(8,128)(2,1)S(1)}, bf16[512,384]{1,0:T(8,128)(2,1)S(1)}, u32[]{:S(2)}, u32[]{:S(2)}) %collective-permute-start.23) | collective-permute-done | bytes 393248 | tf_op jit(solution)/shard_map/ppermute | solution.py:239
  141.2 5.6 %collective-permute-start.25 = (bf16[256,384]{1,0:T(8,128)(2,1)S(1)}, bf16[256,384]{1,0:T(8,128)(2,1)S(1)}, u32[]{:S(2)}, u32[]{:S(2)}) collective-permute-start(bf16[256,384]{1,0:T(8,128)(2,1)S(1)} %slice.24), channel_id=1, source_target_pairs={{0,7},{1,0},{2,1},{3,2},{4,3},{5,4},{6,5},{7,6},{8,15},{9,8},{10,9... | collective-permute-start | bytes 589832 | tf_op jit(solution)/shard_map/ppermute | solution.py:239
  148.8 1.9 %collective-permute-start.24 = (bf16[256,384]{1,0:T(8,128)(2,1)S(1)}, bf16[256,384]{1,0:T(8,128)(2,1)S(1)}, u32[]{:S(2)}, u32[]{:S(2)}) collective-permute-start(bf16[256,384]{1,0:T(8,128)(2,1)S(1)} %slice.22), channel_id=1, source_target_pairs={{0,1},{1,2},{2,3},{3,4},{4,5},{5,6},{6,7},{7,0},{8,9},{9,10},{10,1... | collective-permute-start | bytes 589832 | tf_op jit(solution)/shard_map/ppermute | solution.py:239
  151.4 6.2 %collective-permute-done.24.refs_1_ = bf16[256,384]{1,0:T(8,128)(2,1)S(1)} collective-permute-done((bf16[256,384]{1,0:T(8,128)(2,1)S(1)}, bf16[256,384]{1,0:T(8,128)(2,1)S(1)}, u32[]{:S(2)}, u32[]{:S(2)}) %collective-permute-start.24) | collective-permute-done | bytes 196640 | tf_op jit(solution)/shard_map/ppermute | solution.py:239
  (42 shorter events, 18.6 us)
Async XLA Ops:
  0.0 42.5 %collective-permute-start.10 = (bf16[512,384]{1,0:T(8,128)(2,1)}, bf16[512,384]{1,0:T(8,128)(2,1)S(1)}, u32[]{:S(2)}, u32[]{:S(2)}) collective-permute-start(bf16[512,384]{1,0:T(8,128)(2,1)} %q_ref.1), channel_id=1, source_target_pairs={{0,8},{8,0},{16,24},{24,16},{32,40},{40,32},{48,56},{56,48},{64,72... | collective-permute-start | bytes 1179656 | tf_op jit(solution)/shard_map/ppermute | solution.py:239
  3.7 30.2 %collective-permute-start = (bf16[256,384]{1,0:T(8,128)(2,1)}, bf16[256,384]{1,0:T(8,128)(2,1)S(1)}, u32[]{:S(2)}, u32[]{:S(2)}) collective-permute-start(bf16[256,384]{1,0:T(8,128)(2,1)} %get-tuple-element.56), channel_id=1, source_target_pairs={{0,16},{8,24},{16,32},{24,40},{32,48},{40,56},{48,64},{56,72},{64,... | collective-permute-start | bytes 589832 | tf_op jit(solution)/shard_map/ppermute | solution.py:239
  9.8 28.4 %collective-permute-start.4 = (bf16[256,384]{1,0:T(8,128)(2,1)}, bf16[256,384]{1,0:T(8,128)(2,1)S(1)}, u32[]{:S(2)}, u32[]{:S(2)}) collective-permute-start(bf16[256,384]{1,0:T(8,128)(2,1)} %get-tuple-element.54), channel_id=1, source_target_pairs={{0,16},{8,24},{16,32},{24,40},{32,48},{40,56},{48,64},{56,72},{64,... | collective-permute-start | bytes 589832 | tf_op jit(solution)/shard_map/ppermute | solution.py:239
  14.1 34.9 %collective-permute-start.8 = (bf16[256,384]{1,0:T(8,128)(2,1)}, bf16[256,384]{1,0:T(8,128)(2,1)S(1)}, u32[]{:S(2)}, u32[]{:S(2)}) collective-permute-start(bf16[256,384]{1,0:T(8,128)(2,1)} %get-tuple-element.55), channel_id=1, source_target_pairs={{0,16},{8,24},{16,32},{24,40},{32,48},{40,56},{48,64},{56,72},{64,... | collective-permute-start | bytes 589832 | tf_op jit(solution)/shard_map/ppermute | solution.py:239
  18.4 30.6 %collective-permute-start.9 = (bf16[256,384]{1,0:T(8,128)(2,1)}, bf16[256,384]{1,0:T(8,128)(2,1)S(1)}, u32[]{:S(2)}, u32[]{:S(2)}) collective-permute-start(bf16[256,384]{1,0:T(8,128)(2,1)} %get-tuple-element.53), channel_id=1, source_target_pairs={{0,16},{8,24},{16,32},{24,40},{32,48},{40,56},{48,64},{56,72},{64,... | collective-permute-start | bytes 589832 | tf_op jit(solution)/shard_map/ppermute | solution.py:239
  26.7 15.8 %copy-start = (s32[96]{0:T(128)S(1)}, s32[96]{0:T(128)}, u32[]{:S(2)}) copy-start(s32[96]{0:T(128)} %span_ref.11) | copy-start | bytes 1156
  26.7 15.9 %copy-start.1 = (s32[96]{0:T(128)S(1)}, s32[96]{0:T(128)}, u32[]{:S(2)}) copy-start(s32[96]{0:T(128)} %counts_ref.11) | copy-start | bytes 1156
  26.7 97.4 %all-to-all-start = ((bf16[8,384,384]{2,1,0:T(8,128)(2,1)}), bf16[8,384,384]{2,1,0:T(8,128)(2,1)S(1)}, u32[]{:S(2)}, u32[]{:S(2)}) async-start(bf16[8,384,384]{2,1,0:T(8,128)(2,1)} %column_blocks.1), calls=%async_computation | async-start | bytes 4718592 | tf_op jit(solution)/shard_map/all_to_all | solution.py:254
  33.9 22.5 %collective-permute-start.1 = (bf16[256,384]{1,0:T(8,128)(2,1)S(1)}, bf16[256,384]{1,0:T(8,128)(2,1)S(1)}, u32[]{:S(2)}, u32[]{:S(2)}) collective-permute-start(bf16[256,384]{1,0:T(8,128)(2,1)S(1)} %collective-permute-done.refs_2_), channel_id=1, source_target_pairs={{0,16},{8,24},{16,32},{24,40},{32,48},{40,56},{48,64},{56,72},{64,... | collective-permute-start | bytes 589832 | tf_op jit(solution)/shard_map/ppermute | solution.py:239
  38.2 21.6 %collective-permute-start.5 = (bf16[256,384]{1,0:T(8,128)(2,1)S(1)}, bf16[256,384]{1,0:T(8,128)(2,1)S(1)}, u32[]{:S(2)}, u32[]{:S(2)}) collective-permute-start(bf16[256,384]{1,0:T(8,128)(2,1)S(1)} %collective-permute-done.4.refs_3_), channel_id=1, source_target_pairs={{0,16},{8,24},{16,32},{24,40},{32,48},{40,56},{48,64},{56,72},{64,... | collective-permute-start | bytes 589832 | tf_op jit(solution)/shard_map/ppermute | solution.py:239
  49.0 23.1 %collective-permute-start.11 = (bf16[256,384]{1,0:T(8,128)(2,1)S(1)}, bf16[256,384]{1,0:T(8,128)(2,1)S(1)}, u32[]{:S(2)}, u32[]{:S(2)}) collective-permute-start(bf16[256,384]{1,0:T(8,128)(2,1)S(1)} %collective-permute-done.8.refs_4_), channel_id=1, source_target_pairs={{0,16},{8,24},{16,32},{24,40},{32,48},{40,56},{48,64},{56,72},{64,... | collective-permute-start | bytes 589832 | tf_op jit(solution)/shard_map/ppermute | solution.py:239
  53.0 19.1 %collective-permute-start.12 = (bf16[256,384]{1,0:T(8,128)(2,1)S(1)}, bf16[256,384]{1,0:T(8,128)(2,1)S(1)}, u32[]{:S(2)}, u32[]{:S(2)}) collective-permute-start(bf16[256,384]{1,0:T(8,128)(2,1)S(1)} %collective-permute-done.9.refs_5_), channel_id=1, source_target_pairs={{0,16},{8,24},{16,32},{24,40},{32,48},{40,56},{48,64},{56,72},{64,... | collective-permute-start | bytes 589832 | tf_op jit(solution)/shard_map/ppermute | solution.py:239
  56.4 19.6 %collective-permute-start.2 = (bf16[256,384]{1,0:T(8,128)(2,1)S(1)}, bf16[256,384]{1,0:T(8,128)(2,1)S(1)}, u32[]{:S(2)}, u32[]{:S(2)}) collective-permute-start(bf16[256,384]{1,0:T(8,128)(2,1)S(1)} %collective-permute-done.1.refs_2_), channel_id=1, source_target_pairs={{0,16},{8,24},{16,32},{24,40},{32,48},{40,56},{48,64},{56,72},{64,... | collective-permute-start | bytes 589832 | tf_op jit(solution)/shard_map/ppermute | solution.py:239
  59.8 17.5 %collective-permute-start.6 = (bf16[256,384]{1,0:T(8,128)(2,1)S(1)}, bf16[256,384]{1,0:T(8,128)(2,1)S(1)}, u32[]{:S(2)}, u32[]{:S(2)}) collective-permute-start(bf16[256,384]{1,0:T(8,128)(2,1)S(1)} %collective-permute-done.5.refs_3_), channel_id=1, source_target_pairs={{0,16},{8,24},{16,32},{24,40},{32,48},{40,56},{48,64},{56,72},{64,... | collective-permute-start | bytes 589832 | tf_op jit(solution)/shard_map/ppermute | solution.py:239
  72.2 15.4 %collective-permute-start.13 = (bf16[256,384]{1,0:T(8,128)(2,1)S(1)}, bf16[256,384]{1,0:T(8,128)(2,1)S(1)}, u32[]{:S(2)}, u32[]{:S(2)}) collective-permute-start(bf16[256,384]{1,0:T(8,128)(2,1)S(1)} %collective-permute-done.11.refs_4_), channel_id=1, source_target_pairs={{0,16},{8,24},{16,32},{24,40},{32,48},{40,56},{48,64},{56,72},{64,... | collective-permute-start | bytes 589832 | tf_op jit(solution)/shard_map/ppermute | solution.py:239
  74.1 13.5 %collective-permute-start.14 = (bf16[256,384]{1,0:T(8,128)(2,1)S(1)}, bf16[256,384]{1,0:T(8,128)(2,1)S(1)}, u32[]{:S(2)}, u32[]{:S(2)}) collective-permute-start(bf16[256,384]{1,0:T(8,128)(2,1)S(1)} %collective-permute-done.12.refs_5_), channel_id=1, source_target_pairs={{0,16},{8,24},{16,32},{24,40},{32,48},{40,56},{48,64},{56,72},{64,... | collective-permute-start | bytes 589832 | tf_op jit(solution)/shard_map/ppermute | solution.py:239
  76.0 26.0 %collective-permute-start.3 = (bf16[256,384]{1,0:T(8,128)(2,1)S(1)}, bf16[256,384]{1,0:T(8,128)(2,1)S(1)}, u32[]{:S(2)}, u32[]{:S(2)}) collective-permute-start(bf16[256,384]{1,0:T(8,128)(2,1)S(1)} %collective-permute-done.2.refs_1_), channel_id=1, source_target_pairs={{8,16},{24,32},{40,48},{56,64},{72,80},{88,96},{104,112},{120,128}... | collective-permute-start | bytes 589832 | tf_op jit(solution)/shard_map/ppermute | solution.py:239
  77.4 24.7 %collective-permute-start.7 = (bf16[256,384]{1,0:T(8,128)(2,1)S(1)}, bf16[256,384]{1,0:T(8,128)(2,1)S(1)}, u32[]{:S(2)}, u32[]{:S(2)}) collective-permute-start(bf16[256,384]{1,0:T(8,128)(2,1)S(1)} %collective-permute-done.6.refs_2_), channel_id=1, source_target_pairs={{8,16},{24,32},{40,48},{56,64},{72,80},{88,96},{104,112},{120,128}... | collective-permute-start | bytes 589832 | tf_op jit(solution)/shard_map/ppermute | solution.py:239
  87.6 14.4 %collective-permute-start.15 = (bf16[256,384]{1,0:T(8,128)(2,1)S(1)}, bf16[256,384]{1,0:T(8,128)(2,1)S(1)}, u32[]{:S(2)}, u32[]{:S(2)}) collective-permute-start(bf16[256,384]{1,0:T(8,128)(2,1)S(1)} %collective-permute-done.13.refs_3_), channel_id=1, source_target_pairs={{8,16},{24,32},{40,48},{56,64},{72,80},{88,96},{104,112},{120,128}... | collective-permute-start | bytes 589832 | tf_op jit(solution)/shard_map/ppermute | solution.py:239
  88.9 13.1 %collective-permute-start.16 = (bf16[256,384]{1,0:T(8,128)(2,1)S(1)}, bf16[256,384]{1,0:T(8,128)(2,1)S(1)}, u32[]{:S(2)}, u32[]{:S(2)}) collective-permute-start(bf16[256,384]{1,0:T(8,128)(2,1)S(1)} %collective-permute-done.14.refs_4_), channel_id=1, source_target_pairs={{8,16},{24,32},{40,48},{56,64},{72,80},{88,96},{104,112},{120,128}... | collective-permute-start | bytes 589832 | tf_op jit(solution)/shard_map/ppermute | solution.py:239
  94.7 7.3 %collective-permute-start.17 = (f32[3,512,256]{2,1,0:T(8,128)S(1)}, f32[3,512,256]{2,1,0:T(8,128)S(1)}, u32[]{:S(2)}, u32[]{:S(2)}) collective-permute-start(f32[3,512,256]{2,1,0:T(8,128)S(1)} %attend_3_other.1), channel_id=1, source_target_pairs={{0,8},{8,0},{16,24},{24,16},{32,40},{40,32},{48,56},{56,48},{64,72... | collective-permute-start | bytes 4718600 | tf_op jit(solution)/shard_map/ppermute | solution.py:239
  107.9 10.4 %collective-permute-start.20 = (bf16[512,384]{1,0:T(8,128)(2,1)S(1)}, bf16[512,384]{1,0:T(8,128)(2,1)S(1)}, u32[]{:S(2)}, u32[]{:S(2)}) collective-permute-start(bf16[512,384]{1,0:T(8,128)(2,1)S(1)} %finish.1.refs_0_), channel_id=1, source_target_pairs={{0,7},{1,0},{2,1},{3,2},{4,3},{5,4},{6,5},{7,6},{8,15},{9,8},{10,9... | collective-permute-start | bytes 1179656 | tf_op jit(solution)/shard_map/ppermute | solution.py:239
  113.1 11.5 %collective-permute-start.18 = (bf16[512,384]{1,0:T(8,128)(2,1)S(1)}, bf16[512,384]{1,0:T(8,128)(2,1)}, u32[]{:S(2)}, u32[]{:S(2)}) collective-permute-start(bf16[512,384]{1,0:T(8,128)(2,1)S(1)} %finish.1.refs_0_), channel_id=1, source_target_pairs={{0,1},{1,2},{2,3},{3,4},{4,5},{5,6},{6,7},{7,0},{8,9},{9,10},{10,1... | collective-permute-start | bytes 1179656 | tf_op jit(solution)/shard_map/ppermute | solution.py:239
  118.4 10.9 %collective-permute-start.22 = (bf16[512,384]{1,0:T(8,128)(2,1)S(1)}, bf16[512,384]{1,0:T(8,128)(2,1)S(1)}, u32[]{:S(2)}, u32[]{:S(2)}) collective-permute-start(bf16[512,384]{1,0:T(8,128)(2,1)S(1)} %collective-permute-done.20.refs_2_), channel_id=1, source_target_pairs={{0,7},{1,0},{2,1},{3,2},{4,3},{5,4},{6,5},{7,6},{8,15},{9,8},{10,9... | collective-permute-start | bytes 1179656 | tf_op jit(solution)/shard_map/ppermute | solution.py:239
  124.6 11.9 %collective-permute-start.19 = (bf16[512,384]{1,0:T(8,128)(2,1)}, bf16[512,384]{1,0:T(8,128)(2,1)S(1)}, u32[]{:S(2)}, u32[]{:S(2)}) collective-permute-start(bf16[512,384]{1,0:T(8,128)(2,1)} %collective-permute-done.18.refs_1_), channel_id=1, source_target_pairs={{0,1},{1,2},{2,3},{3,4},{4,5},{5,6},{6,7},{7,0},{8,9},{9,10},{10,1... | collective-permute-start | bytes 1179656 | tf_op jit(solution)/shard_map/ppermute | solution.py:239
  129.2 12.0 %collective-permute-start.23 = (bf16[512,384]{1,0:T(8,128)(2,1)S(1)}, bf16[512,384]{1,0:T(8,128)(2,1)S(1)}, u32[]{:S(2)}, u32[]{:S(2)}) collective-permute-start(bf16[512,384]{1,0:T(8,128)(2,1)S(1)} %collective-permute-done.22.refs_2_), channel_id=1, source_target_pairs={{0,7},{1,0},{2,1},{3,2},{4,3},{5,4},{6,5},{7,6},{8,15},{9,8},{10,9... | collective-permute-start | bytes 1179656 | tf_op jit(solution)/shard_map/ppermute | solution.py:239
  136.5 12.3 %collective-permute-start.21 = (bf16[512,384]{1,0:T(8,128)(2,1)S(1)}, bf16[512,384]{1,0:T(8,128)(2,1)S(1)}, u32[]{:S(2)}, u32[]{:S(2)}) collective-permute-start(bf16[512,384]{1,0:T(8,128)(2,1)S(1)} %collective-permute-done.19.refs_1_), channel_id=1, source_target_pairs={{0,1},{1,2},{2,3},{3,4},{4,5},{5,6},{6,7},{7,0},{8,9},{9,10},{10,1... | collective-permute-start | bytes 1179656 | tf_op jit(solution)/shard_map/ppermute | solution.py:239
  141.2 10.2 %collective-permute-start.25 = (bf16[256,384]{1,0:T(8,128)(2,1)S(1)}, bf16[256,384]{1,0:T(8,128)(2,1)S(1)}, u32[]{:S(2)}, u32[]{:S(2)}) collective-permute-start(bf16[256,384]{1,0:T(8,128)(2,1)S(1)} %slice.24), channel_id=1, source_target_pairs={{0,7},{1,0},{2,1},{3,2},{4,3},{5,4},{6,5},{7,6},{8,15},{9,8},{10,9... | collective-permute-start | bytes 589832 | tf_op jit(solution)/shard_map/ppermute | solution.py:239
  148.8 8.8 %collective-permute-start.24 = (bf16[256,384]{1,0:T(8,128)(2,1)S(1)}, bf16[256,384]{1,0:T(8,128)(2,1)S(1)}, u32[]{:S(2)}, u32[]{:S(2)}) collective-permute-start(bf16[256,384]{1,0:T(8,128)(2,1)S(1)} %slice.22), channel_id=1, source_target_pairs={{0,1},{1,2},{2,3},{3,4},{4,5},{5,6},{6,7},{7,0},{8,9},{9,10},{10,1... | collective-permute-start | bytes 589832 | tf_op jit(solution)/shard_map/ppermute | solution.py:239

commit v7 on v5

--- a/solution.py
+++ b/solution.py
@@ -204,9 +204,7 @@
             in_specs=[pl.BlockSpec(x.shape, lambda i, g, n=x.ndim: (0,) * n) for x in operands],
             out_specs=pl.BlockSpec((per_frame, columns), lambda i, g: (0, 0)),
         ),
-        cost_estimate=pl.CostEstimate(
-            flops=len(pieces) * per_frame * weight.shape[1] * columns, transcendentals=0, bytes_accessed=4 << 20
-        ),
+        cost_estimate=LONG,
         compiler_params=pltpu.CompilerParams(vmem_limit_bytes=LARGE_VMEM),
         name=name,
     )(group, *operands)
@@ -240,10 +238,8 @@
     blocks = column_blocks(out_weight, groups)
     weight = lax.all_to_all(blocks, "head", split_axis=0, concat_axis=0, tiled=True)
     parts = attend([(in_hbm(keys), in_hbm(values))], (0, 1), (0,), None, "attend_0")
-    k1, parts = after((k1, parts))
     k2, v2 = send(k1, by_chip), send(v1, by_chip)
     parts = attend([(k1, v1)], (0, 1), (1,), parts, "attend_1")
-    k2, parts = after((k2, parts))
     k3, v3 = send(k2, by_chip), send(v2, by_chip)
     own, other = attend([(k2, v2)], (0, 1), (2,), parts, "attend_2")
     k3, v3, own, other = after((k3, v3, own, other))
@@ -263,7 +259,6 @@
         up, down = send(up, upward, "head"), send(down, downward, "head")
         total = project(total, held, places, jnp.float32, f"project_{step - 1}")
         held, places = [up, down], [(None, groups - step), (None, step)]
-        down, total = after((down, total))
     far = [send(up[:half], upward, "head"), send(down[half:], downward, "head")]
     total = project(total, held, places, jnp.float32, "project_3")
     return project(total, far, [(0, 4), (1, 4)], jnp.bfloat16, "project_4")

time: 142 us -> 148 us (1.042)
  Pallas kernels: 29.8 us -> 38.1 us
  waiting for transfers between devices: 51.6 us -> 45.4 us
  local copies, waits for them, and re-layouts: 0.05 us -> 3.6 us
    ppermute x18, waiting for transfers between devices: 51.6 us -> 45.4 us  [send(): return lax.ppermute(block, axis, route)]
    pallas_call x5, Pallas kernels: 19.3 us -> 24.7 us  [attention_call(): pl.pallas_call(_attention_body(sides, hops, states is None), out_shape=[j...]
    unnamed x4 -> x12, local copies, waits for them, and re-layouts: 0.01 us -> 2.18 us
    pallas_call x1, Pallas kernels: 3.28 us -> 4.99 us  [finish_call(): pl.pallas_call(_finish_body, out_shape=jax.ShapeDtypeStruct((per_frame, w...]
  transfers between devices with their start and end apart: 19 -> 19, of which waited for: 12 -> 11; matrix products, arithmetic and copies ran while one was open for 0% -> 1% of each run, Pallas kernels for 20% -> 24%
where the time goes in v7:
time: 148 us; the launch traced here: 147 us
  starting transfers between devices  59.9 us (40%)
  waiting for transfers between devices  45.4 us (31%)
  Pallas kernels  38.1 us (26%)
  local copies, waits for them, and re-layouts  3.6 us (2%)
    ppermute x18, starting transfers between devices, send(): return lax.ppermute(block, axis, route)  52.5 us
    ppermute x18, waiting for transfers between devices, send(): return lax.ppermute(block, axis, route)  45.4 us
    pallas_call x5, Pallas kernels, attention_call(): pl.pallas_call(_attention_body(sides, hops, states is None), out_shape=[j...  24.7 us
    all_to_all x1, starting transfers between devices, on_device(): lax.all_to_all(blocks, 'head', split_axis=0, concat_axis=0, tiled=True)  7.45 us
    pallas_call x5, Pallas kernels, project_call(): pl.pallas_call(_project_body(places, base is not None), out_shape=jax.Sha...  5.6 us
    pallas_call x1, Pallas kernels, finish_call(): pl.pallas_call(_finish_body, out_shape=jax.ShapeDtypeStruct((per_frame, w...  4.99 us
  transfers between devices with their start and end apart: 19, of which 11 were waited for; matrix products, arithmetic and copies ran while one was open for 1% of the time, Pallas kernels for 24%

profile of v7, /device:TPU:30, one launch (start us, length us, event | category | flops | bytes accessed | tf_op | source)
XLA Modules:
  0.0 147.4 jit_solution(10359691958389790840)
XLA Ops:
  0.0 4.3 %collective-permute-start = (bf16[512,384]{1,0:T(8,128)(2,1)}, bf16[512,384]{1,0:T(8,128)(2,1)S(1)}, u32[]{:S(2)}, u32[]{:S(2)}) collective-permute-start(bf16[512,384]{1,0:T(8,128)(2,1)} %refs_2_.1), channel_id=1, source_target_pairs={{0,16},{8,24},{16,32},{24,40},{32,48},{40,56},{48,64},{56,72},{64,... | collective-permute-start | bytes 1179656 | tf_op jit(solution)/shard_map/ppermute | solution.py:228
  4.3 4.3 %collective-permute-start.3 = (bf16[512,384]{1,0:T(8,128)(2,1)}, bf16[512,384]{1,0:T(8,128)(2,1)S(1)}, u32[]{:S(2)}, u32[]{:S(2)}) collective-permute-start(bf16[512,384]{1,0:T(8,128)(2,1)} %refs_3_.1), channel_id=1, source_target_pairs={{0,16},{8,24},{16,32},{24,40},{32,48},{40,56},{48,64},{56,72},{64,... | collective-permute-start | bytes 1179656 | tf_op jit(solution)/shard_map/ppermute | solution.py:228
  8.6 1.9 %collective-permute-start.6 = (bf16[512,384]{1,0:T(8,128)(2,1)}, bf16[512,384]{1,0:T(8,128)(2,1)S(1)}, u32[]{:S(2)}, u32[]{:S(2)}) collective-permute-start(bf16[512,384]{1,0:T(8,128)(2,1)} %q_ref.1), channel_id=1, source_target_pairs={{0,8},{8,0},{16,24},{24,16},{32,40},{40,32},{48,56},{56,48},{64,72... | collective-permute-start | bytes 1179656 | tf_op jit(solution)/shard_map/ppermute | solution.py:228
  10.5 2.8 %column_blocks.1 = bf16[8,384,384]{2,1,0:T(8,128)(2,1)} custom-call(bf16[384,3072]{1,0:T(8,128)(2,1)} %w_ref.1), custom_call_target="tpu_custom_call" | custom-call | flops 1 | bytes 1 | tf_op jit(solution)/shard_map/column_blocks/pallas_call | solution.py:165
  13.3 7.5 %all-to-all-start = ((bf16[8,384,384]{2,1,0:T(8,128)(2,1)}), bf16[8,384,384]{2,1,0:T(8,128)(2,1)S(1)}, u32[]{:S(2)}, u32[]{:S(2)}) async-start(bf16[8,384,384]{2,1,0:T(8,128)(2,1)} %column_blocks.1), calls=%async_computation | async-start | bytes 4718592 | tf_op jit(solution)/shard_map/all_to_all | solution.py:239
  20.8 4.2 %collective-permute-done.refs_2_ = bf16[512,384]{1,0:T(8,128)(2,1)S(1)} collective-permute-done((bf16[512,384]{1,0:T(8,128)(2,1)}, bf16[512,384]{1,0:T(8,128)(2,1)S(1)}, u32[]{:S(2)}, u32[]{:S(2)}) %collective-permute-start) | collective-permute-done | bytes 393248 | tf_op jit(solution)/shard_map/ppermute | solution.py:228
  25.0 1.9 %collective-permute-start.1 = (bf16[512,384]{1,0:T(8,128)(2,1)S(1)}, bf16[512,384]{1,0:T(8,128)(2,1)S(1)}, u32[]{:S(2)}, u32[]{:S(2)}) collective-permute-start(bf16[512,384]{1,0:T(8,128)(2,1)S(1)} %collective-permute-done.refs_2_), channel_id=1, source_target_pairs={{0,16},{8,24},{16,32},{24,40},{32,48},{40,56},{48,64},{56,72},{64,... | collective-permute-start | bytes 1179656 | tf_op jit(solution)/shard_map/ppermute | solution.py:228
  26.9 6.5 %collective-permute-done.3.refs_3_ = bf16[512,384]{1,0:T(8,128)(2,1)S(1)} collective-permute-done((bf16[512,384]{1,0:T(8,128)(2,1)}, bf16[512,384]{1,0:T(8,128)(2,1)S(1)}, u32[]{:S(2)}, u32[]{:S(2)}) %collective-permute-start.3) | collective-permute-done | bytes 393248 | tf_op jit(solution)/shard_map/ppermute | solution.py:228
  33.4 1.9 %collective-permute-start.4 = (bf16[512,384]{1,0:T(8,128)(2,1)S(1)}, bf16[512,384]{1,0:T(8,128)(2,1)S(1)}, u32[]{:S(2)}, u32[]{:S(2)}) collective-permute-start(bf16[512,384]{1,0:T(8,128)(2,1)S(1)} %collective-permute-done.3.refs_3_), channel_id=1, source_target_pairs={{0,16},{8,24},{16,32},{24,40},{32,48},{40,56},{48,64},{56,72},{64,... | collective-permute-start | bytes 1179656 | tf_op jit(solution)/shard_map/ppermute | solution.py:228
  35.4 6.5 %attend_0.1 = (f32[3,512,256]{2,1,0:T(8,128)S(1)}, f32[3,512,256]{2,1,0:T(8,128)S(1)}) custom-call(s32[1]{0:T(128)} %bitcast.1.frame_ref, s32[96]{0:T(128)S(1)} %copy-done, s32[96]{0:T(128)S(1)} %copy-done.1, bf16[512,384]{1,0:T(8,128)(2,1)} %q_ref.1, bf16[512,384]{1,0:T(8,128)(2,1)S(1)} %collective-permute-done.6.refs_1_.refs_0_, bf16[512,384]{1,0:T(8,128)(2,1)} %refs_2_.1, ...), custom_call_target="tpu_custom_call" | custom-call | flops 17179869184 | bytes 1 | tf_op jit(solution)/shard_map/attend_0/pallas_call | solution.py:108
  41.8 7.2 %attend_1.1 = (f32[3,512,256]{2,1,0:T(8,128)S(1)}, f32[3,512,256]{2,1,0:T(8,128)S(1)}) custom-call(s32[1]{0:T(128)} %bitcast.1.frame_ref, s32[96]{0:T(128)S(1)} %copy-done, s32[96]{0:T(128)S(1)} %copy-done.1, bf16[512,384]{1,0:T(8,128)(2,1)} %q_ref.1, bf16[512,384]{1,0:T(8,128)(2,1)S(1)} %collective-permute-done.6.refs_1_.refs_0_, ...), custom_call_target="tpu_custom_call" | custom-call | flops 17179869184 | bytes 1 | tf_op jit(solution)/shard_map/attend_1/pallas_call | solution.py:108
  49.0 1.9 %collective-permute-start.2 = (bf16[512,384]{1,0:T(8,128)(2,1)S(1)}, bf16[512,384]{1,0:T(8,128)(2,1)S(1)}, u32[]{:S(2)}, u32[]{:S(2)}) collective-permute-start(bf16[512,384]{1,0:T(8,128)(2,1)S(1)} %collective-permute-done.1.refs_2_), channel_id=1, source_target_pairs={{0,16},{8,24},{16,32},{24,40},{32,48},{40,56},{48,64},{56,72},{64,... | collective-permute-start | bytes 1179656 | tf_op jit(solution)/shard_map/ppermute | solution.py:228
  51.0 1.9 %collective-permute-start.5 = (bf16[512,384]{1,0:T(8,128)(2,1)S(1)}, bf16[512,384]{1,0:T(8,128)(2,1)S(1)}, u32[]{:S(2)}, u32[]{:S(2)}) collective-permute-start(bf16[512,384]{1,0:T(8,128)(2,1)S(1)} %collective-permute-done.4.refs_3_), channel_id=1, source_target_pairs={{0,16},{8,24},{16,32},{24,40},{32,48},{40,56},{48,64},{56,72},{64,... | collective-permute-start | bytes 1179656 | tf_op jit(solution)/shard_map/ppermute | solution.py:228
  52.9 5.1 %attend_2.1 = (f32[3,512,256]{2,1,0:T(8,128)S(1)}, f32[3,512,256]{2,1,0:T(8,128)S(1)}) custom-call(s32[1]{0:T(128)} %bitcast.1.frame_ref, s32[96]{0:T(128)S(1)} %copy-done, s32[96]{0:T(128)S(1)} %copy-done.1, bf16[512,384]{1,0:T(8,128)(2,1)} %q_ref.1, bf16[512,384]{1,0:T(8,128)(2,1)S(1)} %collective-permute-done.6.refs_1_.refs_0_, ...), custom_call_target="tpu_custom_call" | custom-call | flops 17179869184 | bytes 1 | tf_op jit(solution)/shard_map/attend_2/pallas_call | solution.py:108
  58.0 6.7 %collective-permute-done.2.refs_1_ = bf16[512,384]{1,0:T(8,128)(2,1)S(1)} collective-permute-done((bf16[512,384]{1,0:T(8,128)(2,1)S(1)}, bf16[512,384]{1,0:T(8,128)(2,1)S(1)}, u32[]{:S(2)}, u32[]{:S(2)}) %collective-permute-start.2) | collective-permute-done | bytes 393248 | tf_op jit(solution)/shard_map/ppermute | solution.py:228
  64.7 4.2 %collective-permute-done.5.refs_2_ = bf16[512,384]{1,0:T(8,128)(2,1)S(1)} collective-permute-done((bf16[512,384]{1,0:T(8,128)(2,1)S(1)}, bf16[512,384]{1,0:T(8,128)(2,1)S(1)}, u32[]{:S(2)}, u32[]{:S(2)}) %collective-permute-start.5) | collective-permute-done | bytes 393248 | tf_op jit(solution)/shard_map/ppermute | solution.py:228
  73.1 3.0 %collective-permute-start.9 = (f32[3,512,256]{2,1,0:T(8,128)S(1)}, f32[3,512,256]{2,1,0:T(8,128)S(1)}, u32[]{:S(2)}, u32[]{:S(2)}) collective-permute-start(f32[3,512,256]{2,1,0:T(8,128)S(1)} %attend_3_other.1), channel_id=1, source_target_pairs={{0,8},{8,0},{16,24},{24,16},{32,40},{40,32},{48,56},{56,48},{64,72... | collective-permute-start | bytes 4718600 | tf_op jit(solution)/shard_map/ppermute | solution.py:228
  76.1 4.4 %attend_3_own.1.own = f32[3,512,256]{2,1,0:T(8,128)S(1)} custom-call(s32[1]{0:T(128)} %bitcast.1.frame_ref, s32[96]{0:T(128)S(1)} %copy-done, s32[96]{0:T(128)S(1)} %copy-done.1, bf16[512,384]{1,0:T(8,128)(2,1)} %q_ref.1, bf16[512,384]{1,0:T(8,128)(2,1)S(1)} %collective-permute-done.2.refs_1_, bf16[512,384]{1,0:T(8,128)(2,1)S(1)} %collective-permute-done.5.refs_2_, ...), custom_call_target="tpu_custom_call" | custom-call | flops 17179869184 | bytes 1 | tf_op jit(solution)/shard_map/attend_3_own/pallas_call | solution.py:108
  80.5 3.8 %collective-permute-done.8.v_ref = bf16[512,384]{1,0:T(8,128)(2,1)S(1)} collective-permute-done((bf16[512,384]{1,0:T(8,128)(2,1)S(1)}, bf16[512,384]{1,0:T(8,128)(2,1)S(1)}, u32[]{:S(2)}, u32[]{:S(2)}) %collective-permute-start.8) | collective-permute-done | bytes 393248 | tf_op jit(solution)/shard_map/ppermute | solution.py:228
  84.3 5.0 %finish.1.refs_0_ = bf16[512,384]{1,0:T(8,128)(2,1)S(1)} custom-call(s32[1]{0:T(128)} %bitcast.1.frame_ref, s32[96]{0:T(128)S(1)} %copy-done, s32[96]{0:T(128)S(1)} %copy-done.1, bf16[512,384]{1,0:T(8,128)(2,1)} %q_ref.1, bf16[512,384]{1,0:T(8,128)(2,1)S(1)} %collective-permute-done.7.k_ref, bf16[512,384]{1,0:T(8,128)(2,1)S(1)} %collective-permute-done.8.v_ref, ...), custom_call_target="tpu_custom_call" | custom-call | flops 1 | bytes 1 | tf_op jit(solution)/shard_map/finish/pallas_call | solution.py:136
  89.3 4.7 %collective-permute-start.10 = (bf16[512,384]{1,0:T(8,128)(2,1)S(1)}, bf16[512,384]{1,0:T(8,128)(2,1)S(1)}, u32[]{:S(2)}, u32[]{:S(2)}) collective-permute-start(bf16[512,384]{1,0:T(8,128)(2,1)S(1)} %finish.1.refs_0_), channel_id=1, source_target_pairs={{0,1},{1,2},{2,3},{3,4},{4,5},{5,6},{6,7},{7,0},{8,9},{9,10},{10,1... | collective-permute-start | bytes 1179656 | tf_op jit(solution)/shard_map/ppermute | solution.py:228
  94.0 1.9 %collective-permute-start.11 = (bf16[512,384]{1,0:T(8,128)(2,1)S(1)}, bf16[512,384]{1,0:T(8,128)(2,1)S(1)}, u32[]{:S(2)}, u32[]{:S(2)}) collective-permute-start(bf16[512,384]{1,0:T(8,128)(2,1)S(1)} %finish.1.refs_0_), channel_id=1, source_target_pairs={{0,7},{1,0},{2,1},{3,2},{4,3},{5,4},{6,5},{7,6},{8,15},{9,8},{10,9... | collective-permute-start | bytes 1179656 | tf_op jit(solution)/shard_map/ppermute | solution.py:228
  96.0 5.6 %collective-permute-done.10.refs_1_ = bf16[512,384]{1,0:T(8,128)(2,1)S(1)} collective-permute-done((bf16[512,384]{1,0:T(8,128)(2,1)S(1)}, bf16[512,384]{1,0:T(8,128)(2,1)S(1)}, u32[]{:S(2)}, u32[]{:S(2)}) %collective-permute-start.10) | collective-permute-done | bytes 393248 | tf_op jit(solution)/shard_map/ppermute | solution.py:228
  101.6 5.3 %collective-permute-start.12 = (bf16[512,384]{1,0:T(8,128)(2,1)S(1)}, bf16[512,384]{1,0:T(8,128)(2,1)}, u32[]{:S(2)}, u32[]{:S(2)}) collective-permute-start(bf16[512,384]{1,0:T(8,128)(2,1)S(1)} %collective-permute-done.10.refs_1_), channel_id=1, source_target_pairs={{0,1},{1,2},{2,3},{3,4},{4,5},{5,6},{6,7},{7,0},{8,9},{9,10},{10,1... | collective-permute-start | bytes 1179656 | tf_op jit(solution)/shard_map/ppermute | solution.py:228
  107.7 1.9 %collective-permute-start.13 = (bf16[512,384]{1,0:T(8,128)(2,1)S(1)}, bf16[512,384]{1,0:T(8,128)(2,1)}, u32[]{:S(2)}, u32[]{:S(2)}) collective-permute-start(bf16[512,384]{1,0:T(8,128)(2,1)S(1)} %collective-permute-done.11.refs_2_), channel_id=1, source_target_pairs={{0,7},{1,0},{2,1},{3,2},{4,3},{5,4},{6,5},{7,6},{8,15},{9,8},{10,9... | collective-permute-start | bytes 1179656 | tf_op jit(solution)/shard_map/ppermute | solution.py:228
  110.3 4.6 %collective-permute-done.12.refs_1_ = bf16[512,384]{1,0:T(8,128)(2,1)} collective-permute-done((bf16[512,384]{1,0:T(8,128)(2,1)S(1)}, bf16[512,384]{1,0:T(8,128)(2,1)}, u32[]{:S(2)}, u32[]{:S(2)}) %collective-permute-start.12) | collective-permute-done | bytes 393248 | tf_op jit(solution)/shard_map/ppermute | solution.py:228
  115.0 5.7 %collective-permute-start.14 = (bf16[512,384]{1,0:T(8,128)(2,1)}, bf16[512,384]{1,0:T(8,128)(2,1)S(1)}, u32[]{:S(2)}, u32[]{:S(2)}) collective-permute-start(bf16[512,384]{1,0:T(8,128)(2,1)} %collective-permute-done.12.refs_1_), channel_id=1, source_target_pairs={{0,1},{1,2},{2,3},{3,4},{4,5},{5,6},{6,7},{7,0},{8,9},{9,10},{10,1... | collective-permute-start | bytes 1179656 | tf_op jit(solution)/shard_map/ppermute | solution.py:228
  124.2 4.2 %collective-permute-done.14.refs_1_ = bf16[512,384]{1,0:T(8,128)(2,1)S(1)} collective-permute-done((bf16[512,384]{1,0:T(8,128)(2,1)}, bf16[512,384]{1,0:T(8,128)(2,1)S(1)}, u32[]{:S(2)}, u32[]{:S(2)}) %collective-permute-start.14) | collective-permute-done | bytes 393248 | tf_op jit(solution)/shard_map/ppermute | solution.py:228
  129.1 5.5 %collective-permute-start.16 = (bf16[256,384]{1,0:T(8,128)(2,1)}, bf16[256,384]{1,0:T(8,128)(2,1)}, u32[]{:S(2)}, u32[]{:S(2)}) collective-permute-start(bf16[256,384]{1,0:T(8,128)(2,1)} %slice.8), channel_id=1, source_target_pairs={{0,1},{1,2},{2,3},{3,4},{4,5},{5,6},{6,7},{7,0},{8,9},{9,10},{10,1... | collective-permute-start | bytes 589832 | tf_op jit(solution)/shard_map/ppermute | solution.py:228
  136.2 1.9 %collective-permute-start.17 = (bf16[256,384]{1,0:T(8,128)(2,1)}, bf16[256,384]{1,0:T(8,128)(2,1)}, u32[]{:S(2)}, u32[]{:S(2)}) collective-permute-start(bf16[256,384]{1,0:T(8,128)(2,1)} %slice.9), channel_id=1, source_target_pairs={{0,7},{1,0},{2,1},{3,2},{4,3},{5,4},{6,5},{7,6},{8,15},{9,8},{10,9... | collective-permute-start | bytes 589832 | tf_op jit(solution)/shard_map/ppermute | solution.py:228
  142.3 3.0 %collective-permute-done.17.refs_2_ = bf16[256,384]{1,0:T(8,128)(2,1)} collective-permute-done((bf16[256,384]{1,0:T(8,128)(2,1)}, bf16[256,384]{1,0:T(8,128)(2,1)}, u32[]{:S(2)}, u32[]{:S(2)}) %collective-permute-start.17) | collective-permute-done | bytes 196640 | tf_op jit(solution)/shard_map/ppermute | solution.py:228
  145.2 2.2 %project_4.1 = bf16[512,384]{1,0:T(8,128)(2,1)} custom-call(s32[1]{0:T(128)} %bitcast.group_ref, f32[512,384]{1,0:T(8,128)S(1)} %project_3.1.refs_0_, bf16[256,384]{1,0:T(8,128)(2,1)} %collective-permute-done.16.refs_1_, bf16[256,384]{1,0:T(8,128)(2,1)} %collective-permute-done.17.refs_2_, bf16[8,384,384]{2,1,0:T(8,128)(2,1)S(1)} %all-to-all-done.refs_1_.refs_3_), custom_call_target="tpu_custom_call" | custom-call | flops 17179869184 | bytes 1 | tf_op jit(solution)/shard_map/project_4/pallas_call | solution.py:198
  (32 shorter events, 15.6 us)
Async XLA Ops:
  0.0 25.0 %collective-permute-start = (bf16[512,384]{1,0:T(8,128)(2,1)}, bf16[512,384]{1,0:T(8,128)(2,1)S(1)}, u32[]{:S(2)}, u32[]{:S(2)}) collective-permute-start(bf16[512,384]{1,0:T(8,128)(2,1)} %refs_2_.1), channel_id=1, source_target_pairs={{0,16},{8,24},{16,32},{24,40},{32,48},{40,56},{48,64},{56,72},{64,... | collective-permute-start | bytes 1179656 | tf_op jit(solution)/shard_map/ppermute | solution.py:228
  4.3 29.1 %collective-permute-start.3 = (bf16[512,384]{1,0:T(8,128)(2,1)}, bf16[512,384]{1,0:T(8,128)(2,1)S(1)}, u32[]{:S(2)}, u32[]{:S(2)}) collective-permute-start(bf16[512,384]{1,0:T(8,128)(2,1)} %refs_3_.1), channel_id=1, source_target_pairs={{0,16},{8,24},{16,32},{24,40},{32,48},{40,56},{48,64},{56,72},{64,... | collective-permute-start | bytes 1179656 | tf_op jit(solution)/shard_map/ppermute | solution.py:228
  8.6 26.8 %collective-permute-start.6 = (bf16[512,384]{1,0:T(8,128)(2,1)}, bf16[512,384]{1,0:T(8,128)(2,1)S(1)}, u32[]{:S(2)}, u32[]{:S(2)}) collective-permute-start(bf16[512,384]{1,0:T(8,128)(2,1)} %q_ref.1), channel_id=1, source_target_pairs={{0,8},{8,0},{16,24},{24,16},{32,40},{40,32},{48,56},{56,48},{64,72... | collective-permute-start | bytes 1179656 | tf_op jit(solution)/shard_map/ppermute | solution.py:228
  13.3 22.0 %copy-start = (s32[96]{0:T(128)S(1)}, s32[96]{0:T(128)}, u32[]{:S(2)}) copy-start(s32[96]{0:T(128)} %span_ref.11) | copy-start | bytes 1156
  13.3 22.0 %copy-start.1 = (s32[96]{0:T(128)S(1)}, s32[96]{0:T(128)}, u32[]{:S(2)}) copy-start(s32[96]{0:T(128)} %counts_ref.11) | copy-start | bytes 1156
  13.3 124.8 %all-to-all-start = ((bf16[8,384,384]{2,1,0:T(8,128)(2,1)}), bf16[8,384,384]{2,1,0:T(8,128)(2,1)S(1)}, u32[]{:S(2)}, u32[]{:S(2)}) async-start(bf16[8,384,384]{2,1,0:T(8,128)(2,1)} %column_blocks.1), calls=%async_computation | async-start | bytes 4718592 | tf_op jit(solution)/shard_map/all_to_all | solution.py:239
  25.0 24.0 %collective-permute-start.1 = (bf16[512,384]{1,0:T(8,128)(2,1)S(1)}, bf16[512,384]{1,0:T(8,128)(2,1)S(1)}, u32[]{:S(2)}, u32[]{:S(2)}) collective-permute-start(bf16[512,384]{1,0:T(8,128)(2,1)S(1)} %collective-permute-done.refs_2_), channel_id=1, source_target_pairs={{0,16},{8,24},{16,32},{24,40},{32,48},{40,56},{48,64},{56,72},{64,... | collective-permute-start | bytes 1179656 | tf_op jit(solution)/shard_map/ppermute | solution.py:228
  33.4 17.5 %collective-permute-start.4 = (bf16[512,384]{1,0:T(8,128)(2,1)S(1)}, bf16[512,384]{1,0:T(8,128)(2,1)S(1)}, u32[]{:S(2)}, u32[]{:S(2)}) collective-permute-start(bf16[512,384]{1,0:T(8,128)(2,1)S(1)} %collective-permute-done.3.refs_3_), channel_id=1, source_target_pairs={{0,16},{8,24},{16,32},{24,40},{32,48},{40,56},{48,64},{56,72},{64,... | collective-permute-start | bytes 1179656 | tf_op jit(solution)/shard_map/ppermute | solution.py:228
  49.0 15.7 %collective-permute-start.2 = (bf16[512,384]{1,0:T(8,128)(2,1)S(1)}, bf16[512,384]{1,0:T(8,128)(2,1)S(1)}, u32[]{:S(2)}, u32[]{:S(2)}) collective-permute-start(bf16[512,384]{1,0:T(8,128)(2,1)S(1)} %collective-permute-done.1.refs_2_), channel_id=1, source_target_pairs={{0,16},{8,24},{16,32},{24,40},{32,48},{40,56},{48,64},{56,72},{64,... | collective-permute-start | bytes 1179656 | tf_op jit(solution)/shard_map/ppermute | solution.py:228
  51.0 18.0 %collective-permute-start.5 = (bf16[512,384]{1,0:T(8,128)(2,1)S(1)}, bf16[512,384]{1,0:T(8,128)(2,1)S(1)}, u32[]{:S(2)}, u32[]{:S(2)}) collective-permute-start(bf16[512,384]{1,0:T(8,128)(2,1)S(1)} %collective-permute-done.4.refs_3_), channel_id=1, source_target_pairs={{0,16},{8,24},{16,32},{24,40},{32,48},{40,56},{48,64},{56,72},{64,... | collective-permute-start | bytes 1179656 | tf_op jit(solution)/shard_map/ppermute | solution.py:228
  68.9 11.6 %collective-permute-start.7 = (bf16[512,384]{1,0:T(8,128)(2,1)S(1)}, bf16[512,384]{1,0:T(8,128)(2,1)S(1)}, u32[]{:S(2)}, u32[]{:S(2)}) collective-permute-start(bf16[512,384]{1,0:T(8,128)(2,1)S(1)} %collective-permute-done.2.refs_1_), channel_id=1, source_target_pairs={{8,16},{24,32},{40,48},{56,64},{72,80},{88,96},{104,112},{120,128}... | collective-permute-start | bytes 1179656 | tf_op jit(solution)/shard_map/ppermute | solution.py:228
  70.2 14.1 %collective-permute-start.8 = (bf16[512,384]{1,0:T(8,128)(2,1)S(1)}, bf16[512,384]{1,0:T(8,128)(2,1)S(1)}, u32[]{:S(2)}, u32[]{:S(2)}) collective-permute-start(bf16[512,384]{1,0:T(8,128)(2,1)S(1)} %collective-permute-done.5.refs_2_), channel_id=1, source_target_pairs={{8,16},{24,32},{40,48},{56,64},{72,80},{88,96},{104,112},{120,128}... | collective-permute-start | bytes 1179656 | tf_op jit(solution)/shard_map/ppermute | solution.py:228
  73.1 11.2 %collective-permute-start.9 = (f32[3,512,256]{2,1,0:T(8,128)S(1)}, f32[3,512,256]{2,1,0:T(8,128)S(1)}, u32[]{:S(2)}, u32[]{:S(2)}) collective-permute-start(f32[3,512,256]{2,1,0:T(8,128)S(1)} %attend_3_other.1), channel_id=1, source_target_pairs={{0,8},{8,0},{16,24},{24,16},{32,40},{40,32},{48,56},{56,48},{64,72... | collective-permute-start | bytes 4718600 | tf_op jit(solution)/shard_map/ppermute | solution.py:228
  89.3 12.3 %collective-permute-start.10 = (bf16[512,384]{1,0:T(8,128)(2,1)S(1)}, bf16[512,384]{1,0:T(8,128)(2,1)S(1)}, u32[]{:S(2)}, u32[]{:S(2)}) collective-permute-start(bf16[512,384]{1,0:T(8,128)(2,1)S(1)} %finish.1.refs_0_), channel_id=1, source_target_pairs={{0,1},{1,2},{2,3},{3,4},{4,5},{5,6},{6,7},{7,0},{8,9},{9,10},{10,1... | collective-permute-start | bytes 1179656 | tf_op jit(solution)/shard_map/ppermute | solution.py:228
  94.0 13.6 %collective-permute-start.11 = (bf16[512,384]{1,0:T(8,128)(2,1)S(1)}, bf16[512,384]{1,0:T(8,128)(2,1)S(1)}, u32[]{:S(2)}, u32[]{:S(2)}) collective-permute-start(bf16[512,384]{1,0:T(8,128)(2,1)S(1)} %finish.1.refs_0_), channel_id=1, source_target_pairs={{0,7},{1,0},{2,1},{3,2},{4,3},{5,4},{6,5},{7,6},{8,15},{9,8},{10,9... | collective-permute-start | bytes 1179656 | tf_op jit(solution)/shard_map/ppermute | solution.py:228
  101.6 13.3 %collective-permute-start.12 = (bf16[512,384]{1,0:T(8,128)(2,1)S(1)}, bf16[512,384]{1,0:T(8,128)(2,1)}, u32[]{:S(2)}, u32[]{:S(2)}) collective-permute-start(bf16[512,384]{1,0:T(8,128)(2,1)S(1)} %collective-permute-done.10.refs_1_), channel_id=1, source_target_pairs={{0,1},{1,2},{2,3},{3,4},{4,5},{5,6},{6,7},{7,0},{8,9},{9,10},{10,1... | collective-permute-start | bytes 1179656 | tf_op jit(solution)/shard_map/ppermute | solution.py:228
  106.9 0.7 copy-start.2
  107.7 14.6 %collective-permute-start.13 = (bf16[512,384]{1,0:T(8,128)(2,1)S(1)}, bf16[512,384]{1,0:T(8,128)(2,1)}, u32[]{:S(2)}, u32[]{:S(2)}) collective-permute-start(bf16[512,384]{1,0:T(8,128)(2,1)S(1)} %collective-permute-done.11.refs_2_), channel_id=1, source_target_pairs={{0,7},{1,0},{2,1},{3,2},{4,3},{5,4},{6,5},{7,6},{8,15},{9,8},{10,9... | collective-permute-start | bytes 1179656 | tf_op jit(solution)/shard_map/ppermute | solution.py:228
  109.6 0.7 copy-start.4
  115.0 13.4 %collective-permute-start.14 = (bf16[512,384]{1,0:T(8,128)(2,1)}, bf16[512,384]{1,0:T(8,128)(2,1)S(1)}, u32[]{:S(2)}, u32[]{:S(2)}) collective-permute-start(bf16[512,384]{1,0:T(8,128)(2,1)} %collective-permute-done.12.refs_1_), channel_id=1, source_target_pairs={{0,1},{1,2},{2,3},{3,4},{4,5},{5,6},{6,7},{7,0},{8,9},{9,10},{10,1... | collective-permute-start | bytes 1179656 | tf_op jit(solution)/shard_map/ppermute | solution.py:228
  122.3 13.2 %collective-permute-start.15 = (bf16[512,384]{1,0:T(8,128)(2,1)}, bf16[512,384]{1,0:T(8,128)(2,1)S(1)}, u32[]{:S(2)}, u32[]{:S(2)}) collective-permute-start(bf16[512,384]{1,0:T(8,128)(2,1)} %collective-permute-done.13.refs_2_), channel_id=1, source_target_pairs={{0,7},{1,0},{2,1},{3,2},{4,3},{5,4},{6,5},{7,6},{8,15},{9,8},{10,9... | collective-permute-start | bytes 1179656 | tf_op jit(solution)/shard_map/ppermute | solution.py:228
  129.1 13.2 %collective-permute-start.16 = (bf16[256,384]{1,0:T(8,128)(2,1)}, bf16[256,384]{1,0:T(8,128)(2,1)}, u32[]{:S(2)}, u32[]{:S(2)}) collective-permute-start(bf16[256,384]{1,0:T(8,128)(2,1)} %slice.8), channel_id=1, source_target_pairs={{0,1},{1,2},{2,3},{3,4},{4,5},{5,6},{6,7},{7,0},{8,9},{9,10},{10,1... | collective-permute-start | bytes 589832 | tf_op jit(solution)/shard_map/ppermute | solution.py:228
  136.2 9.1 %collective-permute-start.17 = (bf16[256,384]{1,0:T(8,128)(2,1)}, bf16[256,384]{1,0:T(8,128)(2,1)}, u32[]{:S(2)}, u32[]{:S(2)}) collective-permute-start(bf16[256,384]{1,0:T(8,128)(2,1)} %slice.9), channel_id=1, source_target_pairs={{0,7},{1,0},{2,1},{3,2},{4,3},{5,4},{6,5},{7,6},{8,15},{9,8},{10,9... | collective-permute-start | bytes 589832 | tf_op jit(solution)/shard_map/ppermute | solution.py:228
  138.1 1.0 copy-start.3
  138.1 1.1 copy-start.5

commit v8 on v3

--- a/solution.py
+++ b/solution.py
@@ -48,10 +48,6 @@
     back = query - source
     seen = (source >= 0) & (back >= 0) & (back < span_ref[query])
     return jnp.where(seen, counts_ref[jnp.maximum(source, 0)], 0)
-
-
-def in_hbm(array):
-    return pltpu.with_memory_space_constraint(array, pltpu.HBM)
 
 
 def _unpack(packed, acc, top):
@@ -116,19 +112,22 @@
     )(*scalars, *operands)
 
 
+def _join(packed, acc, top):
+    new_top = jnp.maximum(top[0], packed[0, :, HD : HD + 1])
+    own_part = jnp.exp2((top[0] - new_top) * EXP2_SCALE)
+    other_part = jnp.exp2((packed[0, :, HD : HD + 1] - new_top) * EXP2_SCALE)
+    acc[0, :, :HD] = acc[0, :, :HD] * own_part + packed[0, :, :HD] * other_part
+    acc[0, :, HD:] = acc[0, :, HD:] * own_part + packed[0, :, 2 * HD - 1 :] * other_part
+    top[0] = new_top
+
+
 def _finish_body(frame_ref, span_ref, counts_ref, q_ref, k_ref, v_ref, own, other, upper_ref, lower_ref, acc, top):
     _unpack(own, acc, top)
     limit = _visible(frame_ref[0], 0, WIN - 1, span_ref, counts_ref)
     limit = jnp.where(frame_ref[0] % 2 == 0, limit, 0)
     _attend(limit, q_ref, k_ref, v_ref, acc, top)
-    own_top, other_top = top[0], other[0, :, HD : HD + 1]
-    own_total, other_total = acc[0, :, HD:], other[0, :, 2 * HD - 1 :]
-    both_top = jnp.maximum(own_top, other_top)
-    own_part = jnp.exp2((own_top - both_top) * EXP2_SCALE)
-    other_part = jnp.exp2((other_top - both_top) * EXP2_SCALE)
-    total = own_total * own_part + other_total * other_part
-    mixed = acc[0, :, :HD] * own_part + other[0, :, :HD] * other_part
-    mixed = (mixed / total).astype(jnp.bfloat16)
+    _join(other, acc, top)
+    mixed = (acc[0, :, :HD] / acc[0, :, HD:]).astype(jnp.bfloat16)
     half = upper_ref.shape[0]
     upper_ref[...] = mixed[:half]
     lower_ref[...] = mixed[half:]
@@ -208,9 +207,7 @@
             in_specs=[pl.BlockSpec(x.shape, lambda i, g, n=x.ndim: (0,) * n) for x in operands],
             out_specs=pl.BlockSpec((2 * half, columns), lambda i, g: (0, 0)),
         ),
-        cost_estimate=pl.CostEstimate(
-            flops=2 * len(pieces) * half * height * columns, transcendentals=0, bytes_accessed=4 << 20
-        ),
+        cost_estimate=LONG,
         compiler_params=pltpu.CompilerParams(vmem_limit_bytes=LARGE_VMEM),
         name=name,
     )(group, *operands)
@@ -266,7 +263,6 @@
         total = project(total, held, places, jnp.float32, f"project_{step - 1}")
         held = up + down
         places = ((0, groups - step), (1, groups - step), (0, step), (1, step))
-        up[1], down[1], total = after((up[1], down[1], total))
     far = [send(up[0], upward, "head"), send(down[1], downward, "head")]
     total = project(total, held, places, jnp.float32, "project_3")
     return project(total, far, ((0, 4), (1, 4)), jnp.bfloat16, "project_4")

time: 143 us -> 145 us (1.014)
  the two profiles are of different devices: /device:TPU:30 before, /device:TPU:28 now
where the time goes in v8:
time: 145 us
  starting transfers between devices  79.8 us (55%)
  Pallas kernels  38.6 us (27%)
  waiting for transfers between devices  26.1 us (18%)
    ppermute x24, starting transfers between devices, send(): return lax.ppermute(block, axis, route)  72.3 us
    ppermute x24, waiting for transfers between devices, send(): return lax.ppermute(block, axis, route)  26.1 us
    pallas_call x4, Pallas kernels, attention_call(): pl.pallas_call(_attention_body(sides, hops, states is None), out_shape=[j...  23.9 us
    all_to_all x1, starting transfers between devices, on_device(): lax.all_to_all(blocks, 'head', split_axis=0, concat_axis=0, tiled=True)  7.45 us
    pallas_call x5, Pallas kernels, project_call(): pl.pallas_call(_project_body(places, base is not None), out_shape=jax.Sha...  6.93 us
    pallas_call x1, Pallas kernels, finish_call(): pl.pallas_call(_finish_body, out_shape=[jax.ShapeDtypeStruct((per_frame /...  4.99 us
  transfers between devices with their start and end apart: 25, of which 7 were waited for; matrix products, arithmetic and copies ran while one was open for 0% of the time, Pallas kernels for 25%

profile of v8, /device:TPU:28, one launch (start us, length us, event | category | flops | bytes accessed | tf_op | source)
XLA Modules:
  0.0 144.9 jit_solution(8153386567541875176)
XLA Ops:
  0.0 4.3 %collective-permute-start = (bf16[512,384]{1,0:T(8,128)(2,1)}, bf16[512,384]{1,0:T(8,128)(2,1)S(1)}, u32[]{:S(2)}, u32[]{:S(2)}) collective-permute-start(bf16[512,384]{1,0:T(8,128)(2,1)} %refs_2_.1), channel_id=1, source_target_pairs={{0,16},{8,24},{16,32},{24,40},{32,48},{40,56},{48,64},{56,72},{64,... | collective-permute-start | bytes 1179656 | tf_op jit(solution)/shard_map/ppermute | solution.py:231
  4.3 4.3 %collective-permute-start.3 = (bf16[512,384]{1,0:T(8,128)(2,1)}, bf16[512,384]{1,0:T(8,128)(2,1)S(1)}, u32[]{:S(2)}, u32[]{:S(2)}) collective-permute-start(bf16[512,384]{1,0:T(8,128)(2,1)} %refs_3_.1), channel_id=1, source_target_pairs={{0,16},{8,24},{16,32},{24,40},{32,48},{40,56},{48,64},{56,72},{64,... | collective-permute-start | bytes 1179656 | tf_op jit(solution)/shard_map/ppermute | solution.py:231
  8.6 1.9 %collective-permute-start.6 = (bf16[512,384]{1,0:T(8,128)(2,1)}, bf16[512,384]{1,0:T(8,128)(2,1)S(1)}, u32[]{:S(2)}, u32[]{:S(2)}) collective-permute-start(bf16[512,384]{1,0:T(8,128)(2,1)} %q_ref.1), channel_id=1, source_target_pairs={{0,8},{8,0},{16,24},{24,16},{32,40},{40,32},{48,56},{56,48},{64,72... | collective-permute-start | bytes 1179656 | tf_op jit(solution)/shard_map/ppermute | solution.py:231
  10.5 2.8 %column_blocks.1 = bf16[8,384,384]{2,1,0:T(8,128)(2,1)} custom-call(bf16[384,3072]{1,0:T(8,128)(2,1)} %w_ref.1), custom_call_target="tpu_custom_call" | custom-call | flops 1 | bytes 1 | tf_op jit(solution)/shard_map/column_blocks/pallas_call | solution.py:168
  13.3 7.5 %all-to-all-start = ((bf16[8,384,384]{2,1,0:T(8,128)(2,1)}), bf16[8,384,384]{2,1,0:T(8,128)(2,1)S(1)}, u32[]{:S(2)}, u32[]{:S(2)}) async-start(bf16[8,384,384]{2,1,0:T(8,128)(2,1)} %column_blocks.1), calls=%async_computation | async-start | bytes 4718592 | tf_op jit(solution)/shard_map/all_to_all | solution.py:245
  20.8 3.9 %collective-permute-done.refs_4_ = bf16[512,384]{1,0:T(8,128)(2,1)S(1)} collective-permute-done((bf16[512,384]{1,0:T(8,128)(2,1)}, bf16[512,384]{1,0:T(8,128)(2,1)S(1)}, u32[]{:S(2)}, u32[]{:S(2)}) %collective-permute-start) | collective-permute-done | bytes 393248 | tf_op jit(solution)/shard_map/ppermute | solution.py:231
  24.7 1.9 %collective-permute-start.1 = (bf16[512,384]{1,0:T(8,128)(2,1)S(1)}, bf16[512,384]{1,0:T(8,128)(2,1)S(1)}, u32[]{:S(2)}, u32[]{:S(2)}) collective-permute-start(bf16[512,384]{1,0:T(8,128)(2,1)S(1)} %collective-permute-done.refs_4_), channel_id=1, source_target_pairs={{0,16},{8,24},{16,32},{24,40},{32,48},{40,56},{48,64},{56,72},{64,... | collective-permute-start | bytes 1179656 | tf_op jit(solution)/shard_map/ppermute | solution.py:231
  26.6 6.5 %collective-permute-done.3.refs_5_ = bf16[512,384]{1,0:T(8,128)(2,1)S(1)} collective-permute-done((bf16[512,384]{1,0:T(8,128)(2,1)}, bf16[512,384]{1,0:T(8,128)(2,1)S(1)}, u32[]{:S(2)}, u32[]{:S(2)}) %collective-permute-start.3) | collective-permute-done | bytes 393248 | tf_op jit(solution)/shard_map/ppermute | solution.py:231
  35.1 10.7 %attend_01.1 = (f32[3,512,256]{2,1,0:T(8,128)S(1)}, f32[3,512,256]{2,1,0:T(8,128)S(1)}) custom-call(s32[1]{0:T(128)} %bitcast.1.frame_ref, s32[96]{0:T(128)S(1)} %copy-done, s32[96]{0:T(128)S(1)} %copy-done.1, bf16[512,384]{1,0:T(8,128)(2,1)} %q_ref.1, bf16[512,384]{1,0:T(8,128)(2,1)S(1)} %collective-permute-done.6.refs_1_.refs_0_, ...), custom_call_target="tpu_custom_call" | custom-call | flops 17179869184 | bytes 1 | tf_op jit(solution)/shard_map/attend_01/pallas_call | solution.py:99
  45.8 1.9 %collective-permute-start.2 = (bf16[512,384]{1,0:T(8,128)(2,1)S(1)}, bf16[512,384]{1,0:T(8,128)(2,1)S(1)}, u32[]{:S(2)}, u32[]{:S(2)}) collective-permute-start(bf16[512,384]{1,0:T(8,128)(2,1)S(1)} %collective-permute-done.1.refs_2_), channel_id=1, source_target_pairs={{0,16},{8,24},{16,32},{24,40},{32,48},{40,56},{48,64},{56,72},{64,... | collective-permute-start | bytes 1179656 | tf_op jit(solution)/shard_map/ppermute | solution.py:231
  51.4 7.2 %attend_2.1 = (f32[3,512,256]{2,1,0:T(8,128)S(1)}, f32[3,512,256]{2,1,0:T(8,128)S(1)}) custom-call(s32[1]{0:T(128)} %bitcast.1.frame_ref, s32[96]{0:T(128)S(1)} %copy-done, s32[96]{0:T(128)S(1)} %copy-done.1, bf16[512,384]{1,0:T(8,128)(2,1)} %q_ref.1, bf16[512,384]{1,0:T(8,128)(2,1)S(1)} %collective-permute-done.6.refs_1_.refs_0_, ...), custom_call_target="tpu_custom_call" | custom-call | flops 17179869184 | bytes 1 | tf_op jit(solution)/shard_map/attend_2/pallas_call | solution.py:99
  60.1 5.9 %collective-permute-done.5.refs_2_ = bf16[512,384]{1,0:T(8,128)(2,1)S(1)} collective-permute-done((bf16[512,384]{1,0:T(8,128)(2,1)S(1)}, bf16[512,384]{1,0:T(8,128)(2,1)S(1)}, u32[]{:S(2)}, u32[]{:S(2)}) %collective-permute-start.5) | collective-permute-done | bytes 393248 | tf_op jit(solution)/shard_map/ppermute | solution.py:231
  70.2 2.7 %collective-permute-start.9 = (f32[3,512,256]{2,1,0:T(8,128)S(1)}, f32[3,512,256]{2,1,0:T(8,128)S(1)}, u32[]{:S(2)}, u32[]{:S(2)}) collective-permute-start(f32[3,512,256]{2,1,0:T(8,128)S(1)} %attend_3_other.1), channel_id=1, source_target_pairs={{0,8},{8,0},{16,24},{24,16},{32,40},{40,32},{48,56},{56,48},{64,72... | collective-permute-start | bytes 4718600 | tf_op jit(solution)/shard_map/ppermute | solution.py:231
  72.9 4.4 %attend_3_own.1.own = f32[3,512,256]{2,1,0:T(8,128)S(1)} custom-call(s32[1]{0:T(128)} %bitcast.1.frame_ref, s32[96]{0:T(128)S(1)} %copy-done, s32[96]{0:T(128)S(1)} %copy-done.1, bf16[512,384]{1,0:T(8,128)(2,1)} %q_ref.1, bf16[512,384]{1,0:T(8,128)(2,1)S(1)} %collective-permute-done.2.refs_1_, bf16[512,384]{1,0:T(8,128)(2,1)S(1)} %collective-permute-done.5.refs_2_, ...), custom_call_target="tpu_custom_call" | custom-call | flops 17179869184 | bytes 1 | tf_op jit(solution)/shard_map/attend_3_own/pallas_call | solution.py:99
  77.3 4.1 %collective-permute-done.8.v_ref = bf16[512,384]{1,0:T(8,128)(2,1)S(1)} collective-permute-done((bf16[512,384]{1,0:T(8,128)(2,1)S(1)}, bf16[512,384]{1,0:T(8,128)(2,1)S(1)}, u32[]{:S(2)}, u32[]{:S(2)}) %collective-permute-start.8) | collective-permute-done | bytes 393248 | tf_op jit(solution)/shard_map/ppermute | solution.py:231
  81.4 5.0 %finish.1 = (bf16[256,384]{1,0:T(8,128)(2,1)S(1)}, bf16[256,384]{1,0:T(8,128)(2,1)S(1)}) custom-call(s32[1]{0:T(128)} %bitcast.1.frame_ref, s32[96]{0:T(128)S(1)} %copy-done, s32[96]{0:T(128)S(1)} %copy-done.1, bf16[512,384]{1,0:T(8,128)(2,1)} %q_ref.1, bf16[512,384]{1,0:T(8,128)(2,1)S(1)} %collective-permute-done.7.k_ref, ...), custom_call_target="tpu_custom_call" | custom-call | flops 1 | bytes 1 | tf_op jit(solution)/shard_map/finish/pallas_call | solution.py:139
  86.4 4.7 %collective-permute-start.10 = (bf16[256,384]{1,0:T(8,128)(2,1)S(1)}, bf16[256,384]{1,0:T(8,128)(2,1)S(1)}, u32[]{:S(2)}, u32[]{:S(2)}) collective-permute-start(bf16[256,384]{1,0:T(8,128)(2,1)S(1)} %get-tuple-element.23.refs_0_), channel_id=1, source_target_pairs={{0,1},{1,2},{2,3},{3,4},{4,5},{5,6},{6,7},{7,0},{8,9},{9,10},{10,1... | collective-permute-start | bytes 589832 | tf_op jit(solution)/shard_map/ppermute | solution.py:231
  91.1 1.9 %collective-permute-start.13 = (bf16[256,384]{1,0:T(8,128)(2,1)S(1)}, bf16[256,384]{1,0:T(8,128)(2,1)S(1)}, u32[]{:S(2)}, u32[]{:S(2)}) collective-permute-start(bf16[256,384]{1,0:T(8,128)(2,1)S(1)} %get-tuple-element.24.refs_1_), channel_id=1, source_target_pairs={{0,7},{1,0},{2,1},{3,2},{4,3},{5,4},{6,5},{7,6},{8,15},{9,8},{10,9... | collective-permute-start | bytes 589832 | tf_op jit(solution)/shard_map/ppermute | solution.py:231
  93.0 5.1 %collective-permute-start.11 = (bf16[256,384]{1,0:T(8,128)(2,1)S(1)}, bf16[256,384]{1,0:T(8,128)(2,1)S(1)}, u32[]{:S(2)}, u32[]{:S(2)}) collective-permute-start(bf16[256,384]{1,0:T(8,128)(2,1)S(1)} %get-tuple-element.24.refs_1_), channel_id=1, source_target_pairs={{0,1},{1,2},{2,3},{3,4},{4,5},{5,6},{6,7},{7,0},{8,9},{9,10},{10,1... | collective-permute-start | bytes 589832 | tf_op jit(solution)/shard_map/ppermute | solution.py:231
  98.2 1.9 %collective-permute-start.12 = (bf16[256,384]{1,0:T(8,128)(2,1)S(1)}, bf16[256,384]{1,0:T(8,128)(2,1)S(1)}, u32[]{:S(2)}, u32[]{:S(2)}) collective-permute-start(bf16[256,384]{1,0:T(8,128)(2,1)S(1)} %get-tuple-element.23.refs_0_), channel_id=1, source_target_pairs={{0,7},{1,0},{2,1},{3,2},{4,3},{5,4},{6,5},{7,6},{8,15},{9,8},{10,9... | collective-permute-start | bytes 589832 | tf_op jit(solution)/shard_map/ppermute | solution.py:231
  100.1 5.1 %collective-permute-start.14 = (bf16[256,384]{1,0:T(8,128)(2,1)S(1)}, bf16[256,384]{1,0:T(8,128)(2,1)}, u32[]{:S(2)}, u32[]{:S(2)}) collective-permute-start(bf16[256,384]{1,0:T(8,128)(2,1)S(1)} %collective-permute-done.10.refs_1_), channel_id=1, source_target_pairs={{0,1},{1,2},{2,3},{3,4},{4,5},{5,6},{6,7},{7,0},{8,9},{9,10},{10,1... | collective-permute-start | bytes 589832 | tf_op jit(solution)/shard_map/ppermute | solution.py:231
  105.3 1.9 %collective-permute-start.17 = (bf16[256,384]{1,0:T(8,128)(2,1)S(1)}, bf16[256,384]{1,0:T(8,128)(2,1)}, u32[]{:S(2)}, u32[]{:S(2)}) collective-permute-start(bf16[256,384]{1,0:T(8,128)(2,1)S(1)} %collective-permute-done.13.refs_4_), channel_id=1, source_target_pairs={{0,7},{1,0},{2,1},{3,2},{4,3},{5,4},{6,5},{7,6},{8,15},{9,8},{10,9... | collective-permute-start | bytes 589832 | tf_op jit(solution)/shard_map/ppermute | solution.py:231
  107.2 5.1 %collective-permute-start.15 = (bf16[256,384]{1,0:T(8,128)(2,1)S(1)}, bf16[256,384]{1,0:T(8,128)(2,1)}, u32[]{:S(2)}, u32[]{:S(2)}) collective-permute-start(bf16[256,384]{1,0:T(8,128)(2,1)S(1)} %collective-permute-done.11.refs_2_), channel_id=1, source_target_pairs={{0,1},{1,2},{2,3},{3,4},{4,5},{5,6},{6,7},{7,0},{8,9},{9,10},{10,1... | collective-permute-start | bytes 589832 | tf_op jit(solution)/shard_map/ppermute | solution.py:231
  112.4 1.9 %collective-permute-start.16 = (bf16[256,384]{1,0:T(8,128)(2,1)S(1)}, bf16[256,384]{1,0:T(8,128)(2,1)}, u32[]{:S(2)}, u32[]{:S(2)}) collective-permute-start(bf16[256,384]{1,0:T(8,128)(2,1)S(1)} %collective-permute-done.12.refs_3_), channel_id=1, source_target_pairs={{0,7},{1,0},{2,1},{3,2},{4,3},{5,4},{6,5},{7,6},{8,15},{9,8},{10,9... | collective-permute-start | bytes 589832 | tf_op jit(solution)/shard_map/ppermute | solution.py:231
  114.3 5.1 %collective-permute-start.18 = (bf16[256,384]{1,0:T(8,128)(2,1)}, bf16[256,384]{1,0:T(8,128)(2,1)}, u32[]{:S(2)}, u32[]{:S(2)}) collective-permute-start(bf16[256,384]{1,0:T(8,128)(2,1)} %collective-permute-done.14.refs_1_), channel_id=1, source_target_pairs={{0,1},{1,2},{2,3},{3,4},{4,5},{5,6},{6,7},{7,0},{8,9},{9,10},{10,1... | collective-permute-start | bytes 589832 | tf_op jit(solution)/shard_map/ppermute | solution.py:231
  119.5 1.9 %collective-permute-start.21 = (bf16[256,384]{1,0:T(8,128)(2,1)}, bf16[256,384]{1,0:T(8,128)(2,1)}, u32[]{:S(2)}, u32[]{:S(2)}) collective-permute-start(bf16[256,384]{1,0:T(8,128)(2,1)} %collective-permute-done.17.refs_4_), channel_id=1, source_target_pairs={{0,7},{1,0},{2,1},{3,2},{4,3},{5,4},{6,5},{7,6},{8,15},{9,8},{10,9... | collective-permute-start | bytes 589832 | tf_op jit(solution)/shard_map/ppermute | solution.py:231
  121.4 5.1 %collective-permute-start.19 = (bf16[256,384]{1,0:T(8,128)(2,1)}, bf16[256,384]{1,0:T(8,128)(2,1)}, u32[]{:S(2)}, u32[]{:S(2)}) collective-permute-start(bf16[256,384]{1,0:T(8,128)(2,1)} %collective-permute-done.15.refs_2_), channel_id=1, source_target_pairs={{0,1},{1,2},{2,3},{3,4},{4,5},{5,6},{6,7},{7,0},{8,9},{9,10},{10,1... | collective-permute-start | bytes 589832 | tf_op jit(solution)/shard_map/ppermute | solution.py:231
  126.5 1.9 %collective-permute-start.20 = (bf16[256,384]{1,0:T(8,128)(2,1)}, bf16[256,384]{1,0:T(8,128)(2,1)}, u32[]{:S(2)}, u32[]{:S(2)}) collective-permute-start(bf16[256,384]{1,0:T(8,128)(2,1)} %collective-permute-done.16.refs_3_), channel_id=1, source_target_pairs={{0,7},{1,0},{2,1},{3,2},{4,3},{5,4},{6,5},{7,6},{8,15},{9,8},{10,9... | collective-permute-start | bytes 589832 | tf_op jit(solution)/shard_map/ppermute | solution.py:231
  128.5 5.1 %collective-permute-start.22 = (bf16[256,384]{1,0:T(8,128)(2,1)}, bf16[256,384]{1,0:T(8,128)(2,1)}, u32[]{:S(2)}, u32[]{:S(2)}) collective-permute-start(bf16[256,384]{1,0:T(8,128)(2,1)} %collective-permute-done.18.refs_1_), channel_id=1, source_target_pairs={{0,1},{1,2},{2,3},{3,4},{4,5},{5,6},{6,7},{7,0},{8,9},{9,10},{10,1... | collective-permute-start | bytes 589832 | tf_op jit(solution)/shard_map/ppermute | solution.py:231
  133.6 1.9 %collective-permute-start.23 = (bf16[256,384]{1,0:T(8,128)(2,1)}, bf16[256,384]{1,0:T(8,128)(2,1)}, u32[]{:S(2)}, u32[]{:S(2)}) collective-permute-start(bf16[256,384]{1,0:T(8,128)(2,1)} %collective-permute-done.21.refs_4_), channel_id=1, source_target_pairs={{0,7},{1,0},{2,1},{3,2},{4,3},{5,4},{6,5},{7,6},{8,15},{9,8},{10,9... | collective-permute-start | bytes 589832 | tf_op jit(solution)/shard_map/ppermute | solution.py:231
  140.4 2.3 %collective-permute-done.23.refs_2_ = bf16[256,384]{1,0:T(8,128)(2,1)} collective-permute-done((bf16[256,384]{1,0:T(8,128)(2,1)}, bf16[256,384]{1,0:T(8,128)(2,1)}, u32[]{:S(2)}, u32[]{:S(2)}) %collective-permute-start.23) | collective-permute-done | bytes 196640 | tf_op jit(solution)/shard_map/ppermute | solution.py:231
  142.7 2.2 %project_4.1 = bf16[512,384]{1,0:T(8,128)(2,1)} custom-call(s32[1]{0:T(128)} %bitcast.group_ref, f32[512,384]{1,0:T(8,128)S(1)} %project_3.1.refs_0_, bf16[256,384]{1,0:T(8,128)(2,1)} %collective-permute-done.22.refs_1_, bf16[256,384]{1,0:T(8,128)(2,1)} %collective-permute-done.23.refs_2_, bf16[8,384,384]{2,1,0:T(8,128)(2,1)S(1)} %all-to-all-done.refs_2_.refs_5_.refs_3_), custom_call_target="tpu_custom_call" | custom-call | flops 17179869184 | bytes 1 | tf_op jit(solution)/shard_map/project_4/pallas_call | solution.py:201
  (33 shorter events, 16.0 us)
Async XLA Ops:
  0.0 24.7 %collective-permute-start = (bf16[512,384]{1,0:T(8,128)(2,1)}, bf16[512,384]{1,0:T(8,128)(2,1)S(1)}, u32[]{:S(2)}, u32[]{:S(2)}) collective-permute-start(bf16[512,384]{1,0:T(8,128)(2,1)} %refs_2_.1), channel_id=1, source_target_pairs={{0,16},{8,24},{16,32},{24,40},{32,48},{40,56},{48,64},{56,72},{64,... | collective-permute-start | bytes 1179656 | tf_op jit(solution)/shard_map/ppermute | solution.py:231
  4.3 28.8 %collective-permute-start.3 = (bf16[512,384]{1,0:T(8,128)(2,1)}, bf16[512,384]{1,0:T(8,128)(2,1)S(1)}, u32[]{:S(2)}, u32[]{:S(2)}) collective-permute-start(bf16[512,384]{1,0:T(8,128)(2,1)} %refs_3_.1), channel_id=1, source_target_pairs={{0,16},{8,24},{16,32},{24,40},{32,48},{40,56},{48,64},{56,72},{64,... | collective-permute-start | bytes 1179656 | tf_op jit(solution)/shard_map/ppermute | solution.py:231
  8.6 26.5 %collective-permute-start.6 = (bf16[512,384]{1,0:T(8,128)(2,1)}, bf16[512,384]{1,0:T(8,128)(2,1)S(1)}, u32[]{:S(2)}, u32[]{:S(2)}) collective-permute-start(bf16[512,384]{1,0:T(8,128)(2,1)} %q_ref.1), channel_id=1, source_target_pairs={{0,8},{8,0},{16,24},{24,16},{32,40},{40,32},{48,56},{56,48},{64,72... | collective-permute-start | bytes 1179656 | tf_op jit(solution)/shard_map/ppermute | solution.py:231
  13.3 21.7 %copy-start = (s32[96]{0:T(128)S(1)}, s32[96]{0:T(128)}, u32[]{:S(2)}) copy-start(s32[96]{0:T(128)} %span_ref.9) | copy-start | bytes 1156
  13.3 21.7 %copy-start.1 = (s32[96]{0:T(128)S(1)}, s32[96]{0:T(128)}, u32[]{:S(2)}) copy-start(s32[96]{0:T(128)} %counts_ref.9) | copy-start | bytes 1156
  13.3 122.3 %all-to-all-start = ((bf16[8,384,384]{2,1,0:T(8,128)(2,1)}), bf16[8,384,384]{2,1,0:T(8,128)(2,1)S(1)}, u32[]{:S(2)}, u32[]{:S(2)}) async-start(bf16[8,384,384]{2,1,0:T(8,128)(2,1)} %column_blocks.1), calls=%async_computation | async-start | bytes 4718592 | tf_op jit(solution)/shard_map/all_to_all | solution.py:245
  24.7 21.1 %collective-permute-start.1 = (bf16[512,384]{1,0:T(8,128)(2,1)S(1)}, bf16[512,384]{1,0:T(8,128)(2,1)S(1)}, u32[]{:S(2)}, u32[]{:S(2)}) collective-permute-start(bf16[512,384]{1,0:T(8,128)(2,1)S(1)} %collective-permute-done.refs_4_), channel_id=1, source_target_pairs={{0,16},{8,24},{16,32},{24,40},{32,48},{40,56},{48,64},{56,72},{64,... | collective-permute-start | bytes 1179656 | tf_op jit(solution)/shard_map/ppermute | solution.py:231
  33.1 16.3 %collective-permute-start.4 = (bf16[512,384]{1,0:T(8,128)(2,1)S(1)}, bf16[512,384]{1,0:T(8,128)(2,1)S(1)}, u32[]{:S(2)}, u32[]{:S(2)}) collective-permute-start(bf16[512,384]{1,0:T(8,128)(2,1)S(1)} %collective-permute-done.3.refs_5_), channel_id=1, source_target_pairs={{0,16},{8,24},{16,32},{24,40},{32,48},{40,56},{48,64},{56,72},{64,... | collective-permute-start | bytes 1179656 | tf_op jit(solution)/shard_map/ppermute | solution.py:231
  45.8 14.3 %collective-permute-start.2 = (bf16[512,384]{1,0:T(8,128)(2,1)S(1)}, bf16[512,384]{1,0:T(8,128)(2,1)S(1)}, u32[]{:S(2)}, u32[]{:S(2)}) collective-permute-start(bf16[512,384]{1,0:T(8,128)(2,1)S(1)} %collective-permute-done.1.refs_2_), channel_id=1, source_target_pairs={{0,16},{8,24},{16,32},{24,40},{32,48},{40,56},{48,64},{56,72},{64,... | collective-permute-start | bytes 1179656 | tf_op jit(solution)/shard_map/ppermute | solution.py:231
  49.5 16.5 %collective-permute-start.5 = (bf16[512,384]{1,0:T(8,128)(2,1)S(1)}, bf16[512,384]{1,0:T(8,128)(2,1)S(1)}, u32[]{:S(2)}, u32[]{:S(2)}) collective-permute-start(bf16[512,384]{1,0:T(8,128)(2,1)S(1)} %collective-permute-done.4.refs_3_), channel_id=1, source_target_pairs={{0,16},{8,24},{16,32},{24,40},{32,48},{40,56},{48,64},{56,72},{64,... | collective-permute-start | bytes 1179656 | tf_op jit(solution)/shard_map/ppermute | solution.py:231
  66.0 11.3 %collective-permute-start.7 = (bf16[512,384]{1,0:T(8,128)(2,1)S(1)}, bf16[512,384]{1,0:T(8,128)(2,1)S(1)}, u32[]{:S(2)}, u32[]{:S(2)}) collective-permute-start(bf16[512,384]{1,0:T(8,128)(2,1)S(1)} %collective-permute-done.2.refs_1_), channel_id=1, source_target_pairs={{8,16},{24,32},{40,48},{56,64},{72,80},{88,96},{104,112},{120,128}... | collective-permute-start | bytes 1179656 | tf_op jit(solution)/shard_map/ppermute | solution.py:231
  67.3 14.1 %collective-permute-start.8 = (bf16[512,384]{1,0:T(8,128)(2,1)S(1)}, bf16[512,384]{1,0:T(8,128)(2,1)S(1)}, u32[]{:S(2)}, u32[]{:S(2)}) collective-permute-start(bf16[512,384]{1,0:T(8,128)(2,1)S(1)} %collective-permute-done.5.refs_2_), channel_id=1, source_target_pairs={{8,16},{24,32},{40,48},{56,64},{72,80},{88,96},{104,112},{120,128}... | collective-permute-start | bytes 1179656 | tf_op jit(solution)/shard_map/ppermute | solution.py:231
  70.2 11.2 %collective-permute-start.9 = (f32[3,512,256]{2,1,0:T(8,128)S(1)}, f32[3,512,256]{2,1,0:T(8,128)S(1)}, u32[]{:S(2)}, u32[]{:S(2)}) collective-permute-start(f32[3,512,256]{2,1,0:T(8,128)S(1)} %attend_3_other.1), channel_id=1, source_target_pairs={{0,8},{8,0},{16,24},{24,16},{32,40},{40,32},{48,56},{56,48},{64,72... | collective-permute-start | bytes 4718600 | tf_op jit(solution)/shard_map/ppermute | solution.py:231
  86.4 13.7 %collective-permute-start.10 = (bf16[256,384]{1,0:T(8,128)(2,1)S(1)}, bf16[256,384]{1,0:T(8,128)(2,1)S(1)}, u32[]{:S(2)}, u32[]{:S(2)}) collective-permute-start(bf16[256,384]{1,0:T(8,128)(2,1)S(1)} %get-tuple-element.23.refs_0_), channel_id=1, source_target_pairs={{0,1},{1,2},{2,3},{3,4},{4,5},{5,6},{6,7},{7,0},{8,9},{9,10},{10,1... | collective-permute-start | bytes 589832 | tf_op jit(solution)/shard_map/ppermute | solution.py:231
  91.1 14.2 %collective-permute-start.13 = (bf16[256,384]{1,0:T(8,128)(2,1)S(1)}, bf16[256,384]{1,0:T(8,128)(2,1)S(1)}, u32[]{:S(2)}, u32[]{:S(2)}) collective-permute-start(bf16[256,384]{1,0:T(8,128)(2,1)S(1)} %get-tuple-element.24.refs_1_), channel_id=1, source_target_pairs={{0,7},{1,0},{2,1},{3,2},{4,3},{5,4},{6,5},{7,6},{8,15},{9,8},{10,9... | collective-permute-start | bytes 589832 | tf_op jit(solution)/shard_map/ppermute | solution.py:231
  93.0 14.2 %collective-permute-start.11 = (bf16[256,384]{1,0:T(8,128)(2,1)S(1)}, bf16[256,384]{1,0:T(8,128)(2,1)S(1)}, u32[]{:S(2)}, u32[]{:S(2)}) collective-permute-start(bf16[256,384]{1,0:T(8,128)(2,1)S(1)} %get-tuple-element.24.refs_1_), channel_id=1, source_target_pairs={{0,1},{1,2},{2,3},{3,4},{4,5},{5,6},{6,7},{7,0},{8,9},{9,10},{10,1... | collective-permute-start | bytes 589832 | tf_op jit(solution)/shard_map/ppermute | solution.py:231
  98.2 14.2 %collective-permute-start.12 = (bf16[256,384]{1,0:T(8,128)(2,1)S(1)}, bf16[256,384]{1,0:T(8,128)(2,1)S(1)}, u32[]{:S(2)}, u32[]{:S(2)}) collective-permute-start(bf16[256,384]{1,0:T(8,128)(2,1)S(1)} %get-tuple-element.23.refs_0_), channel_id=1, source_target_pairs={{0,7},{1,0},{2,1},{3,2},{4,3},{5,4},{6,5},{7,6},{8,15},{9,8},{10,9... | collective-permute-start | bytes 589832 | tf_op jit(solution)/shard_map/ppermute | solution.py:231
  100.1 14.2 %collective-permute-start.14 = (bf16[256,384]{1,0:T(8,128)(2,1)S(1)}, bf16[256,384]{1,0:T(8,128)(2,1)}, u32[]{:S(2)}, u32[]{:S(2)}) collective-permute-start(bf16[256,384]{1,0:T(8,128)(2,1)S(1)} %collective-permute-done.10.refs_1_), channel_id=1, source_target_pairs={{0,1},{1,2},{2,3},{3,4},{4,5},{5,6},{6,7},{7,0},{8,9},{9,10},{10,1... | collective-permute-start | bytes 589832 | tf_op jit(solution)/shard_map/ppermute | solution.py:231
  105.3 14.2 %collective-permute-start.17 = (bf16[256,384]{1,0:T(8,128)(2,1)S(1)}, bf16[256,384]{1,0:T(8,128)(2,1)}, u32[]{:S(2)}, u32[]{:S(2)}) collective-permute-start(bf16[256,384]{1,0:T(8,128)(2,1)S(1)} %collective-permute-done.13.refs_4_), channel_id=1, source_target_pairs={{0,7},{1,0},{2,1},{3,2},{4,3},{5,4},{6,5},{7,6},{8,15},{9,8},{10,9... | collective-permute-start | bytes 589832 | tf_op jit(solution)/shard_map/ppermute | solution.py:231
  107.2 14.2 %collective-permute-start.15 = (bf16[256,384]{1,0:T(8,128)(2,1)S(1)}, bf16[256,384]{1,0:T(8,128)(2,1)}, u32[]{:S(2)}, u32[]{:S(2)}) collective-permute-start(bf16[256,384]{1,0:T(8,128)(2,1)S(1)} %collective-permute-done.11.refs_2_), channel_id=1, source_target_pairs={{0,1},{1,2},{2,3},{3,4},{4,5},{5,6},{6,7},{7,0},{8,9},{9,10},{10,1... | collective-permute-start | bytes 589832 | tf_op jit(solution)/shard_map/ppermute | solution.py:231
  112.4 14.2 %collective-permute-start.16 = (bf16[256,384]{1,0:T(8,128)(2,1)S(1)}, bf16[256,384]{1,0:T(8,128)(2,1)}, u32[]{:S(2)}, u32[]{:S(2)}) collective-permute-start(bf16[256,384]{1,0:T(8,128)(2,1)S(1)} %collective-permute-done.12.refs_3_), channel_id=1, source_target_pairs={{0,7},{1,0},{2,1},{3,2},{4,3},{5,4},{6,5},{7,6},{8,15},{9,8},{10,9... | collective-permute-start | bytes 589832 | tf_op jit(solution)/shard_map/ppermute | solution.py:231
  114.3 14.2 %collective-permute-start.18 = (bf16[256,384]{1,0:T(8,128)(2,1)}, bf16[256,384]{1,0:T(8,128)(2,1)}, u32[]{:S(2)}, u32[]{:S(2)}) collective-permute-start(bf16[256,384]{1,0:T(8,128)(2,1)} %collective-permute-done.14.refs_1_), channel_id=1, source_target_pairs={{0,1},{1,2},{2,3},{3,4},{4,5},{5,6},{6,7},{7,0},{8,9},{9,10},{10,1... | collective-permute-start | bytes 589832 | tf_op jit(solution)/shard_map/ppermute | solution.py:231
  119.5 14.2 %collective-permute-start.21 = (bf16[256,384]{1,0:T(8,128)(2,1)}, bf16[256,384]{1,0:T(8,128)(2,1)}, u32[]{:S(2)}, u32[]{:S(2)}) collective-permute-start(bf16[256,384]{1,0:T(8,128)(2,1)} %collective-permute-done.17.refs_4_), channel_id=1, source_target_pairs={{0,7},{1,0},{2,1},{3,2},{4,3},{5,4},{6,5},{7,6},{8,15},{9,8},{10,9... | collective-permute-start | bytes 589832 | tf_op jit(solution)/shard_map/ppermute | solution.py:231
  121.4 17.1 %collective-permute-start.19 = (bf16[256,384]{1,0:T(8,128)(2,1)}, bf16[256,384]{1,0:T(8,128)(2,1)}, u32[]{:S(2)}, u32[]{:S(2)}) collective-permute-start(bf16[256,384]{1,0:T(8,128)(2,1)} %collective-permute-done.15.refs_2_), channel_id=1, source_target_pairs={{0,1},{1,2},{2,3},{3,4},{4,5},{5,6},{6,7},{7,0},{8,9},{9,10},{10,1... | collective-permute-start | bytes 589832 | tf_op jit(solution)/shard_map/ppermute | solution.py:231
  126.5 12.0 %collective-permute-start.20 = (bf16[256,384]{1,0:T(8,128)(2,1)}, bf16[256,384]{1,0:T(8,128)(2,1)}, u32[]{:S(2)}, u32[]{:S(2)}) collective-permute-start(bf16[256,384]{1,0:T(8,128)(2,1)} %collective-permute-done.16.refs_3_), channel_id=1, source_target_pairs={{0,7},{1,0},{2,1},{3,2},{4,3},{5,4},{6,5},{7,6},{8,15},{9,8},{10,9... | collective-permute-start | bytes 589832 | tf_op jit(solution)/shard_map/ppermute | solution.py:231
  128.5 11.9 %collective-permute-start.22 = (bf16[256,384]{1,0:T(8,128)(2,1)}, bf16[256,384]{1,0:T(8,128)(2,1)}, u32[]{:S(2)}, u32[]{:S(2)}) collective-permute-start(bf16[256,384]{1,0:T(8,128)(2,1)} %collective-permute-done.18.refs_1_), channel_id=1, source_target_pairs={{0,1},{1,2},{2,3},{3,4},{4,5},{5,6},{6,7},{7,0},{8,9},{9,10},{10,1... | collective-permute-start | bytes 589832 | tf_op jit(solution)/shard_map/ppermute | solution.py:231
  133.6 9.1 %collective-permute-start.23 = (bf16[256,384]{1,0:T(8,128)(2,1)}, bf16[256,384]{1,0:T(8,128)(2,1)}, u32[]{:S(2)}, u32[]{:S(2)}) collective-permute-start(bf16[256,384]{1,0:T(8,128)(2,1)} %collective-permute-done.21.refs_4_), channel_id=1, source_target_pairs={{0,7},{1,0},{2,1},{3,2},{4,3},{5,4},{6,5},{7,6},{8,15},{9,8},{10,9... | collective-permute-start | bytes 589832 | tf_op jit(solution)/shard_map/ppermute | solution.py:231
